TPU v7x, 128 devices: a whole 4x4x4 slice. The times are simulated.
128 devices in a mesh: tiles: 16 (over y, x), gauss: 8 (over z, core).
Axes of the slice: x: 4, y: 4, z: 4, core: 2. Of those that a mesh axis runs over, the one named last changes fastest.
Arguments:
- params: float32 [59, 2097152], P(None, ('tiles', 'gauss')), may hold values from -9 to 4.5, as said below
- adam_m: float32 [59, 2097152], P(None, ('tiles', 'gauss')), may hold values from -0.03 to 0.03
- adam_v: float32 [59, 2097152], P(None, ('tiles', 'gauss')), may hold values from 0.05 to 2
- cameras: float32 [4, 13], replicated, may hold values from -0.5 to 2000, as said below
- exposure: float32 [4, 3], replicated, may hold values from 0.5 to 1.5
- entry_owner: int32 [512, 1024], P(('tiles', 'gauss')), may hold values from 0 to 127, as said below
- entry_local: int32 [512, 1024], P(('tiles', 'gauss')), may hold values from 0 to 16383
- block_counts: int32 [512], P(('tiles', 'gauss')), may hold values from 2 to 4, as said below
- tile_view: int32 [512], P(('tiles', 'gauss')), may hold values from 0 to 3
- tile_spot: int32 [512], P(('tiles', 'gauss')), may hold values from 12580 to 19579
- d_image: float32 [512, 3, 256], P(('tiles', 'gauss')), may hold values from -320 to 320
Outputs:
- new_params: float32 [59, 2097152], P(None, ('tiles', 'gauss'))
- new_m: float32 [59, 2097152], P(None, ('tiles', 'gauss'))
- new_v: float32 [59, 2097152], P(None, ('tiles', 'gauss'))
- exposure_grad: float32 [4, 3], replicated
Inputs may be any that keep to these rules, and one draw needn't show every extreme that they name: `params`: components 0 to 2 lie in -4.5 to 4.5, components 3 to 5 in -5 to -2, component 6 in 0.5 to 1.5, component 10 in -9 to -7.5. `cameras`: each row holds a matrix whose entries differ from the identity's by at most 0.1, a translation with first two entries in -0.5 to 0.5 and third in 5 to 6, and a focal length in 1400 to 2000. `entry_owner`: of the 4096 entries of one device's lists (rendered or not), at most 48 name any one owner; in every draw one owner is named exactly 48 times by every device. `block_counts`: every device holds a tile of 4 blocks.
All inputs are finite; a program needn't handle non-finite values.
Results may differ from a plain program's by a relative error of at most 0.0003.
Values sent between devices are 32-bit elements; how exact they have to be, the bound alone decides.
No kernel may reach another device: no remote copies, remote signals or barrier semaphores. Data moves between devices by JAX's collectives and lax.ppermute only.
A program may use at most 256 MiB of HBM per device.

v0:
```python
import jax
import jax.numpy as jnp
from jax import lax
from jax.sharding import PartitionSpec as P

VIEWS = 4
BLOCK = 256
TILE = 16
IMG_W = 3840
IMG_H = 2160
PARAMS = 59
TPIX = 256


sh_c0 = 0.28209479177387814
sh_c1 = 0.4886025119029199
sh_c2 = (
    1.0925484305920792,
    -1.0925484305920792,
    0.31539156525252005,
    -1.0925484305920792,
    0.5462742152960396,
)
sh_c3 = (
    -0.5900435899266435,
    2.890611442640554,
    -0.4570457994644658,
    0.3731763325901154,
    -0.4570457994644658,
    1.445305721320277,
    -0.5900435899266435,
)
beta_first = 0.9
beta_second = 0.999
learn_rate = 0.01
adam_eps = 1e-08
fix_first = 1.0
fix_second = 0.632304575229036
blur_add = 0.3


def sh_color(values, unit_x, unit_y, unit_z):
    coefficients = [values[11 + 3 * index_k : 14 + 3 * index_k] for index_k in range(16)]
    square_x = unit_x * unit_x
    square_y = unit_y * unit_y
    square_z = unit_z * unit_z
    basis_list = [
        -sh_c1 * unit_y,
        sh_c1 * unit_z,
        -sh_c1 * unit_x,
        sh_c2[0] * unit_x * unit_y,
        sh_c2[1] * unit_y * unit_z,
        sh_c2[2] * (2.0 * square_z - square_x - square_y),
        sh_c2[3] * unit_x * unit_z,
        sh_c2[4] * (square_x - square_y),
        sh_c3[0] * unit_y * (3.0 * square_x - square_y),
        sh_c3[1] * unit_x * unit_y * unit_z,
        sh_c3[2] * unit_y * (4.0 * square_z - square_x - square_y),
        sh_c3[3] * unit_z * (2.0 * square_z - 3.0 * square_x - 3.0 * square_y),
        sh_c3[4] * unit_x * (4.0 * square_z - square_x - square_y),
        sh_c3[5] * unit_z * (square_x - square_y),
        sh_c3[6] * unit_x * (square_x - 3.0 * square_y),
    ]
    summed = 0.5 + sh_c0 * coefficients[0]
    for index_k in range(15):
        summed = summed + basis_list[index_k] * coefficients[index_k + 1]
    return jnp.maximum(summed, 0.0)


def project(values, camera):
    points = [values[0], values[1], values[2]]
    matrix = [[camera[3 * row_at + col_at] for col_at in range(3)] for row_at in range(3)]
    translation = [camera[9], camera[10], camera[11]]
    focal_len = camera[12]
    viewed = [
        matrix[row_at][0] * points[0]
        + matrix[row_at][1] * points[1]
        + matrix[row_at][2] * points[2]
        + translation[row_at]
        for row_at in range(3)
    ]
    inverse_depth = 1.0 / viewed[2]
    screen_x = focal_len * viewed[0] * inverse_depth + 0.5 * IMG_W
    screen_y = focal_len * viewed[1] * inverse_depth + 0.5 * IMG_H
    slope_x = focal_len * viewed[0] * inverse_depth * inverse_depth
    slope_y = focal_len * viewed[1] * inverse_depth * inverse_depth
    jac_w = [
        [
            focal_len * inverse_depth * matrix[0][col_at] - slope_x * matrix[2][col_at]
            for col_at in range(3)
        ],
        [
            focal_len * inverse_depth * matrix[1][col_at] - slope_y * matrix[2][col_at]
            for col_at in range(3)
        ],
    ]
    quat_len = jnp.sqrt(
        values[6] * values[6]
        + values[7] * values[7]
        + values[8] * values[8]
        + values[9] * values[9]
    )
    quat_w = values[6] / quat_len
    quat_x = values[7] / quat_len
    quat_y = values[8] / quat_len
    quat_z = values[9] / quat_len
    rotation = [
        [
            1.0 - 2.0 * (quat_y * quat_y + quat_z * quat_z),
            2.0 * (quat_x * quat_y - quat_w * quat_z),
            2.0 * (quat_x * quat_z + quat_w * quat_y),
        ],
        [
            2.0 * (quat_x * quat_y + quat_w * quat_z),
            1.0 - 2.0 * (quat_x * quat_x + quat_z * quat_z),
            2.0 * (quat_y * quat_z - quat_w * quat_x),
        ],
        [
            2.0 * (quat_x * quat_z - quat_w * quat_y),
            2.0 * (quat_y * quat_z + quat_w * quat_x),
            1.0 - 2.0 * (quat_x * quat_x + quat_y * quat_y),
        ],
    ]
    extent = [jnp.exp(values[3]), jnp.exp(values[4]), jnp.exp(values[5])]
    spread = [
        [
            (
                jac_w[row_at][0] * rotation[0][col_at]
                + jac_w[row_at][1] * rotation[1][col_at]
                + jac_w[row_at][2] * rotation[2][col_at]
            )
            * extent[col_at]
            for col_at in range(3)
        ]
        for row_at in range(2)
    ]
    cov_a = (
        spread[0][0] * spread[0][0]
        + spread[0][1] * spread[0][1]
        + spread[0][2] * spread[0][2]
        + blur_add
    )
    cov_b = spread[0][0] * spread[1][0] + spread[0][1] * spread[1][1] + spread[0][2] * spread[1][2]
    cov_c = (
        spread[1][0] * spread[1][0]
        + spread[1][1] * spread[1][1]
        + spread[1][2] * spread[1][2]
        + blur_add
    )
    determinant = cov_a * cov_c - cov_b * cov_b
    opacity = jax.nn.sigmoid(values[10])
    center = [
        -(
            matrix[0][col_at] * translation[0]
            + matrix[1][col_at] * translation[1]
            + matrix[2][col_at] * translation[2]
        )
        for col_at in range(3)
    ]
    offset = [points[col_at] - center[col_at] for col_at in range(3)]
    distance = jnp.sqrt(offset[0] * offset[0] + offset[1] * offset[1] + offset[2] * offset[2])
    colors = sh_color(values, offset[0] / distance, offset[1] / distance, offset[2] / distance)
    first_rows = jnp.stack(
        [
            screen_x,
            screen_y,
            cov_c / determinant,
            -cov_b / determinant,
            cov_a / determinant,
            opacity,
        ]
    )
    return jnp.concatenate([first_rows, colors], axis=0)


def render_blocks(proj_rows, live_mask, pix_x, pix_y):
    nblocks = proj_rows.shape[1] // BLOCK
    grouped = proj_rows.reshape(proj_rows.shape[0], nblocks, BLOCK).transpose(1, 0, 2)
    block_masks = live_mask.reshape(nblocks, BLOCK)

    def block_step(carried, block_item):
        log_level, painted = carried
        block_rows, block_mask = block_item
        off_x = pix_x[None, :] - block_rows[0][:, None]
        off_y = pix_y[None, :] - block_rows[1][:, None]
        exponent = (
            -0.5 * (block_rows[2][:, None] * off_x * off_x + block_rows[4][:, None] * off_y * off_y)
            - block_rows[3][:, None] * off_x * off_y
        )
        alpha_px = (block_rows[5] * block_mask)[:, None] * jnp.exp(exponent)
        fade_log = jnp.log1p(-alpha_px)
        running = jnp.cumsum(fade_log, axis=0)
        weights = alpha_px * jnp.exp(log_level[None, :] + running - fade_log)
        painted = painted + jnp.dot(block_rows[6:9], weights, precision=lax.Precision.HIGHEST)
        return ((log_level + running[-1], painted), None)

    initial = (jnp.zeros(pix_x.shape, jnp.float32), jnp.zeros((3, pix_x.shape[0]), jnp.float32))
    (log_level, painted), unused = lax.scan(block_step, initial, (grouped, block_masks))
    return painted


def body(
    params,
    adam_m,
    adam_v,
    cameras,
    exposure,
    entry_owner,
    entry_local,
    block_counts,
    tile_view,
    tile_spot,
    d_image,
):
    devices = lax.axis_size(("tiles", "gauss"))
    gauss_dev = params.shape[1]
    tile_dev, slot_count = entry_owner.shape
    entries = tile_dev * slot_count
    capacity = 3 * entries // (2 * devices)
    owners = entry_owner.reshape(entries)
    request = jnp.repeat(tile_view, slot_count) * gauss_dev + entry_local.reshape(entries)
    sort_order = jnp.argsort(owners, stable=True)
    sorted_owner = owners[sort_order]
    starts = jnp.searchsorted(sorted_owner, jnp.arange(devices, dtype=jnp.int32), side="left")
    ranked = jnp.arange(entries, dtype=jnp.int32) - starts[sorted_owner]
    target = jnp.zeros((entries,), jnp.int32).at[sort_order].set(sorted_owner * capacity + ranked)
    outgoing = jnp.full((devices * capacity,), -1, jnp.int32).at[target].set(request)
    incoming = lax.all_to_all(outgoing, ("tiles", "gauss"), split_axis=0, concat_axis=0, tiled=True)
    present = incoming >= 0
    across = IMG_W // TILE
    pixel_ids = jnp.arange(TPIX, dtype=jnp.int32)
    pix_x = ((tile_spot % across)[:, None] * TILE + pixel_ids[None, :] % TILE).astype(
        jnp.float32
    ) + 0.5
    pix_y = ((tile_spot // across)[:, None] * TILE + pixel_ids[None, :] // TILE).astype(
        jnp.float32
    ) + 0.5
    live_mask = (
        (jnp.arange(slot_count, dtype=jnp.int32) // BLOCK)[None, :] < block_counts[:, None]
    ).astype(jnp.float32)
    picker = (tile_view[:, None] == jnp.arange(VIEWS, dtype=jnp.int32)[None, :]).astype(jnp.float32)
    tile_gains = jnp.dot(picker, exposure, precision=lax.Precision.HIGHEST)
    tile_cameras = jnp.dot(picker, cameras, precision=lax.Precision.HIGHEST)
    replies = jnp.take(params, jnp.maximum(incoming, 0) % gauss_dev, axis=1)
    arrived = lax.all_to_all(replies, ("tiles", "gauss"), split_axis=1, concat_axis=1, tiled=True)
    entry_rows = (
        jnp.take(arrived, target, axis=1).reshape(PARAMS, tile_dev, slot_count).transpose(1, 0, 2)
    )

    def tile_grad(tile_item):
        row_block, camera_row, mask_row, x_row, y_row, gain_vec, cotangent = tile_item

        def tile_image(rows_in, gains_in):
            return gains_in[:, None] * render_blocks(
                project(rows_in, camera_row[:, None]), mask_row, x_row, y_row
            )

        rendered, pullback = jax.vjp(tile_image, row_block, gain_vec)
        return pullback(cotangent)

    grad_rows, grad_gains = lax.map(
        tile_grad, (entry_rows, tile_cameras, live_mask, pix_x, pix_y, tile_gains, d_image)
    )
    entry_grads = grad_rows.transpose(1, 0, 2).reshape(PARAMS, entries)
    outgoing_grads = (
        jnp.zeros((PARAMS, devices * capacity), jnp.float32).at[:, target].set(entry_grads)
    )
    returned = lax.all_to_all(
        outgoing_grads, ("tiles", "gauss"), split_axis=1, concat_axis=1, tiled=True
    )
    local_index = jnp.where(present, incoming % gauss_dev, gauss_dev)
    gradient = (
        jnp.zeros((PARAMS, gauss_dev + 1), jnp.float32).at[:, local_index].add(returned)[:, :-1]
    )
    expo_local = jnp.dot(picker.T, grad_gains, precision=lax.Precision.HIGHEST)
    exposure_grad = lax.psum(expo_local, ("tiles", "gauss")) / devices
    new_m = beta_first * adam_m + (1.0 - beta_first) * gradient
    new_v = beta_second * adam_v + (1.0 - beta_second) * gradient * gradient
    new_params = params - learn_rate * (new_m / fix_first) / (
        jnp.sqrt(new_v / fix_second) + adam_eps
    )
    return (new_params, new_m, new_v, exposure_grad)


def solution(mesh):
    placed = (
        P(None, ("tiles", "gauss")),
        P(None, ("tiles", "gauss")),
        P(None, ("tiles", "gauss")),
        P(),
        P(),
        P(("tiles", "gauss"), None),
        P(("tiles", "gauss"), None),
        P(("tiles", "gauss")),
        P(("tiles", "gauss")),
        P(("tiles", "gauss")),
        P(("tiles", "gauss"), None, None),
    )
    return jax.shard_map(
        body,
        mesh=mesh,
        in_specs=placed,
        out_specs=(
            P(None, ("tiles", "gauss")),
            P(None, ("tiles", "gauss")),
            P(None, ("tiles", "gauss")),
            P(),
        ),
        check_vma=False,
    )
```

profile of v0, /device:TPU:1, one launch (start us, length us, event | category | flops | bytes accessed | tf_op | source)
XLA Modules:
  0.0 852.9 jit_solution(9691868540588589673)
XLA Ops:
  1.4 5.8 sort.17
  7.2 23.0 %gather_fusion.1 = s32[4096]{0:T(1024)S(1)} fusion(s32[4096]{0:T(1024)S(1)} %bitcast.1032, s32[4096]{0:T(1024)S(1)} %get-tuple-element.1639), kind=kCustom, calls=%fused_computation.1 | custom fusion | bytes 49152 | tf_op jit(solution)/shard_map/gather | solution.py:223
  30.2 15.8 %while.148 = (s32[]{:T(128)}, u32[128]{0:T(128)S(1)}, u32[128]{0:T(128)S(1)}, s32[4096]{0:T(1024)S(1)}, s32[]{:T(128)}, /*index=5*/s32[]{:T(128)}, s32[]{}) while((s32[]{:T(128)}, u32[128]{0:T(128)S(1)}, u32[128]{0:T(128)S(1)}, s32[4096]{0:T(1024)S(1)}, s32[]{:T(128)}, /*index=5*/s32[]{:T(128)}, s32[]{}) %tuple.508), condition=%wide.region_2.3_spmd.clone, body=%wide.region_1.2_spmd.clone.sunk | while | flops 2692 | bytes 10340 | solution.py:224
  46.1 24.7 %gather_fusion.2 = s32[4096]{0:T(1024)S(1)} fusion(s32[128]{0:T(128)S(1)} %convert_element_type.20, s32[4096]{0:T(1024)S(1)} %broadcast_clamp_fusion.2), kind=kCustom, calls=%fused_computation.2 | custom fusion | bytes 49152 | tf_op jit(solution)/shard_map/gather | solution.py:225
  70.8 15.5 %scatter_custom_fusion = s32[4096]{0:T(1024)S(1)} fusion(s32[4096]{0:T(1024)S(1)} %get-tuple-element.1640, s32[4096]{0:T(1024)S(1)} %subtract_add_fusion, s32[]{:T(128)} %constant.484.clone.1), kind=kCustom, calls=%fused_computation.596 | custom fusion | bytes 16388 | tf_op jit(solution)/shard_map/scatter | solution.py:226
  86.5 15.5 %scatter_custom_fusion.1 = s32[6144]{0:T(1024)S(1)} fusion(s32[4096]{0:T(1024)S(1)} %get-tuple-element.1638, s32[4096]{0:T(1024)S(1)} %bitcast.1134, s32[]{:T(128)} %constant.483.clone.1), kind=kCustom, calls=%fused_computation.588 | custom fusion | bytes 24580 | tf_op jit(solution)/shard_map/scatter | solution.py:227
  102.8 11.5 %all-to-all-start = ((s32[128,48,1]{1,2,0:T(1,128)}), s32[128,48,1]{1,2,0:T(1,128)S(1)}, u32[]{:S(2)}, u32[]{:S(2)}) async-start(s32[128,48,1]{1,2,0:T(1,128)} %bitcast.81), calls=%async_computation | async-start | bytes 131072 | tf_op jit(solution)/shard_map/all_to_all | solution.py:228
  114.3 7.0 copy.134
  121.3 2.3 all-to-all-done
  125.3 24.5 %gather_fusion.3 = f32[6144,59]{1,0:T(8,128)} fusion(f32[59,16384]{0,1:T(8,128)} %copy.134, s32[6144]{0:T(1024)S(1)} %broadcast_clamp_fusion), kind=kCustom, calls=%fused_computation.3 | custom fusion | bytes 2924544 | tf_op jit(solution)/shard_map/jit(_take)/gather | solution.py:244
  149.8 3.2 fusion.200
  153.0 5.5 reshape.9949
  158.5 7.8 all-to-all-start.1
  166.9 23.3 %all-to-all-done.1 = f32[128,1,2832]{2,1,0:T(1,128)S(1)} async-done(((f32[128,1,2832]{2,1,0:T(1,128)}), f32[128,1,2832]{2,1,0:T(1,128)S(1)}, u32[]{:S(2)}, u32[]{:S(2)}) %all-to-all-start.1) | async-done | bytes 1450016 | tf_op jit(solution)/shard_map/all_to_all | solution.py:245
  190.8 5.9 reduce.72
  196.7 3.6 reshape.9950
  200.3 14.2 %gather_fusion.4 = f32[4096,59]{1,0:T(8,128)} fusion(f32[59,6144]{0,1:T(8,128)S(1)} %bitcast.1042, s32[4096]{0:T(1024)S(1)} %get-tuple-element.1637), kind=kCustom, calls=%fused_computation.4 | custom fusion | bytes 1949696 | tf_op jit(solution)/shard_map/jit(_take)/gather | solution.py:247
  217.8 451.8 %while.147 = (s32[]{:T(128)}, f32[4,59,1024]{2,1,0:T(8,128)}, f32[4,3]{1,0:T(4,128)S(1)}, f32[4,59,1024]{2,1,0:T(8,128)}, f32[4,13]{1,0:T(4,128)S(1)}, /*index=5...) while((s32[]{:T(128)}, f32[4,59,1024]{2,1,0:T(8,128)}, ...), condition=%wide.region_37.38_spmd, body=%wide.region_5.37_spmd.sunk | while | flops 33596216 | bytes 15937833 | solution.py:261
  232.4 9.8 %fusion.236 = (f32[1024]{0:T(1024)S(1)}, f32[1,1,1024]{2,1,0:T(1,128)S(1)}, f32[1024]{0:T(1024)S(1)}, f32[1,1,1024]{2,1,0:T(1,128)S(1)}, f32[1,1,1024]{2,1,0:T(1...) fusion(f32[]{:T(128)} %broadcast.13728, f32[]{:T(128)} %bitcast.945, ...), kind=kLoop, calls=%fused_computation.632.clone.1 | loop fusion | flops 21504 | bytes 41028 | tf_op jit(solution)/shard_map/while/body/eval_jaxpr/jvp()/mul | solution.py:84
  242.2 4.5 add_multiply_fusion.38
  246.7 4.4 add_multiply_fusion.39
  253.2 20.0 %while.149 = (s32[]{:T(128)}, f32[256]{0:T(256)S(1)}, f32[3,256]{1,0:T(4,128)S(1)}, f32[4,256,256]{2,1,0:T(8,128)}, f32[4,256,1]{1,2,0:T(1,128)S(1)}, /*index=5*...) while((s32[]{:T(128)}, f32[256]{0:T(256)S(1)}, ...), condition=%wide.region_9.9_spmd.clone, body=%wide.region_6.8_spmd.clone.sunk | while | flops 14749193 | bytes 4594060 | solution.py:198
  274.0 32.6 %while.150 = (s32[]{:T(128)}, f32[256]{0:T(256)S(1)}, f32[4,9,256]{2,1,0:T(8,128)S(1)}, f32[4,256,256]{2,1,0:T(8,128)}, f32[4,3,256]{2,1,0:T(4,128)S(1)}, /*inde...) while((s32[]{:T(128)}, f32[256]{0:T(256)S(1)}, ...), condition=%wide.region_20.20_spmd.clone, body=%wide.region_10.19_spmd.clone.sunk | while | flops 15546372 | bytes 6922508 | solution.py:198
  275.5 2.3 fusion.256
  283.6 2.3 fusion.256
  291.8 2.3 fusion.256
  299.9 2.3 fusion.256
  306.9 7.5 negate_add_fusion.2
  319.3 6.5 multiply_add_fusion.54
  325.8 3.8 multiply_add_fusion.55
  345.3 9.8 %fusion.236 = (f32[1024]{0:T(1024)S(1)}, f32[1,1,1024]{2,1,0:T(1,128)S(1)}, f32[1024]{0:T(1024)S(1)}, f32[1,1,1024]{2,1,0:T(1,128)S(1)}, f32[1,1,1024]{2,1,0:T(1...) fusion(f32[]{:T(128)} %broadcast.13728, f32[]{:T(128)} %bitcast.945, ...), kind=kLoop, calls=%fused_computation.632.clone.1 | loop fusion | flops 21504 | bytes 41028 | tf_op jit(solution)/shard_map/while/body/eval_jaxpr/jvp()/mul | solution.py:84
  355.1 4.5 add_multiply_fusion.38
  359.6 4.4 add_multiply_fusion.39
  366.3 20.0 %while.149 = (s32[]{:T(128)}, f32[256]{0:T(256)S(1)}, f32[3,256]{1,0:T(4,128)S(1)}, f32[4,256,256]{2,1,0:T(8,128)}, f32[4,256,1]{1,2,0:T(1,128)S(1)}, /*index=5*...) while((s32[]{:T(128)}, f32[256]{0:T(256)S(1)}, ...), condition=%wide.region_9.9_spmd.clone, body=%wide.region_6.8_spmd.clone.sunk | while | flops 14749193 | bytes 4594060 | solution.py:198
  387.1 32.6 %while.150 = (s32[]{:T(128)}, f32[256]{0:T(256)S(1)}, f32[4,9,256]{2,1,0:T(8,128)S(1)}, f32[4,256,256]{2,1,0:T(8,128)}, f32[4,3,256]{2,1,0:T(4,128)S(1)}, /*inde...) while((s32[]{:T(128)}, f32[256]{0:T(256)S(1)}, ...), condition=%wide.region_20.20_spmd.clone, body=%wide.region_10.19_spmd.clone.sunk | while | flops 15546372 | bytes 6922508 | solution.py:198
  420.0 7.5 negate_add_fusion.2
  432.4 6.5 multiply_add_fusion.54
  438.9 3.8 multiply_add_fusion.55
  458.3 9.8 %fusion.236 = (f32[1024]{0:T(1024)S(1)}, f32[1,1,1024]{2,1,0:T(1,128)S(1)}, f32[1024]{0:T(1024)S(1)}, f32[1,1,1024]{2,1,0:T(1,128)S(1)}, f32[1,1,1024]{2,1,0:T(1...) fusion(f32[]{:T(128)} %broadcast.13728, f32[]{:T(128)} %bitcast.945, ...), kind=kLoop, calls=%fused_computation.632.clone.1 | loop fusion | flops 21504 | bytes 41028 | tf_op jit(solution)/shard_map/while/body/eval_jaxpr/jvp()/mul | solution.py:84
  468.1 4.5 add_multiply_fusion.38
  472.7 4.4 add_multiply_fusion.39
  479.2 20.0 %while.149 = (s32[]{:T(128)}, f32[256]{0:T(256)S(1)}, f32[3,256]{1,0:T(4,128)S(1)}, f32[4,256,256]{2,1,0:T(8,128)}, f32[4,256,1]{1,2,0:T(1,128)S(1)}, /*index=5*...) while((s32[]{:T(128)}, f32[256]{0:T(256)S(1)}, ...), condition=%wide.region_9.9_spmd.clone, body=%wide.region_6.8_spmd.clone.sunk | while | flops 14749193 | bytes 4594060 | solution.py:198
  500.0 32.6 %while.150 = (s32[]{:T(128)}, f32[256]{0:T(256)S(1)}, f32[4,9,256]{2,1,0:T(8,128)S(1)}, f32[4,256,256]{2,1,0:T(8,128)}, f32[4,3,256]{2,1,0:T(4,128)S(1)}, /*inde...) while((s32[]{:T(128)}, f32[256]{0:T(256)S(1)}, ...), condition=%wide.region_20.20_spmd.clone, body=%wide.region_10.19_spmd.clone.sunk | while | flops 15546372 | bytes 6922508 | solution.py:198
  532.9 7.5 negate_add_fusion.2
  545.3 6.5 multiply_add_fusion.54
  551.8 3.8 multiply_add_fusion.55
  571.2 9.8 %fusion.236 = (f32[1024]{0:T(1024)S(1)}, f32[1,1,1024]{2,1,0:T(1,128)S(1)}, f32[1024]{0:T(1024)S(1)}, f32[1,1,1024]{2,1,0:T(1,128)S(1)}, f32[1,1,1024]{2,1,0:T(1...) fusion(f32[]{:T(128)} %broadcast.13728, f32[]{:T(128)} %bitcast.945, ...), kind=kLoop, calls=%fused_computation.632.clone.1 | loop fusion | flops 21504 | bytes 41028 | tf_op jit(solution)/shard_map/while/body/eval_jaxpr/jvp()/mul | solution.py:84
  581.0 4.5 add_multiply_fusion.38
  585.5 4.4 add_multiply_fusion.39
  592.1 20.0 %while.149 = (s32[]{:T(128)}, f32[256]{0:T(256)S(1)}, f32[3,256]{1,0:T(4,128)S(1)}, f32[4,256,256]{2,1,0:T(8,128)}, f32[4,256,1]{1,2,0:T(1,128)S(1)}, /*index=5*...) while((s32[]{:T(128)}, f32[256]{0:T(256)S(1)}, ...), condition=%wide.region_9.9_spmd.clone, body=%wide.region_6.8_spmd.clone.sunk | while | flops 14749193 | bytes 4594060 | solution.py:198
  612.9 32.6 %while.150 = (s32[]{:T(128)}, f32[256]{0:T(256)S(1)}, f32[4,9,256]{2,1,0:T(8,128)S(1)}, f32[4,256,256]{2,1,0:T(8,128)}, f32[4,3,256]{2,1,0:T(4,128)S(1)}, /*inde...) while((s32[]{:T(128)}, f32[256]{0:T(256)S(1)}, ...), condition=%wide.region_20.20_spmd.clone, body=%wide.region_10.19_spmd.clone.sunk | while | flops 15546372 | bytes 6922508 | solution.py:198
  645.8 7.5 negate_add_fusion.2
  658.2 6.5 multiply_add_fusion.54
  664.7 3.8 multiply_add_fusion.55
  674.2 22.6 %scatter_custom_fusion.2 = f32[59,6144]{0,1:T(8,128)S(1)} fusion(s32[4096]{0:T(1024)S(1)} %get-tuple-element.1638, f32[4096,59]{1,0:T(8,128)} %copy.139, f32[]{:T(128)} %constant.482.clone.1), kind=kCustom, calls=%fused_computation.563 | custom fusion | bytes 1450496 | tf_op jit(solution)/shard_map/scatter | solution.py:266
  696.9 5.5 reshape.9951
  702.3 4.7 all-to-all-start.2
  707.2 75.3 %psum.7 = f32[4,3]{0,1:T(4,128)S(1)} all-reduce(f32[4,3]{0,1:T(4,128)S(1)} %fusion.171), channel_id=1, replica_groups=mesh['tiles'=16,'gauss'=8] {'tiles','gauss'}, use_global_device_ids=true, to_apply=%region_40.41 | all-reduce | flops 12 | bytes 96 | tf_op jit(solution)/shard_map/psum | solution.py:276
  783.1 4.3 reduce.73
  787.4 3.6 reshape.9952
  791.0 37.6 %scatter_custom_fusion.3 = f32[59,16385]{0,1:T(8,128)} fusion(s32[6144]{0:T(1024)S(1)} %bitcast.1132, f32[6144,59]{1,0:T(8,128)} %bitcast.1081, f32[]{:T(128)} %constant.482.clone.1), kind=kCustom, calls=%fused_computation.557 | custom fusion | flops 362496 | bytes 3867372 | tf_op jit(solution)/shard_map/scatter-add | solution.py:273
  828.6 5.7 slice.611
  834.3 6.8 copy.145
  841.1 11.6 %divide_subtract_fusion = (f32[59,16384]{1,0:T(8,128)}, f32[59,16384]{1,0:T(8,128)}, f32[59,16384]{1,0:T(8,128)}) fusion(f32[59,16384]{1,0:T(8,128)} %param.19, f32[59,16384]{1,0:T(8,128)} %copy.145, f32[59,16384]{1,0:T(8,128)} %param.20, f32[59,16384]{1,0:T(8,128)} %param.21), kind=kLoop, calls=%fused_computation.560 | loop fusion | flops 11599872 | bytes 27066368 | tf_op jit(solution)/shard_map/sub | solution.py:279
  (1173 shorter events, 275.2 us)
Async XLA Ops:
  0.6 165.9 %copy-start = (f32[4,13]{1,0:T(4,128)S(1)}, f32[4,13]{1,0:T(4,128)}, u32[]{:S(2)}) copy-start(f32[4,13]{1,0:T(4,128)} %param.22) | copy-start | bytes 628
  46.1 40.3 %copy-start.6 = (s32[4]{0:T(128)S(1)}, s32[4]{0:T(128)}, u32[]{:S(2)}) copy-start(s32[4]{0:T(128)} %param.27) | copy-start | bytes 52
  46.1 40.3 %copy-start.2 = (s32[4,1024]{1,0:T(4,128)S(1)}, s32[4,1024]{1,0:T(4,128)}, u32[]{:S(2)}) copy-start(s32[4,1024]{1,0:T(4,128)} %param.25) | copy-start | bytes 49156
  102.8 20.8 %all-to-all-start = ((s32[128,48,1]{1,2,0:T(1,128)}), s32[128,48,1]{1,2,0:T(1,128)S(1)}, u32[]{:S(2)}, u32[]{:S(2)}) async-start(s32[128,48,1]{1,2,0:T(1,128)} %bitcast.81), calls=%async_computation | async-start | bytes 131072 | tf_op jit(solution)/shard_map/all_to_all | solution.py:228
  153.0 13.4 %copy-start.5 = (s32[4]{0:T(128)S(1)}, s32[4]{0:T(128)}, u32[]{:S(2)}) copy-start(s32[4]{0:T(128)} %param.28) | copy-start | bytes 52
  153.0 13.4 %copy-start.4 = (f32[4,3]{1,0:T(4,128)S(1)}, f32[4,3]{1,0:T(4,128)}, u32[]{:S(2)}) copy-start(f32[4,3]{1,0:T(4,128)} %param.23) | copy-start | bytes 148
  153.0 13.8 %copy-start.3 = (s32[4]{0:T(128)S(1)}, s32[4]{0:T(128)}, u32[]{:S(2)}) copy-start(s32[4]{0:T(128)} %param.26) | copy-start | bytes 52
  158.5 31.7 %all-to-all-start.1 = ((f32[128,1,2832]{2,1,0:T(1,128)}), f32[128,1,2832]{2,1,0:T(1,128)S(1)}, u32[]{:S(2)}, u32[]{:S(2)}) async-start(f32[128,1,2832]{2,1,0:T(1,128)} %reshape.9949), calls=%async_computation.1 | async-start | bytes 3014656 | tf_op jit(solution)/shard_map/all_to_all | solution.py:245
  702.3 80.8 %all-to-all-start.2 = ((f32[128,1,2832]{2,1,0:T(1,128)}), f32[128,1,2832]{2,1,0:T(1,128)S(1)}, u32[]{:S(2)}, u32[]{:S(2)}) async-start(f32[128,1,2832]{2,1,0:T(1,128)} %reshape.9951), calls=%async_computation.2 | async-start | bytes 3014656 | tf_op jit(solution)/shard_map/all_to_all | solution.py:268
  841.1 11.6 %copy-start.1 = (f32[4,13]{1,0:T(4,128)S(1)}, f32[4,13]{1,0:T(4,128)}, u32[]{:S(2)}) copy-start(f32[4,13]{1,0:T(4,128)} %param.22) | copy-start | bytes 628
where the time goes:
time: 869 us; the launch traced here: 853 us
  other arithmetic  399 us (46%)
  local copies, waits for them, and re-layouts  226 us (26%)
  blocking collectives  75.3 us (9%)
  matrix products  51.3 us (6%)
  loops' own time  51 us (6%)
  waiting for transfers between devices  25.6 us (3%)
  starting transfers between devices  24 us (3%)
    psum x1, blocking collectives, body(): exposure_grad = lax.psum(expo_local, ('tiles', 'gauss')) / devices  75.3 us
    another operation x157, other arithmetic  53.4 us
    dot_general x48, matrix products, block_step(): jnp.dot(block_rows[6:9], weights, precision=lax.Precision.HIGHEST)  50.7 us
    another operation x1, loops' own time, body(): lax.map(tile_grad, (entry_rows, tile_cameras, live_mask, pix_x, pix_y, ti...  47.4 us
    dynamic_update_slice x64, other arithmetic, render_blocks(): lax.scan(block_step, initial, (grouped, block_masks))  43.3 us
    mul x4, other arithmetic, project(): screen_y = focal_len * viewed[1] * inverse_depth + 0.5 * IMG_H  39 us
    scatter-add x1, other arithmetic, body(): jnp.zeros((PARAMS, gauss_dev + 1), jnp.float32).at[:, local_index]  37.6 us
    mul x16, other arithmetic, project(): (jac_w[row_at][0] * rotation[0][col_at] + jac_w[row_at][1] * rotation[1][...  35.4 us
  transfers between devices with their start and end apart: 3, of which 2 were waited for; matrix products, arithmetic and copies ran while one was open for 1% of the time, Pallas kernels for 0%

commit v1 on v0

v1 whole, which is shorter than its diff:
```python
import jax
import jax.numpy as jnp
from jax import lax
from jax.experimental import pallas as pl
from jax.experimental.pallas import tpu as pltpu
from jax.sharding import PartitionSpec as P

AXES = ("tiles", "gauss")
DEVS = 128
CAP = 48
TILES = 4
SLOTS = 1024
BLOCK = 256
NBLK = 4
TPIX = 256
TILE = 16
ACROSS = 240
IMG_W = 3840
IMG_H = 2160
PARAMS = 59
GDEV = 16384
HALF = GDEV // 2
VALS = 9
USED = CAP * VALS
WIDE = 512
TABLES = 4
UNROLL = 16

sh_c0 = 0.28209479177387814
sh_c1 = 0.4886025119029199
sh_c2 = (
    1.0925484305920792,
    -1.0925484305920792,
    0.31539156525252005,
    -1.0925484305920792,
    0.5462742152960396,
)
sh_c3 = (
    -0.5900435899266435,
    2.890611442640554,
    -0.4570457994644658,
    0.3731763325901154,
    -0.4570457994644658,
    1.445305721320277,
    -0.5900435899266435,
)
beta_first = 0.9
beta_second = 0.999
learn_rate = 0.01
adam_eps = 1e-08
fix_first = 1.0
fix_second = 0.632304575229036
blur_add = 0.3

F32 = jnp.float32
BF16 = jnp.bfloat16


def sh_color(coefficients, unit_x, unit_y, unit_z):
    square_x = unit_x * unit_x
    square_y = unit_y * unit_y
    square_z = unit_z * unit_z
    basis_list = [
        -sh_c1 * unit_y,
        sh_c1 * unit_z,
        -sh_c1 * unit_x,
        sh_c2[0] * unit_x * unit_y,
        sh_c2[1] * unit_y * unit_z,
        sh_c2[2] * (2.0 * square_z - square_x - square_y),
        sh_c2[3] * unit_x * unit_z,
        sh_c2[4] * (square_x - square_y),
        sh_c3[0] * unit_y * (3.0 * square_x - square_y),
        sh_c3[1] * unit_x * unit_y * unit_z,
        sh_c3[2] * unit_y * (4.0 * square_z - square_x - square_y),
        sh_c3[3] * unit_z * (2.0 * square_z - 3.0 * square_x - 3.0 * square_y),
        sh_c3[4] * unit_x * (4.0 * square_z - square_x - square_y),
        sh_c3[5] * unit_z * (square_x - square_y),
        sh_c3[6] * unit_x * (square_x - 3.0 * square_y),
    ]
    colors = []
    for channel in range(3):
        summed = 0.5 + sh_c0 * coefficients[channel]
        for index_k in range(15):
            summed = summed + basis_list[index_k] * coefficients[3 * (index_k + 1) + channel]
        colors.append(jnp.maximum(summed, 0.0))
    return colors


def project(values, camera):
    points = [values[0], values[1], values[2]]
    matrix = [[camera[3 * row_at + col_at] for col_at in range(3)] for row_at in range(3)]
    translation = [camera[9], camera[10], camera[11]]
    focal_len = camera[12]
    viewed = [
        matrix[row_at][0] * points[0]
        + matrix[row_at][1] * points[1]
        + matrix[row_at][2] * points[2]
        + translation[row_at]
        for row_at in range(3)
    ]
    inverse_depth = 1.0 / viewed[2]
    screen_x = focal_len * viewed[0] * inverse_depth + 0.5 * IMG_W
    screen_y = focal_len * viewed[1] * inverse_depth + 0.5 * IMG_H
    slope_x = focal_len * viewed[0] * inverse_depth * inverse_depth
    slope_y = focal_len * viewed[1] * inverse_depth * inverse_depth
    jac_w = [
        [
            focal_len * inverse_depth * matrix[0][col_at] - slope_x * matrix[2][col_at]
            for col_at in range(3)
        ],
        [
            focal_len * inverse_depth * matrix[1][col_at] - slope_y * matrix[2][col_at]
            for col_at in range(3)
        ],
    ]
    quat_len = jnp.sqrt(
        values[6] * values[6]
        + values[7] * values[7]
        + values[8] * values[8]
        + values[9] * values[9]
    )
    quat_w = values[6] / quat_len
    quat_x = values[7] / quat_len
    quat_y = values[8] / quat_len
    quat_z = values[9] / quat_len
    rotation = [
        [
            1.0 - 2.0 * (quat_y * quat_y + quat_z * quat_z),
            2.0 * (quat_x * quat_y - quat_w * quat_z),
            2.0 * (quat_x * quat_z + quat_w * quat_y),
        ],
        [
            2.0 * (quat_x * quat_y + quat_w * quat_z),
            1.0 - 2.0 * (quat_x * quat_x + quat_z * quat_z),
            2.0 * (quat_y * quat_z - quat_w * quat_x),
        ],
        [
            2.0 * (quat_x * quat_z - quat_w * quat_y),
            2.0 * (quat_y * quat_z + quat_w * quat_x),
            1.0 - 2.0 * (quat_x * quat_x + quat_y * quat_y),
        ],
    ]
    extent = [jnp.exp(values[3]), jnp.exp(values[4]), jnp.exp(values[5])]
    spread = [
        [
            (
                jac_w[row_at][0] * rotation[0][col_at]
                + jac_w[row_at][1] * rotation[1][col_at]
                + jac_w[row_at][2] * rotation[2][col_at]
            )
            * extent[col_at]
            for col_at in range(3)
        ]
        for row_at in range(2)
    ]
    cov_a = (
        spread[0][0] * spread[0][0]
        + spread[0][1] * spread[0][1]
        + spread[0][2] * spread[0][2]
        + blur_add
    )
    cov_b = spread[0][0] * spread[1][0] + spread[0][1] * spread[1][1] + spread[0][2] * spread[1][2]
    cov_c = (
        spread[1][0] * spread[1][0]
        + spread[1][1] * spread[1][1]
        + spread[1][2] * spread[1][2]
        + blur_add
    )
    determinant = cov_a * cov_c - cov_b * cov_b
    logit = values[10]
    log_opacity = jnp.minimum(logit, 0.0) - jnp.log(1.0 + jnp.exp(-jnp.abs(logit)))
    center = [
        -(
            matrix[0][col_at] * translation[0]
            + matrix[1][col_at] * translation[1]
            + matrix[2][col_at] * translation[2]
        )
        for col_at in range(3)
    ]
    offset = [points[col_at] - center[col_at] for col_at in range(3)]
    distance = jnp.sqrt(offset[0] * offset[0] + offset[1] * offset[1] + offset[2] * offset[2])
    colors = sh_color(
        values[11:PARAMS], offset[0] / distance, offset[1] / distance, offset[2] / distance
    )
    return [
        screen_x,
        screen_y,
        cov_c / determinant,
        -cov_b / determinant,
        cov_a / determinant,
        log_opacity,
    ] + colors


def iota(shape, dim):
    return lax.broadcasted_iota(jnp.int32, shape, dim)


def mxu(left, right):
    return jnp.dot(left, right, preferred_element_type=F32)


def mxu_bt(left, right):
    return lax.dot_general(left, right, (((1,), (1,)), ((), ())), preferred_element_type=F32)


def split_two(value):
    high = value.astype(BF16)
    low = (value - high.astype(F32)).astype(BF16)
    return high, low


def split_three(value):
    high = value.astype(BF16).astype(F32)
    rest = value - high
    middle = rest.astype(BF16).astype(F32)
    low = (rest - middle).astype(BF16).astype(F32)
    return high, middle, low


def upper_strict():
    return (iota((BLOCK, BLOCK), 0) < iota((BLOCK, BLOCK), 1)).astype(F32).astype(BF16)


def route_kernel(view_ref, count_ref, owner_ref, local_ref, req_ref, entry_ref):
    tri = upper_strict()
    owners_at = iota((DEVS, BLOCK), 0)
    ranks_at = iota((DEVS, BLOCK), 0)
    before = jnp.zeros((DEVS, 1), F32)
    total_hi = jnp.zeros((DEVS, DEVS), F32)
    total_lo = jnp.zeros((DEVS, DEVS), F32)
    for tile in range(TILES):
        view = view_ref[tile]
        for block in range(NBLK):
            alive = block < count_ref[tile]
            span = slice(block * BLOCK, (block + 1) * BLOCK)
            owner = jnp.where(alive, owner_ref[tile : tile + 1, span], -1)
            local = local_ref[tile : tile + 1, span]
            hit = owners_at == owner
            one_hot = hit.astype(F32)
            one_hot_b = one_hot.astype(BF16)
            earlier = mxu(one_hot_b, tri) + before
            rank = jnp.sum(one_hot * earlier, axis=0, keepdims=True)
            before = before + jnp.sum(one_hot, axis=1, keepdims=True)
            rank = jnp.where(owner >= 0, rank.astype(jnp.int32), -1)
            code = (
                view * GDEV
                + ((local >> 7) & 1) * HALF
                + ((local >> 8) << 7)
                + (local & 127)
                + 1
            )
            at_rank = ranks_at == rank
            high = jnp.where(at_rank, (code >> 8).astype(F32), 0.0).astype(BF16)
            low = jnp.where(at_rank, (code & 255).astype(F32), 0.0).astype(BF16)
            total_hi = total_hi + mxu_bt(one_hot_b, high)
            total_lo = total_lo + mxu_bt(one_hot_b, low)
            at = tile * NBLK + block
            entry_ref[at, 0:1, :] = owner
            entry_ref[at, 1:2, :] = rank
    req_ref[...] = (total_hi * 256.0 + total_lo).astype(jnp.int32) - 1


def route(tile_view, block_counts, entry_owner, entry_local):
    return pl.pallas_call(
        route_kernel,
        name="route",
        out_shape=(
            jax.ShapeDtypeStruct((DEVS, DEVS), jnp.int32),
            jax.ShapeDtypeStruct((TILES * NBLK, 8, BLOCK), jnp.int32),
        ),
        in_specs=[
            pl.BlockSpec(memory_space=pltpu.SMEM),
            pl.BlockSpec(memory_space=pltpu.SMEM),
            pl.BlockSpec(memory_space=pltpu.VMEM),
            pl.BlockSpec(memory_space=pltpu.VMEM),
        ],
        out_specs=(pl.BlockSpec(memory_space=pltpu.VMEM), pl.BlockSpec(memory_space=pltpu.VMEM)),
        compiler_params=pltpu.CompilerParams(vmem_limit_bytes=24 << 20),
    )(tile_view, block_counts, entry_owner, entry_local)


COLS = 2048


def table_kernel(params_ref, table_ref, pad_ref):
    @pl.when(pl.program_id(0) == 0)
    def _():
        pad_ref[...] = jnp.zeros_like(pad_ref)

    for at in range(COLS // 256):
        pad_ref[at, 0:PARAMS, :] = params_ref[:, at * 256 : at * 256 + 128]
        pad_ref[at, 64 : 64 + PARAMS, :] = params_ref[:, at * 256 + 128 : at * 256 + 256]
        table_ref[at * 128 : (at + 1) * 128, :] = pad_ref[at].T


def table_of(params):
    return pl.pallas_call(
        table_kernel,
        name="table",
        grid=(GDEV // COLS,),
        out_shape=jax.ShapeDtypeStruct((HALF, 128), F32),
        in_specs=[pl.BlockSpec((PARAMS, COLS), lambda i: (0, i))],
        out_specs=pl.BlockSpec((COLS // 2, 128), lambda i: (i, 0)),
        scratch_shapes=[pltpu.VMEM((COLS // 256, 128, 128), F32)],
        compiler_params=pltpu.CompilerParams(vmem_limit_bytes=24 << 20),
        cost_estimate=pl.CostEstimate(flops=1 << 20, bytes_accessed=9 << 20, transcendentals=0),
    )(params)


def cameras_of(camera_ref, view):
    return [
        jnp.where(
            view == 0,
            camera_ref[0, at],
            jnp.where(
                view == 1,
                camera_ref[1, at],
                jnp.where(view == 2, camera_ref[2, at], camera_ref[3, at]),
            ),
        )
        for at in range(13)
    ]


def reply_kernel(
    code_ref, camera_ref, code_vec_ref, table_ref, reply_ref, rows_ref, code_t_ref, got_ref, proj_ref
):
    code_t_ref[...] = code_vec_ref[...].T
    proj_ref[USED:WIDE, :] = jnp.zeros((WIDE - USED, DEVS), F32)

    def gather(rank, carry):
        for src in range(DEVS):
            row = code_ref[src, rank] & (HALF - 1)
            got_ref[src : src + 1, :] = table_ref[pl.ds(row, 1), :]
        both = got_ref[...].T
        half = (code_t_ref[pl.ds(rank, 1), :] >> 13) & 1
        picked = jnp.where(half == 0, both[0:64], both[64:128])
        for group in range(8):
            rows_ref[pl.ds(group * 8 * CAP + rank, 8, stride=CAP), :] = picked[
                group * 8 : (group + 1) * 8
            ]
        return carry

    lax.fori_loop(0, CAP, gather, 0)

    def chunk(at, carry):
        base = pl.multiple_of(at * 8, 8)
        values = [rows_ref[pl.ds(k * CAP + base, 8), :] for k in range(PARAMS)]
        view = (code_t_ref[pl.ds(base, 8), :] >> 14) & 3
        for k, value in enumerate(project(values, cameras_of(camera_ref, view))):
            proj_ref[pl.ds(k * CAP + base, 8), :] = value
        return carry

    lax.fori_loop(0, CAP // 8, chunk, 0)
    for part in range(WIDE // 128):
        span = slice(part * 128, (part + 1) * 128)
        reply_ref[:, span] = proj_ref[span, :].T


def reply_of(codes, cameras, table):
    return pl.pallas_call(
        reply_kernel,
        name="reply",
        out_shape=(
            jax.ShapeDtypeStruct((DEVS, WIDE), F32),
            jax.ShapeDtypeStruct((64 * CAP, DEVS), F32),
        ),
        in_specs=[
            pl.BlockSpec(memory_space=pltpu.SMEM),
            pl.BlockSpec(memory_space=pltpu.SMEM),
            pl.BlockSpec(memory_space=pltpu.VMEM),
            pl.BlockSpec(memory_space=pltpu.VMEM),
        ],
        out_specs=(pl.BlockSpec(memory_space=pltpu.VMEM), pl.BlockSpec(memory_space=pltpu.VMEM)),
        scratch_shapes=[
            pltpu.VMEM((DEVS, DEVS), jnp.int32),
            pltpu.VMEM((DEVS, 128), F32),
            pltpu.VMEM((WIDE, DEVS), F32),
        ],
        compiler_params=pltpu.CompilerParams(vmem_limit_bytes=32 << 20),
    )(codes, cameras, codes, table)


def render_kernel(
    view_ref,
    spot_ref,
    count_ref,
    gain_ref,
    d_image_ref,
    entry_ref,
    arrived_ref,
    back_ref,
    split_ref,
    tri_ref,
    low_ref,
    basis_t_ref,
    basis_ref,
    vals_ref,
    alpha_ref,
    q_ref,
    color_grad_ref,
    shade_ref,
):
    for part in range(WIDE // 128):
        span = slice(part * 128, (part + 1) * 128)
        flipped = arrived_ref[:, span].T
        for piece, value in enumerate(split_three(flipped)):
            split_ref[piece, span, :] = value.astype(BF16)
    tri_ref[...] = upper_strict()
    low_ref[...] = (
        (iota((BLOCK, BLOCK), 0) > iota((BLOCK, BLOCK), 1)).astype(F32).astype(BF16)
    )

    def monomial(which, x, y):
        return jnp.where(
            which == 0,
            1.0,
            jnp.where(
                which == 1,
                x,
                jnp.where(
                    which == 2,
                    y,
                    jnp.where(
                        which == 3,
                        x * x,
                        jnp.where(which == 4, x * y, jnp.where(which == 5, y * y, 0.0)),
                    ),
                ),
            ),
        )

    pixel = iota((TPIX, 128), 0)
    lane = iota((TPIX, 128), 1)
    basis_t_ref[...] = jnp.where(
        lane < 24,
        monomial(lane & 7, (pixel & 15).astype(F32) - 7.5, (pixel >> 4).astype(F32) - 7.5),
        0.0,
    ).astype(BF16)
    pixel = iota((16, TPIX), 1)
    basis_ref[...] = monomial(
        iota((16, TPIX), 0), (pixel & 15).astype(F32) - 7.5, (pixel >> 4).astype(F32) - 7.5
    ).astype(BF16)
    back_ref[...] = jnp.zeros_like(back_ref)
    owners_at = iota((DEVS, BLOCK), 0)
    ranks_at = iota((CAP, BLOCK), 0)
    row8 = iota((8, BLOCK), 0)

    def rows8(rows):
        out = jnp.zeros((8, BLOCK), F32)
        for at, row in enumerate(rows):
            out = jnp.where(row8 == at, row, out)
        return out

    def tile_step(tile, expo):
        view = view_ref[tile]
        spot = spot_ref[tile]
        line = spot // ACROSS
        mid_x = ((spot - line * ACROSS) * TILE + TILE // 2).astype(F32)
        mid_y = (line * TILE + TILE // 2).astype(F32)
        gains = [gain_ref[view, ch] for ch in range(3)]
        d_rows = [d_image_ref[tile, ch : ch + 1, :] for ch in range(3)]
        d_raw = rows8(d_rows)
        d1, d2, d3 = split_three(d_raw)
        pixel_rows = jnp.concatenate([d1, d2, d3, jnp.zeros((8, TPIX), F32)], axis=0).astype(BF16)
        g1, g2, g3 = split_three(rows8([gains[ch] * d_rows[ch] for ch in range(3)]))
        shade_ref[...] = (
            jnp.concatenate([g1, g1, g2, g2, g1, g3, jnp.zeros((80, TPIX), F32)], axis=0)
            .T.astype(BF16)
        )
        blocks = count_ref[tile]

        def forward(block, carried):
            level, expo_rows = carried
            at = tile * NBLK + block
            owner = entry_ref[at, 0:1, :]
            rank = entry_ref[at, 1:2, :]
            one_hot = (owners_at == owner).astype(F32).astype(BF16)
            found = (
                mxu(split_ref[0, 0:USED, :], one_hot)
                + mxu(split_ref[1, 0:USED, :], one_hot)
                + mxu(split_ref[2, 0:USED, :], one_hot)
            )
            here = ranks_at == rank
            vals = [
                jnp.sum(
                    jnp.where(here, found[k * CAP : (k + 1) * CAP], 0.0), axis=0, keepdims=True
                )
                for k in range(VALS)
            ]
            shift_x = vals[0] - mid_x
            shift_y = vals[1] - mid_y
            con_a, con_b, con_c = vals[2], vals[3], vals[4]
            lin_x = con_a * shift_x + con_b * shift_y
            lin_y = con_c * shift_y + con_b * shift_x
            poly = rows8(
                [
                    vals[5] - 0.5 * (lin_x * shift_x + lin_y * shift_y),
                    lin_x,
                    lin_y,
                    -0.5 * con_a,
                    -con_b,
                    -0.5 * con_c,
                ]
            )
            vals_ref[block] = rows8([shift_x, shift_y, con_a, con_b, con_c])
            k1, k2, k3 = split_three(poly)
            poly_rows = jnp.concatenate(
                [k1, k2, k3, jnp.zeros((104, BLOCK), F32)], axis=0
            ).astype(BF16)
            color = rows8(vals[6:9])
            c1, c2, c3 = split_three(color)
            color_rows = jnp.concatenate(
                [c1, c2, c1, c2, c3, c1, jnp.zeros((80, BLOCK), F32)], axis=0
            ).astype(BF16)
            alpha = jnp.exp(mxu(basis_t_ref[...], poly_rows))
            fade = alpha * (1.0 + alpha * (0.5 + alpha * (1.0 / 3.0)))
            fade_hi, fade_lo = split_two(fade)
            summed = mxu(fade_hi, tri_ref[...]) + mxu(fade_lo, tri_ref[...]) + level
            weight = alpha * jnp.exp(-summed)
            level = summed[:, BLOCK - 1 : BLOCK] + fade[:, BLOCK - 1 : BLOCK]
            q_val = mxu(shade_ref[...], color_rows) * weight
            alpha_ref[block] = alpha
            q_ref[block] = q_val
            weight_hi, weight_lo = split_two(weight)
            seen = mxu(pixel_rows, weight_hi) + mxu(pixel_rows, weight_lo)
            seen = seen[0:8] + seen[8:16] + seen[16:24]
            color_grad_ref[block] = seen
            return level, expo_rows + color * seen

        level0 = jnp.zeros((TPIX, 1), F32)
        unused, expo_rows = lax.fori_loop(
            0, blocks, forward, (level0, jnp.zeros((8, BLOCK), F32))
        )
        expo_cols = jnp.sum(expo_rows, axis=1, keepdims=True)

        def backward(step, tail):
            block = blocks - 1 - step
            at = tile * NBLK + block
            owner = entry_ref[at, 0:1, :]
            rank = entry_ref[at, 1:2, :]
            alpha = alpha_ref[block]
            q_val = q_ref[block]
            q_hi, q_lo = split_two(q_val)
            later = mxu(q_hi, low_ref[...]) + mxu(q_lo, low_ref[...]) + tail
            d_exp = q_val - later * (alpha * (1.0 + alpha * (1.0 + alpha)))
            tail = later[:, 0:1] + q_val[:, 0:1]
            d_hi, d_lo = split_two(d_exp)
            grad = mxu(basis_ref[...], d_hi) + mxu(basis_ref[...], d_lo)
            d_poly = [grad[k : k + 1] for k in range(6)]
            held = vals_ref[block]
            shift_x, shift_y, con_a, con_b, con_c = [held[k : k + 1] for k in range(5)]
            lin_x = con_a * shift_x + con_b * shift_y
            lin_y = con_c * shift_y + con_b * shift_x
            seen = color_grad_ref[block]
            grads = [
                d_poly[1] * con_a + d_poly[2] * con_b - d_poly[0] * lin_x,
                d_poly[1] * con_b + d_poly[2] * con_c - d_poly[0] * lin_y,
                shift_x * d_poly[1] - 0.5 * (d_poly[3] + shift_x * shift_x * d_poly[0]),
                shift_y * d_poly[1]
                + shift_x * d_poly[2]
                - d_poly[4]
                - shift_x * shift_y * d_poly[0],
                shift_y * d_poly[2] - 0.5 * (d_poly[5] + shift_y * shift_y * d_poly[0]),
                d_poly[0],
                gains[0] * seen[0:1],
                gains[1] * seen[1:2],
                gains[2] * seen[2:3],
            ]
            one_hot = (owners_at == owner).astype(F32).astype(BF16)
            here = ranks_at == rank
            high_rows = []
            low_rows = []
            for value in grads:
                high = value.astype(BF16).astype(F32)
                high_rows.append(jnp.where(here, high, 0.0).astype(BF16))
                low_rows.append(jnp.where(here, value - high, 0.0).astype(BF16))
            back_ref[:, 0:USED] += mxu_bt(one_hot, jnp.concatenate(high_rows, axis=0)) + mxu_bt(
                one_hot, jnp.concatenate(low_rows, axis=0)
            )
            return tail

        lax.fori_loop(0, blocks, backward, jnp.zeros((TPIX, 1), F32))
        lane_at = iota((8, 128), 1) - (USED - 384) - 3 * view
        return expo + jnp.where(lane_at == iota((8, 128), 0), expo_cols, 0.0)

    expo = lax.fori_loop(0, TILES, tile_step, jnp.zeros((8, 128), F32))
    lane = iota((8, 128), 1)
    expo = jnp.where((lane >= USED - 384) & (lane < USED - 384 + 12), expo, 0.0)
    back_ref[:, 384:WIDE] += jnp.sum(expo, axis=0, keepdims=True)


def render_of(tile_view, tile_spot, block_counts, exposure, d_image, entries, arrived):
    smem = pl.BlockSpec(memory_space=pltpu.SMEM)
    vmem = pl.BlockSpec(memory_space=pltpu.VMEM)
    return pl.pallas_call(
        render_kernel,
        name="render",
        out_shape=jax.ShapeDtypeStruct((DEVS, WIDE), F32),
        in_specs=[smem, smem, smem, smem, vmem, vmem, vmem],
        out_specs=vmem,
        scratch_shapes=[
            pltpu.VMEM((3, WIDE, DEVS), BF16),
            pltpu.VMEM((BLOCK, BLOCK), BF16),
            pltpu.VMEM((BLOCK, BLOCK), BF16),
            pltpu.VMEM((TPIX, 128), BF16),
            pltpu.VMEM((16, TPIX), BF16),
            pltpu.VMEM((NBLK, 8, BLOCK), F32),
            pltpu.VMEM((NBLK, TPIX, BLOCK), F32),
            pltpu.VMEM((NBLK, TPIX, BLOCK), F32),
            pltpu.VMEM((NBLK, 8, BLOCK), F32),
            pltpu.VMEM((TPIX, 128), BF16),
        ],
        compiler_params=pltpu.CompilerParams(vmem_limit_bytes=32 << 20),
    )(tile_view, tile_spot, block_counts, exposure, d_image, entries, arrived)


def collect_kernel(
    code_ref,
    camera_ref,
    code_vec_ref,
    arrived_ref,
    rows_ref,
    total_ref,
    expo_ref,
    code_t_ref,
    cot_ref,
    grad_ref,
    spread_ref,
    *tables,
):
    code_t_ref[...] = code_vec_ref[...].T
    expo_ref[...] = jnp.broadcast_to(
        jnp.sum(arrived_ref[:, 384:WIDE], axis=0, keepdims=True), (8, 128)
    )
    for part in range(WIDE // 128):
        span = slice(part * 128, (part + 1) * 128)
        cot_ref[span, :] = arrived_ref[:, span].T
    for table in tables:
        table[...] = jnp.zeros_like(table)
    grad_ref[PARAMS * CAP :, :] = jnp.zeros(((64 - PARAMS) * CAP, DEVS), F32)

    def chunk(at, carry):
        base = pl.multiple_of(at * 8, 8)
        values = [rows_ref[pl.ds(k * CAP + base, 8), :] for k in range(PARAMS)]
        code = code_t_ref[pl.ds(base, 8), :]
        camera = cameras_of(camera_ref, (code >> 14) & 3)
        unused, pull = jax.vjp(lambda held: project(held, camera), values)
        (grads,) = pull([cot_ref[pl.ds(k * CAP + base, 8), :] for k in range(VALS)])
        for k in range(PARAMS):
            grad_ref[pl.ds(k * CAP + base, 8), :] = jnp.where(code >= 0, grads[k], 0.0)
        return carry

    lax.fori_loop(0, CAP // 8, chunk, 0)

    def scatter(rank, carry):
        half = (code_t_ref[pl.ds(rank, 1), :] >> 13) & 1
        mine = jnp.concatenate(
            [
                grad_ref[pl.ds(group * 8 * CAP + rank, 8, stride=CAP), :]
                for group in range(8)
            ],
            axis=0,
        )
        both = jnp.concatenate(
            [jnp.where(half == 0, mine, 0.0), jnp.where(half == 1, mine, 0.0)], axis=0
        )
        spread_ref[...] = both.T
        for src in range(DEVS):
            row = code_ref[src, rank] & (HALF - 1)
            table = tables[src % TABLES]
            table[pl.ds(row, 1), :] = table[pl.ds(row, 1), :] + spread_ref[src : src + 1, :]
        return carry

    lax.fori_loop(0, CAP, scatter, 0)

    def merge(at, carry):
        span = pl.ds(pl.multiple_of(at * 128, 128), 128)
        total = tables[0][span, :]
        for table in tables[1:]:
            total = total + table[span, :]
        total_ref[span, :] = total
        return carry

    lax.fori_loop(0, HALF // 128, merge, 0)


def collect_of(codes, cameras, arrived, rows):
    smem = pl.BlockSpec(memory_space=pltpu.SMEM)
    vmem = pl.BlockSpec(memory_space=pltpu.VMEM)
    return pl.pallas_call(
        collect_kernel,
        name="collect",
        out_shape=(
            jax.ShapeDtypeStruct((HALF, 128), F32),
            jax.ShapeDtypeStruct((8, 128), F32),
        ),
        in_specs=[smem, smem, vmem, vmem, vmem],
        out_specs=(vmem, vmem),
        scratch_shapes=[
            pltpu.VMEM((DEVS, DEVS), jnp.int32),
            pltpu.VMEM((WIDE, DEVS), F32),
            pltpu.VMEM((64 * CAP, DEVS), F32),
            pltpu.VMEM((DEVS, 128), F32),
        ]
        + [pltpu.VMEM((HALF, 128), F32)] * TABLES,
        compiler_params=pltpu.CompilerParams(vmem_limit_bytes=48 << 20),
    )(codes, cameras, codes, arrived, rows)


def adam_kernel(total_ref, params_ref, m_ref, v_ref, params_out, m_out, v_out, flip_ref):
    for at in range(COLS // 256):
        flip_ref[at] = total_ref[at * 128 : (at + 1) * 128, :].T
        for half in range(2):
            span = slice(at * 256 + half * 128, at * 256 + (half + 1) * 128)
            gradient = flip_ref[at, half * 64 : half * 64 + PARAMS, :]
            new_m = beta_first * m_ref[:, span] + (1.0 - beta_first) * gradient
            new_v = beta_second * v_ref[:, span] + (1.0 - beta_second) * gradient * gradient
            m_out[:, span] = new_m
            v_out[:, span] = new_v
            params_out[:, span] = params_ref[:, span] - learn_rate * (new_m / fix_first) / (
                jnp.sqrt(new_v / fix_second) + adam_eps
            )


def adam_of(total, params, adam_m, adam_v):
    wide = pl.BlockSpec((PARAMS, COLS), lambda i: (0, i))
    return pl.pallas_call(
        adam_kernel,
        name="adam",
        grid=(GDEV // COLS,),
        out_shape=(jax.ShapeDtypeStruct((PARAMS, GDEV), F32),) * 3,
        in_specs=[pl.BlockSpec((COLS // 2, 128), lambda i: (i, 0)), wide, wide, wide],
        out_specs=(wide, wide, wide),
        scratch_shapes=[pltpu.VMEM((COLS // 256, 128, 128), F32)],
        compiler_params=pltpu.CompilerParams(vmem_limit_bytes=32 << 20),
    )(total, params, adam_m, adam_v)


def exchange(value):
    return lax.all_to_all(value, AXES, split_axis=0, concat_axis=0, tiled=True)


def body(
    params,
    adam_m,
    adam_v,
    cameras,
    exposure,
    entry_owner,
    entry_local,
    block_counts,
    tile_view,
    tile_spot,
    d_image,
):
    requests, entries = route(tile_view, block_counts, entry_owner, entry_local)
    codes = exchange(requests)
    table = table_of(params)
    reply, rows = reply_of(codes, cameras, table)
    arrived = exchange(reply)
    back = render_of(tile_view, tile_spot, block_counts, exposure, d_image, entries, arrived)
    returned = exchange(back)
    total, expo = collect_of(codes, cameras, returned, rows)
    new_params, new_m, new_v = adam_of(total, params, adam_m, adam_v)
    first = USED - 384
    exposure_grad = expo[0, first : first + 12].reshape(4, 3) / DEVS
    return (new_params, new_m, new_v, exposure_grad)


def solution(mesh):
    both = ("tiles", "gauss")
    placed = (
        P(None, both),
        P(None, both),
        P(None, both),
        P(),
        P(),
        P(both, None),
        P(both, None),
        P(both),
        P(both),
        P(both),
        P(both, None, None),
    )
    return jax.shard_map(
        body,
        mesh=mesh,
        in_specs=placed,
        out_specs=(P(None, both), P(None, both), P(None, both), P()),
        check_vma=False,
    )
```

time: 869 us -> 147 us (0.17); the launches traced: 853 us -> 147 us
  other arithmetic: 399 us -> 0.09 us
  local copies, waits for them, and re-layouts: 226 us -> 21.8 us
  Pallas kernels: 0 us -> 71.8 us
  blocking collectives: 75.3 us -> 20.2 us
  matrix products: 51.3 us -> 0 us
  loops' own time: 51 us -> 0 us
  waiting for transfers between devices: 25.6 us -> 14 us
    gather x18 -> x0, local copies, waits for them, and re-layouts: 104 us -> none  [the longest x1 24.7 us: body(): ranked = jnp.arange(entries, dtype=jnp.int32) - starts[sorted_owner]]
    mul x142 -> x0, other arithmetic: 89.8 us -> none  [the longest x4 39 us: project(): screen_y = focal_len * viewed[1] * inverse_depth + 0.5 * IMG_H]
    psum x1 -> x0, blocking collectives: 75.3 us -> none  [body(): exposure_grad = lax.psum(expo_local, ('tiles', 'gauss')) / devices]
    pallas_call x0 -> x6, Pallas kernels: none -> 71.8 us  [the longest x1 24.5 us: render_of(): pl.pallas_call(render_kernel, name='render', out_shape=jax.ShapeDtypeStru...]
    add_any x32 -> x0, other arithmetic: 71.7 us -> none  [the longest x4 29.9 us: project(): cov_c / determinant]
    scatter x3 -> x0, local copies, waits for them, and re-layouts: 53.7 us -> none  [the longest x1 22.6 us: body(): jnp.zeros((PARAMS, devices * capacity), jnp.float32).at[:, target]]
    another operation x157 -> x0, other arithmetic: 53.4 us -> none
    dot_general x51 -> x0, matrix products: 51.3 us -> none  [the longest x48 50.7 us: block_step(): jnp.dot(block_rows[6:9], weights, precision=lax.Precision.HIGHEST)]
  transfers between devices with their start and end apart: 3 -> 2, of which waited for: 2 -> 2; matrix products, arithmetic and copies ran while one was open for 1% -> 0% of each run, Pallas kernels for 0% -> 1%
where the time goes in v1:
time: 147 us
  Pallas kernels  71.8 us (49%)
  local copies, waits for them, and re-layouts  21.8 us (15%)
  blocking collectives  20.2 us (14%)
  starting transfers between devices  18.2 us (12%)
  waiting for transfers between devices  14 us (10%)
    pallas_call x1, Pallas kernels, render_of(): pl.pallas_call(render_kernel, name='render', out_shape=jax.ShapeDtypeStru...  24.5 us
    all_to_all x1, blocking collectives, exchange(): return lax.all_to_all(value, AXES, split_axis=0, concat_axis=0, tiled=True)  20.2 us
    unnamed x39, local copies, waits for them, and re-layouts  19.9 us
    pallas_call x1, Pallas kernels, collect_of(): pl.pallas_call(collect_kernel, name='collect', out_shape=(jax.ShapeDtypeS...  18.5 us
    all_to_all x2, starting transfers between devices, exchange(): return lax.all_to_all(value, AXES, split_axis=0, concat_axis=0, tiled=True)  18.2 us
    pallas_call x1, Pallas kernels, reply_of(): pl.pallas_call(reply_kernel, name='reply', out_shape=(jax.ShapeDtypeStruc...  14.4 us
    all_to_all x2, waiting for transfers between devices, exchange(): return lax.all_to_all(value, AXES, split_axis=0, concat_axis=0, tiled=True)  14 us
    pallas_call x1, Pallas kernels, adam_of(): pl.pallas_call(adam_kernel, name='adam', grid=(GDEV // COLS,), out_shape=...  7.16 us
  transfers between devices with their start and end apart: 2, of which 2 were waited for; matrix products, arithmetic and copies ran while one was open for 0% of the time, Pallas kernels for 1%

profile of v1, /device:TPU:1, one launch (start us, length us, event | category | flops | bytes accessed | tf_op | source)
XLA Modules:
  0.0 146.9 jit_solution(13828759023417378979)
XLA Ops:
  0.6 0.0 copy-start.8
  0.6 0.7 copy-done.8
  1.3 0.0 copy-start.9
  1.4 0.7 copy-done.9
  2.1 0.0 copy-start.12
  2.1 0.7 copy-done.12
  2.7 0.0 copy-start.14
  2.7 0.7 copy-done.14
  3.4 5.2 %route.1 = (s32[128,128]{1,0:T(8,128)}, s32[16,8,256]{2,1,0:T(8,128)S(1)}) custom-call(s32[4]{0:T(128)S(1)} %copy-done.12, s32[4]{0:T(128)S(1)} %copy-done.14, s32[4,1024]{1,0:T(4,128)S(1)} %copy-done.8, s32[4,1024]{1,0:T(4,128)S(1)} %copy-done.9), custom_call_target="tpu_custom_call" | custom-call | tf_op jit(solution)/shard_map/route/pallas_call | solution.py:265
  8.6 11.5 %all-to-all-start = ((s32[128,1,128]{2,1,0:T(1,128)}), s32[128,1,128]{2,1,0:T(1,128)S(1)}, u32[]{:S(2)}, u32[]{:S(2)}) async-start(s32[128,1,128]{2,1,0:T(1,128)} %bitcast.1), calls=%async_computation | async-start | bytes 131072 | tf_op jit(solution)/shard_map/all_to_all | solution.py:742
  20.1 0.0 copy-start.2
  20.1 2.2 %copy-done.2 = f32[59,16384]{1,0:T(8,128)S(1)} copy-done((f32[59,16384]{1,0:T(8,128)S(1)}, f32[59,16384]{1,0:T(8,128)}, u32[]{:S(2)}) %copy-start.2) | copy-done | bytes 3866648
  22.3 0.0 copy-start.10
  22.3 0.0 copy-start.17
  22.3 0.0 copy-start.11
  22.3 2.0 %table.1.table_ref = f32[8192,128]{1,0:T(8,128)S(1)} custom-call(f32[59,16384]{1,0:T(8,128)S(1)} %copy-done.2), custom_call_target="tpu_custom_call" | custom-call | flops 1048576 | bytes 9437184 | tf_op jit(solution)/shard_map/table/pallas_call | solution.py:298
  24.3 0.0 copy-start
  24.3 2.0 %copy-done = f32[8192,128]{1,0:T(8,128)} copy-done((f32[8192,128]{1,0:T(8,128)}, f32[8192,128]{1,0:T(8,128)S(1)}, u32[]{:S(2)}) %copy-start) | copy-done | bytes 4194328
  26.3 0.0 copy-start.13
  26.3 0.0 copy-start.15
  26.3 0.0 copy-start.16
  26.3 3.1 %all-to-all-done = s32[128,1,128]{2,1,0:T(1,128)S(1)} async-done(((s32[128,1,128]{2,1,0:T(1,128)}), s32[128,1,128]{2,1,0:T(1,128)S(1)}, u32[]{:S(2)}, u32[]{:S(2)}) %all-to-all-start) | async-done | bytes 65568 | tf_op jit(solution)/shard_map/all_to_all | solution.py:742
  29.5 0.0 copy-done.10
  29.5 0.0 copy-start.1
  29.5 2.2 %copy-done.1 = f32[8192,128]{1,0:T(8,128)S(1)} copy-done((f32[8192,128]{1,0:T(8,128)S(1)}, f32[8192,128]{1,0:T(8,128)}, u32[]{:S(2)}) %copy-start.1) | copy-done | bytes 4194328
  31.6 14.4 %reply.1 = (f32[128,512]{1,0:T(8,128)S(1)}, f32[3072,128]{1,0:T(8,128)S(1)}) custom-call(s32[128,128]{1,0:T(8,128)S(1)} %bitcast.12, f32[4,13]{1,0:T(4,128)S(1)} %copy-done.10, s32[128,128]{1,0:T(8,128)S(1)} %bitcast.13, f32[8192,128]{1,0:T(8,128)S(1)} %copy-done.1), custom_call_target="tpu_custom_call" | custom-call | tf_op jit(solution)/shard_map/reply/pallas_call | solution.py:362
  46.1 1.0 copy.17
  47.0 6.7 %all-to-all-start.1 = ((f32[128,1,512]{2,1,0:T(1,128)}), f32[128,1,512]{2,1,0:T(1,128)S(1)}, u32[]{:S(2)}, u32[]{:S(2)}) async-start(f32[128,1,512]{2,1,0:T(1,128)} %copy.17), calls=%async_computation.1 | async-start | bytes 524288 | tf_op jit(solution)/shard_map/all_to_all | solution.py:742
  53.7 0.0 copy-done.17
  53.7 10.9 %all-to-all-done.1 = f32[128,1,512]{2,1,0:T(1,128)S(1)} async-done(((f32[128,1,512]{2,1,0:T(1,128)}), f32[128,1,512]{2,1,0:T(1,128)S(1)}, u32[]{:S(2)}, u32[]{:S(2)}) %all-to-all-start.1) | async-done | bytes 262176 | tf_op jit(solution)/shard_map/all_to_all | solution.py:742
  64.6 0.0 copy-done.11
  64.6 0.0 copy-done.13
  64.6 0.0 copy-done.15
  64.6 0.0 copy-done.16
  64.6 24.5 %render.1 = f32[128,512]{1,0:T(8,128)S(1)} custom-call(s32[4]{0:T(128)S(1)} %copy-done.13, s32[4]{0:T(128)S(1)} %copy-done.16, s32[4]{0:T(128)S(1)} %copy-done.15, f32[4,3]{1,0:T(4,128)S(1)} %copy-done.11, f32[4,3,256]{2,1,0:T(4,128)S(1)} %copy.18.d_image_ref, s32[16,8,256]{2,1,0:T(8,128)S(1)} %get-tuple-element.14.entry_ref, f32[128,512]{1,0:T(8,128)S(1)} %bitcast.17), custom_call_target="tpu_custom_call" | custom-call | tf_op jit(solution)/shard_map/render/pallas_call | solution.py:597
  89.2 0.3 copy.19
  89.5 20.2 %all_to_all.33 = f32[128,1,512]{2,1,0:T(1,128)S(1)} all-to-all(f32[128,1,512]{2,1,0:T(1,128)S(1)} %copy.19), channel_id=1, replica_groups=mesh['tiles'=16,'gauss'=8] {'tiles','gauss'}, dimensions={0} | all-to-all | bytes 524288 | tf_op jit(solution)/shard_map/all_to_all | solution.py:742
  109.7 18.5 %collect.1 = (f32[8192,128]{1,0:T(8,128)S(1)}, f32[8,128]{1,0:T(8,128)S(1)}) custom-call(s32[128,128]{1,0:T(8,128)S(1)} %bitcast.14, f32[4,13]{1,0:T(4,128)S(1)} %copy-done.10, s32[128,128]{1,0:T(8,128)S(1)} %bitcast.15, f32[128,512]{1,0:T(8,128)S(1)} %bitcast.16, f32[3072,128]{1,0:T(8,128)S(1)} %get-tuple-element.16.rows_ref), custom_call_target="tpu_custom_call" | custom-call | tf_op jit(solution)/shard_map/collect/pallas_call | solution.py:692
  128.2 0.0 copy-start.6
  128.3 2.0 %copy-done.6 = f32[8192,128]{1,0:T(8,128)} copy-done((f32[8192,128]{1,0:T(8,128)}, f32[8192,128]{1,0:T(8,128)S(1)}, u32[]{:S(2)}) %copy-start.6) | copy-done | bytes 4194328
  130.3 0.1 multiply_reduce_fusion
  130.3 0.7 div.6
  131.0 0.0 copy-start.3
  131.0 2.2 %copy-done.3 = f32[59,16384]{1,0:T(8,128)S(1)} copy-done((f32[59,16384]{1,0:T(8,128)S(1)}, f32[59,16384]{1,0:T(8,128)}, u32[]{:S(2)}) %copy-start.3) | copy-done | bytes 3866648
  133.2 0.0 copy-start.4
  133.2 2.2 %copy-done.4 = f32[59,16384]{1,0:T(8,128)S(1)} copy-done((f32[59,16384]{1,0:T(8,128)S(1)}, f32[59,16384]{1,0:T(8,128)}, u32[]{:S(2)}) %copy-start.4) | copy-done | bytes 3866648
  135.4 0.0 copy-start.5
  135.4 2.2 %copy-done.5 = f32[59,16384]{1,0:T(8,128)S(1)} copy-done((f32[59,16384]{1,0:T(8,128)S(1)}, f32[59,16384]{1,0:T(8,128)}, u32[]{:S(2)}) %copy-start.5) | copy-done | bytes 3866648
  137.6 0.0 copy-start.7
  137.6 2.2 %copy-done.7 = f32[8192,128]{1,0:T(8,128)S(1)} copy-done((f32[8192,128]{1,0:T(8,128)S(1)}, f32[8192,128]{1,0:T(8,128)}, u32[]{:S(2)}) %copy-start.7) | copy-done | bytes 4194328
  139.8 7.2 %adam.1 = (f32[59,16384]{1,0:T(8,128)}, f32[59,16384]{1,0:T(8,128)}, f32[59,16384]{1,0:T(8,128)}) custom-call(f32[8192,128]{1,0:T(8,128)S(1)} %copy-done.7, f32[59,16384]{1,0:T(8,128)S(1)} %copy-done.3, f32[59,16384]{1,0:T(8,128)S(1)} %copy-done.4, f32[59,16384]{1,0:T(8,128)S(1)} %copy-done.5), custom_call_target="tpu_custom_call" | custom-call | tf_op jit(solution)/shard_map/adam/pallas_call | solution.py:729
  (3 shorter events, 0.0 us)
Async XLA Ops:
  0.6 0.7 copy-start.8
  1.3 0.7 copy-start.9
  2.1 0.7 copy-start.12
  2.7 0.7 copy-start.14
  8.6 20.8 %all-to-all-start = ((s32[128,1,128]{2,1,0:T(1,128)}), s32[128,1,128]{2,1,0:T(1,128)S(1)}, u32[]{:S(2)}, u32[]{:S(2)}) async-start(s32[128,1,128]{2,1,0:T(1,128)} %bitcast.1), calls=%async_computation | async-start | bytes 131072 | tf_op jit(solution)/shard_map/all_to_all | solution.py:742
  20.1 2.2 %copy-start.2 = (f32[59,16384]{1,0:T(8,128)S(1)}, f32[59,16384]{1,0:T(8,128)}, u32[]{:S(2)}) copy-start(f32[59,16384]{1,0:T(8,128)} %params_ref.3) | copy-start | bytes 11599876
  22.3 7.1 %copy-start.10 = (f32[4,13]{1,0:T(4,128)S(1)}, f32[4,13]{1,0:T(4,128)}, u32[]{:S(2)}) copy-start(f32[4,13]{1,0:T(4,128)} %camera_ref.3) | copy-start | bytes 628
  22.3 31.4 %copy-start.17 = (f32[4,3,256]{2,0,1:T(4,128)S(1)}, f32[4,3,256]{2,0,1:T(4,128)}, u32[]{:S(2)}) copy-start(f32[4,3,256]{2,0,1:T(4,128)} %param.21) | copy-start | bytes 36868
  22.3 42.3 %copy-start.11 = (f32[4,3]{1,0:T(4,128)S(1)}, f32[4,3]{1,0:T(4,128)}, u32[]{:S(2)}) copy-start(f32[4,3]{1,0:T(4,128)} %gain_ref.1) | copy-start | bytes 148
  24.3 2.0 %copy-start = (f32[8192,128]{1,0:T(8,128)}, f32[8192,128]{1,0:T(8,128)S(1)}, u32[]{:S(2)}) copy-start(f32[8192,128]{1,0:T(8,128)S(1)} %table.1.table_ref) | copy-start | bytes 12582916
  26.3 38.3 %copy-start.13 = (s32[4]{0:T(128)S(1)}, s32[4]{0:T(128)}, u32[]{:S(2)}) copy-start(s32[4]{0:T(128)} %view_ref.3) | copy-start | bytes 52
  26.3 38.3 %copy-start.15 = (s32[4]{0:T(128)S(1)}, s32[4]{0:T(128)}, u32[]{:S(2)}) copy-start(s32[4]{0:T(128)} %count_ref.3) | copy-start | bytes 52
  26.3 38.3 %copy-start.16 = (s32[4]{0:T(128)S(1)}, s32[4]{0:T(128)}, u32[]{:S(2)}) copy-start(s32[4]{0:T(128)} %spot_ref.1) | copy-start | bytes 52
  29.5 2.2 %copy-start.1 = (f32[8192,128]{1,0:T(8,128)S(1)}, f32[8192,128]{1,0:T(8,128)}, u32[]{:S(2)}) copy-start(f32[8192,128]{1,0:T(8,128)} %copy-done) | copy-start | bytes 12582916
  47.0 17.6 %all-to-all-start.1 = ((f32[128,1,512]{2,1,0:T(1,128)}), f32[128,1,512]{2,1,0:T(1,128)S(1)}, u32[]{:S(2)}, u32[]{:S(2)}) async-start(f32[128,1,512]{2,1,0:T(1,128)} %copy.17), calls=%async_computation.1 | async-start | bytes 524288 | tf_op jit(solution)/shard_map/all_to_all | solution.py:742
  128.2 2.0 %copy-start.6 = (f32[8192,128]{1,0:T(8,128)}, f32[8192,128]{1,0:T(8,128)S(1)}, u32[]{:S(2)}) copy-start(f32[8192,128]{1,0:T(8,128)S(1)} %get-tuple-element.17.total_ref) | copy-start | bytes 12582916
  131.0 2.2 %copy-start.3 = (f32[59,16384]{1,0:T(8,128)S(1)}, f32[59,16384]{1,0:T(8,128)}, u32[]{:S(2)}) copy-start(f32[59,16384]{1,0:T(8,128)} %params_ref.3) | copy-start | bytes 11599876
  133.2 2.2 %copy-start.4 = (f32[59,16384]{1,0:T(8,128)S(1)}, f32[59,16384]{1,0:T(8,128)}, u32[]{:S(2)}) copy-start(f32[59,16384]{1,0:T(8,128)} %m_ref.1) | copy-start | bytes 11599876
  135.4 2.2 %copy-start.5 = (f32[59,16384]{1,0:T(8,128)S(1)}, f32[59,16384]{1,0:T(8,128)}, u32[]{:S(2)}) copy-start(f32[59,16384]{1,0:T(8,128)} %v_ref.1) | copy-start | bytes 11599876
  137.6 2.2 %copy-start.7 = (f32[8192,128]{1,0:T(8,128)S(1)}, f32[8192,128]{1,0:T(8,128)}, u32[]{:S(2)}) copy-start(f32[8192,128]{1,0:T(8,128)} %copy-done.6) | copy-start | bytes 12582916

commit v2 on v1

--- a/solution.py
+++ b/solution.py
@@ -222,8 +222,35 @@
     return (iota((BLOCK, BLOCK), 0) < iota((BLOCK, BLOCK), 1)).astype(F32).astype(BF16)
 
 
-def route_kernel(view_ref, count_ref, owner_ref, local_ref, req_ref, entry_ref):
+def route_kernel(
+    view_hbm,
+    count_hbm,
+    owner_hbm,
+    local_hbm,
+    req_ref,
+    entry_ref,
+    view_ref,
+    count_ref,
+    owner_ref,
+    local_ref,
+    sems,
+):
+    copies = [
+        pltpu.make_async_copy(source, target, sems.at[at])
+        for at, (source, target) in enumerate(
+            (
+                (view_hbm, view_ref),
+                (count_hbm, count_ref),
+                (owner_hbm, owner_ref),
+                (local_hbm, local_ref),
+            )
+        )
+    ]
+    for copy in copies:
+        copy.start()
     tri = upper_strict()
+    for copy in copies:
+        copy.wait()
     owners_at = iota((DEVS, BLOCK), 0)
     ranks_at = iota((DEVS, BLOCK), 0)
     before = jnp.zeros((DEVS, 1), F32)
@@ -236,8 +263,7 @@
             span = slice(block * BLOCK, (block + 1) * BLOCK)
             owner = jnp.where(alive, owner_ref[tile : tile + 1, span], -1)
             local = local_ref[tile : tile + 1, span]
-            hit = owners_at == owner
-            one_hot = hit.astype(F32)
+            one_hot = (owners_at == owner).astype(F32)
             one_hot_b = one_hot.astype(BF16)
             earlier = mxu(one_hot_b, tri) + before
             rank = jnp.sum(one_hot * earlier, axis=0, keepdims=True)
@@ -255,28 +281,33 @@
             low = jnp.where(at_rank, (code & 255).astype(F32), 0.0).astype(BF16)
             total_hi = total_hi + mxu_bt(one_hot_b, high)
             total_lo = total_lo + mxu_bt(one_hot_b, low)
-            at = tile * NBLK + block
-            entry_ref[at, 0:1, :] = owner
-            entry_ref[at, 1:2, :] = rank
-    req_ref[...] = (total_hi * 256.0 + total_lo).astype(jnp.int32) - 1
+            entry_ref[0:1, tile * SLOTS + block * BLOCK : tile * SLOTS + (block + 1) * BLOCK] = owner
+            entry_ref[1:2, tile * SLOTS + block * BLOCK : tile * SLOTS + (block + 1) * BLOCK] = rank
+    code = (total_hi * 256.0 + total_lo).astype(jnp.int32) - 1
+    req_ref[:, 0:64] = code[:, 0:64]
+    req_ref[:, 64:128] = code[:, 0:64] & (HALF - 1)
 
 
 def route(tile_view, block_counts, entry_owner, entry_local):
+    hbm = pl.BlockSpec(memory_space=pltpu.HBM)
+    vmem = pl.BlockSpec(memory_space=pltpu.VMEM)
     return pl.pallas_call(
         route_kernel,
         name="route",
         out_shape=(
             jax.ShapeDtypeStruct((DEVS, DEVS), jnp.int32),
-            jax.ShapeDtypeStruct((TILES * NBLK, 8, BLOCK), jnp.int32),
+            jax.ShapeDtypeStruct((8, TILES * SLOTS), jnp.int32),
         ),
-        in_specs=[
-            pl.BlockSpec(memory_space=pltpu.SMEM),
-            pl.BlockSpec(memory_space=pltpu.SMEM),
-            pl.BlockSpec(memory_space=pltpu.VMEM),
-            pl.BlockSpec(memory_space=pltpu.VMEM),
+        in_specs=[hbm, hbm, hbm, hbm],
+        out_specs=(vmem, vmem),
+        scratch_shapes=[
+            pltpu.SMEM((TILES,), jnp.int32),
+            pltpu.SMEM((TILES,), jnp.int32),
+            pltpu.VMEM((TILES, SLOTS), jnp.int32),
+            pltpu.VMEM((TILES, SLOTS), jnp.int32),
+            pltpu.SemaphoreType.DMA((4,)),
         ],
-        out_specs=(pl.BlockSpec(memory_space=pltpu.VMEM), pl.BlockSpec(memory_space=pltpu.VMEM)),
-        compiler_params=pltpu.CompilerParams(vmem_limit_bytes=24 << 20),
+        compiler_params=pltpu.CompilerParams(vmem_limit_bytes=16 << 20),
     )(tile_view, block_counts, entry_owner, entry_local)
 
 
@@ -305,7 +336,7 @@
         scratch_shapes=[pltpu.VMEM((COLS // 256, 128, 128), F32)],
         compiler_params=pltpu.CompilerParams(vmem_limit_bytes=24 << 20),
         cost_estimate=pl.CostEstimate(flops=1 << 20, bytes_accessed=9 << 20, transcendentals=0),
-    )(params)
+    )(pltpu.with_memory_space_constraint(params, pltpu.HBM))
 
 
 def cameras_of(camera_ref, view):
@@ -331,7 +362,7 @@
 
     def gather(rank, carry):
         for src in range(DEVS):
-            row = code_ref[src, rank] & (HALF - 1)
+            row = code_ref[src, rank + 64]
             got_ref[src : src + 1, :] = table_ref[pl.ds(row, 1), :]
         both = got_ref[...].T
         half = (code_t_ref[pl.ds(rank, 1), :] >> 13) & 1
@@ -385,7 +416,6 @@
 def render_kernel(
     view_ref,
     spot_ref,
-    count_ref,
     gain_ref,
     d_image_ref,
     entry_ref,
@@ -396,21 +426,22 @@
     low_ref,
     basis_t_ref,
     basis_ref,
-    vals_ref,
     alpha_ref,
     q_ref,
-    color_grad_ref,
     shade_ref,
+    sum_ref,
 ):
     for part in range(WIDE // 128):
         span = slice(part * 128, (part + 1) * 128)
         flipped = arrived_ref[:, span].T
         for piece, value in enumerate(split_three(flipped)):
-            split_ref[piece, span, :] = value.astype(BF16)
-    tri_ref[...] = upper_strict()
-    low_ref[...] = (
-        (iota((BLOCK, BLOCK), 0) > iota((BLOCK, BLOCK), 1)).astype(F32).astype(BF16)
-    )
+            split_ref[span, piece * 128 : (piece + 1) * 128] = value.astype(BF16)
+    upper = upper_strict()
+    lower = (iota((BLOCK, BLOCK), 0) > iota((BLOCK, BLOCK), 1)).astype(F32).astype(BF16)
+    tri_ref[0:BLOCK, :] = upper
+    tri_ref[BLOCK : 2 * BLOCK, :] = upper
+    low_ref[0:BLOCK, :] = lower
+    low_ref[BLOCK : 2 * BLOCK, :] = lower
 
     def monomial(which, x, y):
         return jnp.where(
@@ -439,18 +470,18 @@
         0.0,
     ).astype(BF16)
     pixel = iota((16, TPIX), 1)
-    basis_ref[...] = monomial(
+    basis = monomial(
         iota((16, TPIX), 0), (pixel & 15).astype(F32) - 7.5, (pixel >> 4).astype(F32) - 7.5
     ).astype(BF16)
-    back_ref[...] = jnp.zeros_like(back_ref)
-    owners_at = iota((DEVS, BLOCK), 0)
-    ranks_at = iota((CAP, BLOCK), 0)
-    row8 = iota((8, BLOCK), 0)
+    basis_ref[:, 0:TPIX] = basis
+    basis_ref[:, TPIX : 2 * TPIX] = basis
+    sum_ref[...] = jnp.zeros_like(sum_ref)
 
     def rows8(rows):
-        out = jnp.zeros((8, BLOCK), F32)
+        at_row = iota((8, rows[0].shape[1]), 0)
+        out = jnp.zeros((8, rows[0].shape[1]), F32)
         for at, row in enumerate(rows):
-            out = jnp.where(row8 == at, row, out)
+            out = jnp.where(at_row == at, row, out)
         return out
 
     def tile_step(tile, expo):
@@ -461,175 +492,187 @@
         mid_y = (line * TILE + TILE // 2).astype(F32)
         gains = [gain_ref[view, ch] for ch in range(3)]
         d_rows = [d_image_ref[tile, ch : ch + 1, :] for ch in range(3)]
-        d_raw = rows8(d_rows)
-        d1, d2, d3 = split_three(d_raw)
+        d1, d2, d3 = split_three(rows8(d_rows))
         pixel_rows = jnp.concatenate([d1, d2, d3, jnp.zeros((8, TPIX), F32)], axis=0).astype(BF16)
+        pixel_rows = jnp.concatenate([pixel_rows, pixel_rows], axis=1)
         g1, g2, g3 = split_three(rows8([gains[ch] * d_rows[ch] for ch in range(3)]))
         shade_ref[...] = (
             jnp.concatenate([g1, g1, g2, g2, g1, g3, jnp.zeros((80, TPIX), F32)], axis=0)
             .T.astype(BF16)
         )
-        blocks = count_ref[tile]
-
-        def forward(block, carried):
-            level, expo_rows = carried
-            at = tile * NBLK + block
-            owner = entry_ref[at, 0:1, :]
-            rank = entry_ref[at, 1:2, :]
-            one_hot = (owners_at == owner).astype(F32).astype(BF16)
-            found = (
-                mxu(split_ref[0, 0:USED, :], one_hot)
-                + mxu(split_ref[1, 0:USED, :], one_hot)
-                + mxu(split_ref[2, 0:USED, :], one_hot)
-            )
-            here = ranks_at == rank
-            vals = [
-                jnp.sum(
-                    jnp.where(here, found[k * CAP : (k + 1) * CAP], 0.0), axis=0, keepdims=True
-                )
-                for k in range(VALS)
+        slots = pl.ds(pl.multiple_of(tile * SLOTS, SLOTS), SLOTS)
+        owner = entry_ref[0:1, slots]
+        rank = entry_ref[1:2, slots]
+        one_hot = (iota((DEVS, SLOTS), 0) == owner).astype(F32).astype(BF16)
+        found = mxu(
+            split_ref[0:USED, :], jnp.concatenate([one_hot, one_hot, one_hot], axis=0)
+        )
+        here = iota((CAP, SLOTS), 0) == rank
+        vals = [
+            jnp.sum(jnp.where(here, found[k * CAP : (k + 1) * CAP], 0.0), axis=0, keepdims=True)
+            for k in range(VALS)
+        ]
+        shift_x = vals[0] - mid_x
+        shift_y = vals[1] - mid_y
+        con_a, con_b, con_c = vals[2], vals[3], vals[4]
+        lin_x = con_a * shift_x + con_b * shift_y
+        lin_y = con_c * shift_y + con_b * shift_x
+        level_row = vals[5] - 0.5 * (lin_x * shift_x + lin_y * shift_y)
+        poly = rows8(
+            [
+                jnp.where(owner >= 0, level_row, -200.0),
+                lin_x,
+                lin_y,
+                -0.5 * con_a,
+                -con_b,
+                -0.5 * con_c,
             ]
-            shift_x = vals[0] - mid_x
-            shift_y = vals[1] - mid_y
-            con_a, con_b, con_c = vals[2], vals[3], vals[4]
-            lin_x = con_a * shift_x + con_b * shift_y
-            lin_y = con_c * shift_y + con_b * shift_x
-            poly = rows8(
-                [
-                    vals[5] - 0.5 * (lin_x * shift_x + lin_y * shift_y),
-                    lin_x,
-                    lin_y,
-                    -0.5 * con_a,
-                    -con_b,
-                    -0.5 * con_c,
-                ]
-            )
-            vals_ref[block] = rows8([shift_x, shift_y, con_a, con_b, con_c])
-            k1, k2, k3 = split_three(poly)
-            poly_rows = jnp.concatenate(
-                [k1, k2, k3, jnp.zeros((104, BLOCK), F32)], axis=0
-            ).astype(BF16)
-            color = rows8(vals[6:9])
-            c1, c2, c3 = split_three(color)
-            color_rows = jnp.concatenate(
-                [c1, c2, c1, c2, c3, c1, jnp.zeros((80, BLOCK), F32)], axis=0
-            ).astype(BF16)
-            alpha = jnp.exp(mxu(basis_t_ref[...], poly_rows))
+        )
+        poly = jnp.where(owner >= 0, poly, jnp.where(iota((8, SLOTS), 0) == 0, -200.0, 0.0))
+        k1, k2, k3 = split_three(poly)
+        poly_rows = jnp.concatenate([k1, k2, k3, jnp.zeros((104, SLOTS), F32)], axis=0).astype(
+            BF16
+        )
+        color = rows8(vals[6:9])
+        c1, c2, c3 = split_three(color)
+        color_rows = jnp.concatenate(
+            [c1, c2, c1, c2, c3, c1, jnp.zeros((80, SLOTS), F32)], axis=0
+        ).astype(BF16)
+        level = jnp.zeros((TPIX, 1), F32)
+        seen_parts = []
+        for block in range(NBLK):
+            span = slice(block * BLOCK, (block + 1) * BLOCK)
+            alpha = jnp.exp(mxu(basis_t_ref[...], poly_rows[:, span]))
             fade = alpha * (1.0 + alpha * (0.5 + alpha * (1.0 / 3.0)))
             fade_hi, fade_lo = split_two(fade)
-            summed = mxu(fade_hi, tri_ref[...]) + mxu(fade_lo, tri_ref[...]) + level
+            summed = mxu(jnp.concatenate([fade_hi, fade_lo], axis=1), tri_ref[...]) + level
             weight = alpha * jnp.exp(-summed)
             level = summed[:, BLOCK - 1 : BLOCK] + fade[:, BLOCK - 1 : BLOCK]
-            q_val = mxu(shade_ref[...], color_rows) * weight
             alpha_ref[block] = alpha
-            q_ref[block] = q_val
+            q_ref[block] = mxu(shade_ref[...], color_rows[:, span]) * weight
             weight_hi, weight_lo = split_two(weight)
-            seen = mxu(pixel_rows, weight_hi) + mxu(pixel_rows, weight_lo)
-            seen = seen[0:8] + seen[8:16] + seen[16:24]
-            color_grad_ref[block] = seen
-            return level, expo_rows + color * seen
-
-        level0 = jnp.zeros((TPIX, 1), F32)
-        unused, expo_rows = lax.fori_loop(
-            0, blocks, forward, (level0, jnp.zeros((8, BLOCK), F32))
-        )
-        expo_cols = jnp.sum(expo_rows, axis=1, keepdims=True)
-
-        def backward(step, tail):
-            block = blocks - 1 - step
-            at = tile * NBLK + block
-            owner = entry_ref[at, 0:1, :]
-            rank = entry_ref[at, 1:2, :]
+            seen = mxu(pixel_rows, jnp.concatenate([weight_hi, weight_lo], axis=0))
+            seen_parts.append(seen[0:8] + seen[8:16] + seen[16:24])
+        seen = jnp.concatenate(seen_parts, axis=1)
+        expo_cols = jnp.sum(color * seen, axis=1, keepdims=True)
+        tail = jnp.zeros((TPIX, 1), F32)
+        grad_parts = [None] * NBLK
+        for block in reversed(range(NBLK)):
             alpha = alpha_ref[block]
             q_val = q_ref[block]
             q_hi, q_lo = split_two(q_val)
-            later = mxu(q_hi, low_ref[...]) + mxu(q_lo, low_ref[...]) + tail
+            later = mxu(jnp.concatenate([q_hi, q_lo], axis=1), low_ref[...]) + tail
             d_exp = q_val - later * (alpha * (1.0 + alpha * (1.0 + alpha)))
             tail = later[:, 0:1] + q_val[:, 0:1]
             d_hi, d_lo = split_two(d_exp)
-            grad = mxu(basis_ref[...], d_hi) + mxu(basis_ref[...], d_lo)
-            d_poly = [grad[k : k + 1] for k in range(6)]
-            held = vals_ref[block]
-            shift_x, shift_y, con_a, con_b, con_c = [held[k : k + 1] for k in range(5)]
-            lin_x = con_a * shift_x + con_b * shift_y
-            lin_y = con_c * shift_y + con_b * shift_x
-            seen = color_grad_ref[block]
-            grads = [
-                d_poly[1] * con_a + d_poly[2] * con_b - d_poly[0] * lin_x,
-                d_poly[1] * con_b + d_poly[2] * con_c - d_poly[0] * lin_y,
-                shift_x * d_poly[1] - 0.5 * (d_poly[3] + shift_x * shift_x * d_poly[0]),
-                shift_y * d_poly[1]
-                + shift_x * d_poly[2]
-                - d_poly[4]
-                - shift_x * shift_y * d_poly[0],
-                shift_y * d_poly[2] - 0.5 * (d_poly[5] + shift_y * shift_y * d_poly[0]),
-                d_poly[0],
-                gains[0] * seen[0:1],
-                gains[1] * seen[1:2],
-                gains[2] * seen[2:3],
-            ]
-            one_hot = (owners_at == owner).astype(F32).astype(BF16)
-            here = ranks_at == rank
-            high_rows = []
-            low_rows = []
-            for value in grads:
-                high = value.astype(BF16).astype(F32)
-                high_rows.append(jnp.where(here, high, 0.0).astype(BF16))
-                low_rows.append(jnp.where(here, value - high, 0.0).astype(BF16))
-            back_ref[:, 0:USED] += mxu_bt(one_hot, jnp.concatenate(high_rows, axis=0)) + mxu_bt(
-                one_hot, jnp.concatenate(low_rows, axis=0)
-            )
-            return tail
-
-        lax.fori_loop(0, blocks, backward, jnp.zeros((TPIX, 1), F32))
+            grad_parts[block] = mxu(basis_ref[...], jnp.concatenate([d_hi, d_lo], axis=0))[0:8]
+        grad = jnp.concatenate(grad_parts, axis=1)
+        d_poly = [grad[k : k + 1] for k in range(6)]
+        grads = [
+            d_poly[1] * con_a + d_poly[2] * con_b - d_poly[0] * lin_x,
+            d_poly[1] * con_b + d_poly[2] * con_c - d_poly[0] * lin_y,
+            shift_x * d_poly[1] - 0.5 * (d_poly[3] + shift_x * shift_x * d_poly[0]),
+            shift_y * d_poly[1] + shift_x * d_poly[2] - d_poly[4] - shift_x * shift_y * d_poly[0],
+            shift_y * d_poly[2] - 0.5 * (d_poly[5] + shift_y * shift_y * d_poly[0]),
+            d_poly[0],
+            gains[0] * seen[0:1],
+            gains[1] * seen[1:2],
+            gains[2] * seen[2:3],
+        ]
+        high_rows = []
+        low_rows = []
+        for value in grads:
+            high = value.astype(BF16).astype(F32)
+            high_rows.append(jnp.where(here, high, 0.0).astype(BF16))
+            low_rows.append(jnp.where(here, value - high, 0.0).astype(BF16))
+        both = mxu_bt(jnp.concatenate(high_rows + low_rows, axis=0), one_hot)
+        sum_ref[0:USED, :] += both[0:USED] + both[USED : 2 * USED]
         lane_at = iota((8, 128), 1) - (USED - 384) - 3 * view
-        return expo + jnp.where(lane_at == iota((8, 128), 0), expo_cols, 0.0)
+        return expo + jnp.where(
+            (lane_at == iota((8, 128), 0)) & (lane_at < 3), expo_cols, 0.0
+        )
 
     expo = lax.fori_loop(0, TILES, tile_step, jnp.zeros((8, 128), F32))
-    lane = iota((8, 128), 1)
-    expo = jnp.where((lane >= USED - 384) & (lane < USED - 384 + 12), expo, 0.0)
-    back_ref[:, 384:WIDE] += jnp.sum(expo, axis=0, keepdims=True)
-
-
-def render_of(tile_view, tile_spot, block_counts, exposure, d_image, entries, arrived):
+    for part in range(WIDE // 128):
+        span = slice(part * 128, (part + 1) * 128)
+        back = sum_ref[span, :].T
+        if part == WIDE // 128 - 1:
+            back = back + jnp.sum(expo, axis=0, keepdims=True)
+        back_ref[:, span] = back
+
+
+def render_of(tile_view, tile_spot, exposure, d_image, entries, arrived):
     smem = pl.BlockSpec(memory_space=pltpu.SMEM)
     vmem = pl.BlockSpec(memory_space=pltpu.VMEM)
     return pl.pallas_call(
         render_kernel,
         name="render",
         out_shape=jax.ShapeDtypeStruct((DEVS, WIDE), F32),
-        in_specs=[smem, smem, smem, smem, vmem, vmem, vmem],
+        in_specs=[smem, smem, smem, vmem, vmem, vmem],
         out_specs=vmem,
         scratch_shapes=[
-            pltpu.VMEM((3, WIDE, DEVS), BF16),
-            pltpu.VMEM((BLOCK, BLOCK), BF16),
-            pltpu.VMEM((BLOCK, BLOCK), BF16),
+            pltpu.VMEM((WIDE, 3 * DEVS), BF16),
+            pltpu.VMEM((2 * BLOCK, BLOCK), BF16),
+            pltpu.VMEM((2 * BLOCK, BLOCK), BF16),
             pltpu.VMEM((TPIX, 128), BF16),
-            pltpu.VMEM((16, TPIX), BF16),
-            pltpu.VMEM((NBLK, 8, BLOCK), F32),
+            pltpu.VMEM((16, 2 * TPIX), BF16),
             pltpu.VMEM((NBLK, TPIX, BLOCK), F32),
             pltpu.VMEM((NBLK, TPIX, BLOCK), F32),
-            pltpu.VMEM((NBLK, 8, BLOCK), F32),
             pltpu.VMEM((TPIX, 128), BF16),
+            pltpu.VMEM((WIDE, DEVS), F32),
         ],
         compiler_params=pltpu.CompilerParams(vmem_limit_bytes=32 << 20),
-    )(tile_view, tile_spot, block_counts, exposure, d_image, entries, arrived)
-
-
-def collect_kernel(
+    )(tile_view, tile_spot, exposure, d_image, entries, arrived)
+
+
+PARTS = 8
+SPAN = GDEV // PARTS
+
+
+def update_kernel(
     code_ref,
     camera_ref,
     code_vec_ref,
     arrived_ref,
     rows_ref,
-    total_ref,
+    params_hbm,
+    m_hbm,
+    v_hbm,
+    params_out,
+    m_out,
+    v_out,
     expo_ref,
     code_t_ref,
     cot_ref,
     grad_ref,
     spread_ref,
+    flip_ref,
+    params_ref,
+    m_ref,
+    v_ref,
+    in_sems,
+    out_sems,
     *tables,
 ):
+    held = ((params_hbm, params_ref, params_out), (m_hbm, m_ref, m_out), (v_hbm, v_ref, v_out))
+
+    def fetch(part):
+        span = pl.ds(part * SPAN, SPAN)
+        return [
+            pltpu.make_async_copy(source.at[:, span], kept.at[:, span], in_sems.at[at, part])
+            for at, (source, kept, unused) in enumerate(held)
+        ]
+
+    def give(part):
+        span = pl.ds(part * SPAN, SPAN)
+        return [
+            pltpu.make_async_copy(kept.at[:, span], target.at[:, span], out_sems.at[at, part])
+            for at, (unused, kept, target) in enumerate(held)
+        ]
+
+    for part in range(PARTS):
+        for copy in fetch(part):
+            copy.start()
     code_t_ref[...] = code_vec_ref[...].T
     expo_ref[...] = jnp.broadcast_to(
         jnp.sum(arrived_ref[:, 384:WIDE], axis=0, keepdims=True), (8, 128)
@@ -646,7 +689,7 @@
         values = [rows_ref[pl.ds(k * CAP + base, 8), :] for k in range(PARAMS)]
         code = code_t_ref[pl.ds(base, 8), :]
         camera = cameras_of(camera_ref, (code >> 14) & 3)
-        unused, pull = jax.vjp(lambda held: project(held, camera), values)
+        unused, pull = jax.vjp(lambda given: project(given, camera), values)
         (grads,) = pull([cot_ref[pl.ds(k * CAP + base, 8), :] for k in range(VALS)])
         for k in range(PARAMS):
             grad_ref[pl.ds(k * CAP + base, 8), :] = jnp.where(code >= 0, grads[k], 0.0)
@@ -657,10 +700,7 @@
     def scatter(rank, carry):
         half = (code_t_ref[pl.ds(rank, 1), :] >> 13) & 1
         mine = jnp.concatenate(
-            [
-                grad_ref[pl.ds(group * 8 * CAP + rank, 8, stride=CAP), :]
-                for group in range(8)
-            ],
+            [grad_ref[pl.ds(group * 8 * CAP + rank, 8, stride=CAP), :] for group in range(8)],
             axis=0,
         )
         both = jnp.concatenate(
@@ -668,74 +708,66 @@
         )
         spread_ref[...] = both.T
         for src in range(DEVS):
-            row = code_ref[src, rank] & (HALF - 1)
+            row = code_ref[src, rank + 64]
             table = tables[src % TABLES]
             table[pl.ds(row, 1), :] = table[pl.ds(row, 1), :] + spread_ref[src : src + 1, :]
         return carry
 
     lax.fori_loop(0, CAP, scatter, 0)
 
-    def merge(at, carry):
-        span = pl.ds(pl.multiple_of(at * 128, 128), 128)
-        total = tables[0][span, :]
-        for table in tables[1:]:
-            total = total + table[span, :]
-        total_ref[span, :] = total
-        return carry
-
-    lax.fori_loop(0, HALF // 128, merge, 0)
-
-
-def collect_of(codes, cameras, arrived, rows):
+    for part in range(PARTS):
+        for copy in fetch(part):
+            copy.wait()
+
+        def step(at, carry):
+            rows = pl.ds(pl.multiple_of(part * (SPAN // 2) + at * 128, 128), 128)
+            total = tables[0][rows, :]
+            for table in tables[1:]:
+                total = total + table[rows, :]
+            flip_ref[...] = total.T
+            for half in range(2):
+                span = pl.ds(pl.multiple_of(part * SPAN + at * 256 + half * 128, 128), 128)
+                gradient = flip_ref[half * 64 : half * 64 + PARAMS, :]
+                new_m = beta_first * m_ref[:, span] + (1.0 - beta_first) * gradient
+                new_v = beta_second * v_ref[:, span] + (1.0 - beta_second) * gradient * gradient
+                m_ref[:, span] = new_m
+                v_ref[:, span] = new_v
+                params_ref[:, span] = params_ref[:, span] - learn_rate * (new_m / fix_first) / (
+                    jnp.sqrt(new_v / fix_second) + adam_eps
+                )
+            return carry
+
+        lax.fori_loop(0, SPAN // 256, step, 0)
+        for copy in give(part):
+            copy.start()
+    for part in range(PARTS):
+        for copy in give(part):
+            copy.wait()
+
+
+def update_of(codes, cameras, arrived, rows, params, adam_m, adam_v):
     smem = pl.BlockSpec(memory_space=pltpu.SMEM)
     vmem = pl.BlockSpec(memory_space=pltpu.VMEM)
+    hbm = pl.BlockSpec(memory_space=pltpu.HBM)
+    whole = jax.ShapeDtypeStruct((PARAMS, GDEV), F32)
     return pl.pallas_call(
-        collect_kernel,
-        name="collect",
-        out_shape=(
-            jax.ShapeDtypeStruct((HALF, 128), F32),
-            jax.ShapeDtypeStruct((8, 128), F32),
-        ),
-        in_specs=[smem, smem, vmem, vmem, vmem],
-        out_specs=(vmem, vmem),
+        update_kernel,
+        name="update",
+        out_shape=(whole, whole, whole, jax.ShapeDtypeStruct((8, 128), F32)),
+        in_specs=[smem, smem, vmem, vmem, vmem, hbm, hbm, hbm],
+        out_specs=(hbm, hbm, hbm, vmem),
         scratch_shapes=[
             pltpu.VMEM((DEVS, DEVS), jnp.int32),
             pltpu.VMEM((WIDE, DEVS), F32),
             pltpu.VMEM((64 * CAP, DEVS), F32),
             pltpu.VMEM((DEVS, 128), F32),
+            pltpu.VMEM((128, 128), F32),
         ]
+        + [pltpu.VMEM((PARAMS, GDEV), F32)] * 3
+        + [pltpu.SemaphoreType.DMA((3, PARTS))] * 2
         + [pltpu.VMEM((HALF, 128), F32)] * TABLES,
         compiler_params=pltpu.CompilerParams(vmem_limit_bytes=48 << 20),
-    )(codes, cameras, codes, arrived, rows)
-
-
-def adam_kernel(total_ref, params_ref, m_ref, v_ref, params_out, m_out, v_out, flip_ref):
-    for at in range(COLS // 256):
-        flip_ref[at] = total_ref[at * 128 : (at + 1) * 128, :].T
-        for half in range(2):
-            span = slice(at * 256 + half * 128, at * 256 + (half + 1) * 128)
-            gradient = flip_ref[at, half * 64 : half * 64 + PARAMS, :]
-            new_m = beta_first * m_ref[:, span] + (1.0 - beta_first) * gradient
-            new_v = beta_second * v_ref[:, span] + (1.0 - beta_second) * gradient * gradient
-            m_out[:, span] = new_m
-            v_out[:, span] = new_v
-            params_out[:, span] = params_ref[:, span] - learn_rate * (new_m / fix_first) / (
-                jnp.sqrt(new_v / fix_second) + adam_eps
-            )
-
-
-def adam_of(total, params, adam_m, adam_v):
-    wide = pl.BlockSpec((PARAMS, COLS), lambda i: (0, i))
-    return pl.pallas_call(
-        adam_kernel,
-        name="adam",
-        grid=(GDEV // COLS,),
-        out_shape=(jax.ShapeDtypeStruct((PARAMS, GDEV), F32),) * 3,
-        in_specs=[pl.BlockSpec((COLS // 2, 128), lambda i: (i, 0)), wide, wide, wide],
-        out_specs=(wide, wide, wide),
-        scratch_shapes=[pltpu.VMEM((COLS // 256, 128, 128), F32)],
-        compiler_params=pltpu.CompilerParams(vmem_limit_bytes=32 << 20),
-    )(total, params, adam_m, adam_v)
+    )(codes, cameras, codes, arrived, rows, params, adam_m, adam_v)
 
 
 def exchange(value):
@@ -760,10 +792,11 @@
     table = table_of(params)
     reply, rows = reply_of(codes, cameras, table)
     arrived = exchange(reply)
-    back = render_of(tile_view, tile_spot, block_counts, exposure, d_image, entries, arrived)
+    back = render_of(tile_view, tile_spot, exposure, d_image, entries, arrived)
     returned = exchange(back)
-    total, expo = collect_of(codes, cameras, returned, rows)
-    new_params, new_m, new_v = adam_of(total, params, adam_m, adam_v)
+    new_params, new_m, new_v, expo = update_of(
+        codes, cameras, returned, rows, params, adam_m, adam_v
+    )
     first = USED - 384
     exposure_grad = expo[0, first : first + 12].reshape(4, 3) / DEVS
     return (new_params, new_m, new_v, exposure_grad)

time: 147 us -> 130 us (0.88)
  local copies, waits for them, and re-layouts: 21.8 us -> 11.1 us
  blocking collectives: 20.2 us -> 15.3 us
  Pallas kernels: 71.8 us -> 69.6 us
    unnamed x39 -> x27, local copies, waits for them, and re-layouts: 19.9 us -> 9.18 us
    pallas_call x1, Pallas kernels: 24.5 us -> 17.7 us  [render_of(): pl.pallas_call(render_kernel, name='render', out_shape=jax.ShapeDtypeStru...]
    all_to_all x1, blocking collectives: 20.2 us -> 15.3 us  [exchange(): return lax.all_to_all(value, AXES, split_axis=0, concat_axis=0, tiled=True)]
    pallas_call x1, Pallas kernels: 1.97 us -> 5.33 us  [table_of(): pl.pallas_call(table_kernel, name='table', grid=(GDEV // COLS,), out_shap...]
    pallas_call x2 -> x1, Pallas kernels: 25.7 us -> 28.1 us  [update_of(): pl.pallas_call(update_kernel, name='update', out_shape=(whole, whole, who...]
  transfers between devices with their start and end apart: 2 -> 2, of which waited for: 2 -> 2; matrix products, arithmetic and copies ran while one was open for 0% -> 0% of each run, Pallas kernels for 1% -> 4%
where the time goes in v2:
time: 130 us; the launch traced here: 129 us
  Pallas kernels  69.6 us (54%)
  starting transfers between devices  19.4 us (15%)
  blocking collectives  15.3 us (12%)
  waiting for transfers between devices  12.8 us (10%)
  local copies, waits for them, and re-layouts  11.1 us (9%)
    pallas_call x1, Pallas kernels, update_of(): pl.pallas_call(update_kernel, name='update', out_shape=(whole, whole, who...  28.1 us
    all_to_all x2, starting transfers between devices, exchange(): return lax.all_to_all(value, AXES, split_axis=0, concat_axis=0, tiled=True)  19.4 us
    pallas_call x1, Pallas kernels, render_of(): pl.pallas_call(render_kernel, name='render', out_shape=jax.ShapeDtypeStru...  17.7 us
    all_to_all x1, blocking collectives, exchange(): return lax.all_to_all(value, AXES, split_axis=0, concat_axis=0, tiled=True)  15.3 us
    pallas_call x1, Pallas kernels, reply_of(): pl.pallas_call(reply_kernel, name='reply', out_shape=(jax.ShapeDtypeStruc...  13.1 us
    all_to_all x2, waiting for transfers between devices, exchange(): return lax.all_to_all(value, AXES, split_axis=0, concat_axis=0, tiled=True)  12.8 us
    unnamed x27, local copies, waits for them, and re-layouts  9.18 us
    pallas_call x1, Pallas kernels, route(): pl.pallas_call(route_kernel, name='route', out_shape=(jax.ShapeDtypeStruc...  5.36 us
  transfers between devices with their start and end apart: 2, of which 2 were waited for; matrix products, arithmetic and copies ran while one was open for 0% of the time, Pallas kernels for 4%

profile of v2, /device:TPU:1, one launch (start us, length us, event | category | flops | bytes accessed | tf_op | source)
XLA Modules:
  0.0 129.0 jit_solution(17452639581624022389)
XLA Ops:
  0.6 0.0 copy-start.3
  0.6 0.7 copy-done.3
  1.4 0.0 copy-start.4
  1.4 0.7 copy-done.4
  2.1 0.0 copy-start.7
  2.1 0.7 copy-done.7
  2.7 0.0 copy-start.9
  2.7 0.7 copy-done.9
  3.4 5.4 %route.1 = (s32[128,128]{1,0:T(8,128)}, s32[8,4096]{1,0:T(8,128)S(1)}) custom-call(s32[4]{0:T(128)S(1)} %copy-done.7, s32[4]{0:T(128)S(1)} %copy-done.9, s32[4,1024]{1,0:T(4,128)S(1)} %copy-done.3, s32[4,1024]{1,0:T(4,128)S(1)} %copy-done.4), custom_call_target="tpu_custom_call" | custom-call | tf_op jit(solution)/shard_map/route/pallas_call | solution.py:294
  8.7 11.5 %all-to-all-start = ((s32[128,1,128]{2,1,0:T(1,128)}), s32[128,1,128]{2,1,0:T(1,128)S(1)}, u32[]{:S(2)}, u32[]{:S(2)}) async-start(s32[128,1,128]{2,1,0:T(1,128)} %bitcast.1), calls=%async_computation | async-start | bytes 131072 | tf_op jit(solution)/shard_map/all_to_all | solution.py:774
  20.3 0.0 copy-start.5
  20.3 0.0 copy-start.11
  20.3 0.0 copy-start.6
  20.3 5.3 %table.1.table_ref = f32[8192,128]{1,0:T(8,128)S(1)} custom-call(f32[59,16384]{1,0:T(8,128)} %params_hbm.1), custom_call_target="tpu_custom_call" | custom-call | flops 1048576 | bytes 9437184 | tf_op jit(solution)/shard_map/table/pallas_call | solution.py:329
  25.6 0.0 copy-start
  25.6 2.0 %copy-done = f32[8192,128]{1,0:T(8,128)} copy-done((f32[8192,128]{1,0:T(8,128)}, f32[8192,128]{1,0:T(8,128)S(1)}, u32[]{:S(2)}) %copy-start) | copy-done | bytes 4194328
  27.6 0.0 copy-start.8
  27.6 0.0 copy-start.10
  27.7 1.9 %all-to-all-done = s32[128,1,128]{2,1,0:T(1,128)S(1)} async-done(((s32[128,1,128]{2,1,0:T(1,128)}), s32[128,1,128]{2,1,0:T(1,128)S(1)}, u32[]{:S(2)}, u32[]{:S(2)}) %all-to-all-start) | async-done | bytes 65568 | tf_op jit(solution)/shard_map/all_to_all | solution.py:774
  29.6 0.0 copy-done.5
  29.6 0.0 copy-start.1
  29.6 2.2 %copy-done.1 = f32[8192,128]{1,0:T(8,128)S(1)} copy-done((f32[8192,128]{1,0:T(8,128)S(1)}, f32[8192,128]{1,0:T(8,128)}, u32[]{:S(2)}) %copy-start.1) | copy-done | bytes 4194328
  31.8 13.1 %reply.1 = (f32[128,512]{1,0:T(8,128)S(1)}, f32[3072,128]{1,0:T(8,128)S(1)}) custom-call(s32[128,128]{1,0:T(8,128)S(1)} %bitcast.12, f32[4,13]{1,0:T(4,128)S(1)} %copy-done.5, s32[128,128]{1,0:T(8,128)S(1)} %bitcast.13, f32[8192,128]{1,0:T(8,128)S(1)} %copy-done.1), custom_call_target="tpu_custom_call" | custom-call | tf_op jit(solution)/shard_map/reply/pallas_call | solution.py:393
  44.9 1.0 copy.17
  45.9 7.8 %all-to-all-start.1 = ((f32[128,1,512]{2,1,0:T(1,128)}), f32[128,1,512]{2,1,0:T(1,128)S(1)}, u32[]{:S(2)}, u32[]{:S(2)}) async-start(f32[128,1,512]{2,1,0:T(1,128)} %copy.17), calls=%async_computation.1 | async-start | bytes 524288 | tf_op jit(solution)/shard_map/all_to_all | solution.py:774
  53.7 0.0 copy-done.11
  53.8 10.9 %all-to-all-done.1 = f32[128,1,512]{2,1,0:T(1,128)S(1)} async-done(((f32[128,1,512]{2,1,0:T(1,128)}), f32[128,1,512]{2,1,0:T(1,128)S(1)}, u32[]{:S(2)}, u32[]{:S(2)}) %all-to-all-start.1) | async-done | bytes 262176 | tf_op jit(solution)/shard_map/all_to_all | solution.py:774
  64.6 0.0 copy-done.6
  64.7 0.0 copy-done.8
  64.7 0.0 copy-done.10
  64.7 17.7 %render.1 = f32[128,512]{1,0:T(8,128)S(1)} custom-call(s32[4]{0:T(128)S(1)} %copy-done.8, s32[4]{0:T(128)S(1)} %copy-done.10, f32[4,3]{1,0:T(4,128)S(1)} %copy-done.6, f32[4,3,256]{2,1,0:T(4,128)S(1)} %copy.18.d_image_ref, s32[8,4096]{1,0:T(8,128)S(1)} %get-tuple-element.13.entry_ref, f32[128,512]{1,0:T(8,128)S(1)} %bitcast.17), custom_call_target="tpu_custom_call" | custom-call | tf_op jit(solution)/shard_map/render/pallas_call | solution.py:607
  82.3 0.3 copy.19
  82.6 15.3 %all_to_all.33 = f32[128,1,512]{2,1,0:T(1,128)S(1)} all-to-all(f32[128,1,512]{2,1,0:T(1,128)S(1)} %copy.19), channel_id=1, replica_groups=mesh['tiles'=16,'gauss'=8] {'tiles','gauss'}, dimensions={0} | all-to-all | bytes 524288 | tf_op jit(solution)/shard_map/all_to_all | solution.py:774
  97.9 0.0 copy-start.2
  97.9 2.2 %copy-done.2 = f32[59,16384]{1,0:T(8,128)S(1)} copy-done((f32[59,16384]{1,0:T(8,128)S(1)}, f32[59,16384]{1,0:T(8,128)}, u32[]{:S(2)}) %copy-start.2) | copy-done | bytes 3866648
  100.1 28.1 %update.1 = (f32[59,16384]{1,0:T(8,128)}, f32[59,16384]{1,0:T(8,128)}, f32[59,16384]{1,0:T(8,128)}, f32[8,128]{1,0:T(8,128)S(1)}) custom-call(s32[128,128]{1,0:T(8,128)S(1)} %bitcast.14, f32[4,13]{1,0:T(4,128)S(1)} %copy-done.5, s32[128,128]{1,0:T(8,128)S(1)} %bitcast.15, f32[128,512]{1,0:T(8,128)S(1)} %bitcast.16, ...), custom_call_target="tpu_custom_call" | custom-call | tf_op jit(solution)/shard_map/update/pallas_call | solution.py:753
  128.2 0.1 multiply_reduce_fusion
  128.3 0.7 div.6
  (3 shorter events, 0.0 us)
Async XLA Ops:
  0.6 0.7 copy-start.3
  1.4 0.7 copy-start.4
  2.1 0.7 copy-start.7
  2.7 0.7 copy-start.9
  8.7 20.8 %all-to-all-start = ((s32[128,1,128]{2,1,0:T(1,128)}), s32[128,1,128]{2,1,0:T(1,128)S(1)}, u32[]{:S(2)}, u32[]{:S(2)}) async-start(s32[128,1,128]{2,1,0:T(1,128)} %bitcast.1), calls=%async_computation | async-start | bytes 131072 | tf_op jit(solution)/shard_map/all_to_all | solution.py:774
  20.3 9.3 %copy-start.5 = (f32[4,13]{1,0:T(4,128)S(1)}, f32[4,13]{1,0:T(4,128)}, u32[]{:S(2)}) copy-start(f32[4,13]{1,0:T(4,128)} %camera_ref.3) | copy-start | bytes 628
  20.3 33.5 %copy-start.11 = (f32[4,3,256]{2,0,1:T(4,128)S(1)}, f32[4,3,256]{2,0,1:T(4,128)}, u32[]{:S(2)}) copy-start(f32[4,3,256]{2,0,1:T(4,128)} %param.21) | copy-start | bytes 36868
  20.3 44.4 %copy-start.6 = (f32[4,3]{1,0:T(4,128)S(1)}, f32[4,3]{1,0:T(4,128)}, u32[]{:S(2)}) copy-start(f32[4,3]{1,0:T(4,128)} %gain_ref.1) | copy-start | bytes 148
  25.6 2.0 %copy-start = (f32[8192,128]{1,0:T(8,128)}, f32[8192,128]{1,0:T(8,128)S(1)}, u32[]{:S(2)}) copy-start(f32[8192,128]{1,0:T(8,128)S(1)} %table.1.table_ref) | copy-start | bytes 12582916
  27.6 37.0 %copy-start.8 = (s32[4]{0:T(128)S(1)}, s32[4]{0:T(128)}, u32[]{:S(2)}) copy-start(s32[4]{0:T(128)} %view_ref.1) | copy-start | bytes 52
  27.6 37.0 %copy-start.10 = (s32[4]{0:T(128)S(1)}, s32[4]{0:T(128)}, u32[]{:S(2)}) copy-start(s32[4]{0:T(128)} %spot_ref.1) | copy-start | bytes 52
  29.6 2.2 %copy-start.1 = (f32[8192,128]{1,0:T(8,128)S(1)}, f32[8192,128]{1,0:T(8,128)}, u32[]{:S(2)}) copy-start(f32[8192,128]{1,0:T(8,128)} %copy-done) | copy-start | bytes 12582916
  45.9 18.7 %all-to-all-start.1 = ((f32[128,1,512]{2,1,0:T(1,128)}), f32[128,1,512]{2,1,0:T(1,128)S(1)}, u32[]{:S(2)}, u32[]{:S(2)}) async-start(f32[128,1,512]{2,1,0:T(1,128)} %copy.17), calls=%async_computation.1 | async-start | bytes 524288 | tf_op jit(solution)/shard_map/all_to_all | solution.py:774
  97.9 2.2 %copy-start.2 = (f32[59,16384]{1,0:T(8,128)S(1)}, f32[59,16384]{1,0:T(8,128)}, u32[]{:S(2)}) copy-start(f32[59,16384]{1,0:T(8,128)} %params_hbm.1) | copy-start | bytes 11599876

commit v3 on v2

--- a/solution.py
+++ b/solution.py
@@ -192,6 +192,10 @@
     ] + colors
 
 
+def in_hbm(value):
+    return pltpu.with_memory_space_constraint(value, pltpu.HBM)
+
+
 def iota(shape, dim):
     return lax.broadcasted_iota(jnp.int32, shape, dim)
 
@@ -233,6 +237,7 @@
     count_ref,
     owner_ref,
     local_ref,
+    flip_ref,
     sems,
 ):
     copies = [
@@ -251,41 +256,36 @@
     tri = upper_strict()
     for copy in copies:
         copy.wait()
-    owners_at = iota((DEVS, BLOCK), 0)
-    ranks_at = iota((DEVS, BLOCK), 0)
     before = jnp.zeros((DEVS, 1), F32)
-    total_hi = jnp.zeros((DEVS, DEVS), F32)
-    total_lo = jnp.zeros((DEVS, DEVS), F32)
+    total = jnp.zeros((2 * CAP, DEVS), F32)
     for tile in range(TILES):
         view = view_ref[tile]
+        slots = slice(tile * SLOTS, (tile + 1) * SLOTS)
+        alive = (iota((1, SLOTS), 1) >> 8) < count_ref[tile]
+        owner = jnp.where(alive, owner_ref[tile : tile + 1, :], -1)
+        local = local_ref[tile : tile + 1, :]
+        one_hot = (iota((DEVS, SLOTS), 0) == owner).astype(F32)
+        one_hot_b = one_hot.astype(BF16)
+        ranks = []
         for block in range(NBLK):
-            alive = block < count_ref[tile]
             span = slice(block * BLOCK, (block + 1) * BLOCK)
-            owner = jnp.where(alive, owner_ref[tile : tile + 1, span], -1)
-            local = local_ref[tile : tile + 1, span]
-            one_hot = (owners_at == owner).astype(F32)
-            one_hot_b = one_hot.astype(BF16)
-            earlier = mxu(one_hot_b, tri) + before
-            rank = jnp.sum(one_hot * earlier, axis=0, keepdims=True)
-            before = before + jnp.sum(one_hot, axis=1, keepdims=True)
-            rank = jnp.where(owner >= 0, rank.astype(jnp.int32), -1)
-            code = (
-                view * GDEV
-                + ((local >> 7) & 1) * HALF
-                + ((local >> 8) << 7)
-                + (local & 127)
-                + 1
-            )
-            at_rank = ranks_at == rank
-            high = jnp.where(at_rank, (code >> 8).astype(F32), 0.0).astype(BF16)
-            low = jnp.where(at_rank, (code & 255).astype(F32), 0.0).astype(BF16)
-            total_hi = total_hi + mxu_bt(one_hot_b, high)
-            total_lo = total_lo + mxu_bt(one_hot_b, low)
-            entry_ref[0:1, tile * SLOTS + block * BLOCK : tile * SLOTS + (block + 1) * BLOCK] = owner
-            entry_ref[1:2, tile * SLOTS + block * BLOCK : tile * SLOTS + (block + 1) * BLOCK] = rank
-    code = (total_hi * 256.0 + total_lo).astype(jnp.int32) - 1
-    req_ref[:, 0:64] = code[:, 0:64]
-    req_ref[:, 64:128] = code[:, 0:64] & (HALF - 1)
+            earlier = mxu(one_hot_b[:, span], tri) + before
+            ranks.append(jnp.sum(one_hot[:, span] * earlier, axis=0, keepdims=True))
+            last = (block + 1) * BLOCK
+            before = earlier[:, BLOCK - 1 : BLOCK] + one_hot[:, last - 1 : last]
+        rank = jnp.where(owner >= 0, jnp.concatenate(ranks, axis=1).astype(jnp.int32), -1)
+        code = (
+            view * GDEV + ((local >> 7) & 1) * HALF + ((local >> 8) << 7) + (local & 127) + 1
+        )
+        here = iota((CAP, SLOTS), 0) == rank
+        high = jnp.where(here, (code >> 8).astype(F32), 0.0).astype(BF16)
+        low = jnp.where(here, (code & 255).astype(F32), 0.0).astype(BF16)
+        total = total + mxu_bt(jnp.concatenate([high, low], axis=0), one_hot_b)
+        entry_ref[0:1, slots] = owner
+        entry_ref[1:2, slots] = rank
+    flip_ref[...] = jnp.zeros_like(flip_ref)
+    flip_ref[0:CAP, :] = total[0:CAP] * 256.0 + total[CAP : 2 * CAP]
+    req_ref[...] = flip_ref[...].T.astype(jnp.int32) - 1
 
 
 def route(tile_view, block_counts, entry_owner, entry_local):
@@ -305,10 +305,11 @@
             pltpu.SMEM((TILES,), jnp.int32),
             pltpu.VMEM((TILES, SLOTS), jnp.int32),
             pltpu.VMEM((TILES, SLOTS), jnp.int32),
+            pltpu.VMEM((DEVS, DEVS), F32),
             pltpu.SemaphoreType.DMA((4,)),
         ],
         compiler_params=pltpu.CompilerParams(vmem_limit_bytes=16 << 20),
-    )(tile_view, block_counts, entry_owner, entry_local)
+    )(*[in_hbm(given) for given in (tile_view, block_counts, entry_owner, entry_local)])
 
 
 COLS = 2048
@@ -330,13 +331,13 @@
         table_kernel,
         name="table",
         grid=(GDEV // COLS,),
-        out_shape=jax.ShapeDtypeStruct((HALF, 128), F32),
+        out_shape=pltpu.HBM((HALF, 128), F32),
         in_specs=[pl.BlockSpec((PARAMS, COLS), lambda i: (0, i))],
         out_specs=pl.BlockSpec((COLS // 2, 128), lambda i: (i, 0)),
         scratch_shapes=[pltpu.VMEM((COLS // 256, 128, 128), F32)],
         compiler_params=pltpu.CompilerParams(vmem_limit_bytes=24 << 20),
         cost_estimate=pl.CostEstimate(flops=1 << 20, bytes_accessed=9 << 20, transcendentals=0),
-    )(pltpu.with_memory_space_constraint(params, pltpu.HBM))
+    )(in_hbm(params))
 
 
 def cameras_of(camera_ref, view):
@@ -354,26 +355,56 @@
     ]
 
 
+PIECES = 8
+
+
 def reply_kernel(
-    code_ref, camera_ref, code_vec_ref, table_ref, reply_ref, rows_ref, code_t_ref, got_ref, proj_ref
+    camera_ref,
+    code_ref,
+    table_hbm,
+    reply_ref,
+    rows_ref,
+    code_t_ref,
+    row_t_ref,
+    row_smem,
+    table_ref,
+    got_ref,
+    proj_ref,
+    table_sems,
+    row_sem,
 ):
-    code_t_ref[...] = code_vec_ref[...].T
+    copies = []
+    for piece in range(PIECES):
+        span = pl.ds(piece * (HALF // PIECES), HALF // PIECES)
+        copies.append(
+            pltpu.make_async_copy(table_hbm.at[span], table_ref.at[span], table_sems.at[piece])
+        )
+    for copy in copies:
+        copy.start()
+    code_t_ref[...] = code_ref[...].T
+    row_t_ref[...] = code_t_ref[0:CAP, :] & (HALF - 1)
+    send_rows = pltpu.make_async_copy(row_t_ref, row_smem, row_sem)
+    send_rows.start()
     proj_ref[USED:WIDE, :] = jnp.zeros((WIDE - USED, DEVS), F32)
-
-    def gather(rank, carry):
-        for src in range(DEVS):
-            row = code_ref[src, rank + 64]
-            got_ref[src : src + 1, :] = table_ref[pl.ds(row, 1), :]
-        both = got_ref[...].T
-        half = (code_t_ref[pl.ds(rank, 1), :] >> 13) & 1
-        picked = jnp.where(half == 0, both[0:64], both[64:128])
-        for group in range(8):
-            rows_ref[pl.ds(group * 8 * CAP + rank, 8, stride=CAP), :] = picked[
-                group * 8 : (group + 1) * 8
-            ]
+    send_rows.wait()
+    for copy in copies:
+        copy.wait()
+
+    def gather(step, carry):
+        for odd in range(2):
+            rank = step * 2 + odd
+            for src in range(DEVS):
+                got_ref[odd, src : src + 1, :] = table_ref[pl.ds(row_smem[rank, src], 1), :]
+            both = got_ref[odd].T
+            half = (code_t_ref[pl.ds(rank, 1), :] >> 13) & 1
+            picked = jnp.where(half == 0, both[0:64], both[64:128])
+            for group in range(8):
+                rows_ref[pl.ds(group * 8 * CAP + rank, 8, stride=CAP), :] = picked[
+                    group * 8 : (group + 1) * 8
+                ]
         return carry
 
-    lax.fori_loop(0, CAP, gather, 0)
+    lax.fori_loop(0, CAP // 2, gather, 0)
 
     def chunk(at, carry):
         base = pl.multiple_of(at * 8, 8)
@@ -385,32 +416,34 @@
 
     lax.fori_loop(0, CAP // 8, chunk, 0)
     for part in range(WIDE // 128):
-        span = slice(part * 128, (part + 1) * 128)
-        reply_ref[:, span] = proj_ref[span, :].T
+        reply_ref[:, part, :] = proj_ref[part * 128 : (part + 1) * 128, :].T
 
 
 def reply_of(codes, cameras, table):
+    smem = pl.BlockSpec(memory_space=pltpu.SMEM)
+    vmem = pl.BlockSpec(memory_space=pltpu.VMEM)
+    hbm = pl.BlockSpec(memory_space=pltpu.HBM)
     return pl.pallas_call(
         reply_kernel,
         name="reply",
         out_shape=(
-            jax.ShapeDtypeStruct((DEVS, WIDE), F32),
+            jax.ShapeDtypeStruct((DEVS, WIDE // 128, 128), F32),
             jax.ShapeDtypeStruct((64 * CAP, DEVS), F32),
         ),
-        in_specs=[
-            pl.BlockSpec(memory_space=pltpu.SMEM),
-            pl.BlockSpec(memory_space=pltpu.SMEM),
-            pl.BlockSpec(memory_space=pltpu.VMEM),
-            pl.BlockSpec(memory_space=pltpu.VMEM),
-        ],
-        out_specs=(pl.BlockSpec(memory_space=pltpu.VMEM), pl.BlockSpec(memory_space=pltpu.VMEM)),
+        in_specs=[smem, vmem, hbm],
+        out_specs=(vmem, vmem),
         scratch_shapes=[
             pltpu.VMEM((DEVS, DEVS), jnp.int32),
-            pltpu.VMEM((DEVS, 128), F32),
+            pltpu.VMEM((CAP, DEVS), jnp.int32),
+            pltpu.SMEM((CAP, DEVS), jnp.int32),
+            pltpu.VMEM((HALF, 128), F32),
+            pltpu.VMEM((2, DEVS, 128), F32),
             pltpu.VMEM((WIDE, DEVS), F32),
+            pltpu.SemaphoreType.DMA((PIECES,)),
+            pltpu.SemaphoreType.DMA,
         ],
-        compiler_params=pltpu.CompilerParams(vmem_limit_bytes=32 << 20),
-    )(codes, cameras, codes, table)
+        compiler_params=pltpu.CompilerParams(vmem_limit_bytes=48 << 20),
+    )(cameras, codes, in_hbm(table))
 
 
 def render_kernel(
@@ -433,7 +466,7 @@
 ):
     for part in range(WIDE // 128):
         span = slice(part * 128, (part + 1) * 128)
-        flipped = arrived_ref[:, span].T
+        flipped = arrived_ref[:, part, :].T
         for piece, value in enumerate(split_three(flipped)):
             split_ref[span, piece * 128 : (piece + 1) * 128] = value.astype(BF16)
     upper = upper_strict()
@@ -598,7 +631,7 @@
         back = sum_ref[span, :].T
         if part == WIDE // 128 - 1:
             back = back + jnp.sum(expo, axis=0, keepdims=True)
-        back_ref[:, span] = back
+        back_ref[:, part, :] = back
 
 
 def render_of(tile_view, tile_spot, exposure, d_image, entries, arrived):
@@ -607,7 +640,7 @@
     return pl.pallas_call(
         render_kernel,
         name="render",
-        out_shape=jax.ShapeDtypeStruct((DEVS, WIDE), F32),
+        out_shape=jax.ShapeDtypeStruct((DEVS, WIDE // 128, 128), F32),
         in_specs=[smem, smem, smem, vmem, vmem, vmem],
         out_specs=vmem,
         scratch_shapes=[
@@ -630,9 +663,8 @@
 
 
 def update_kernel(
+    camera_ref,
     code_ref,
-    camera_ref,
-    code_vec_ref,
     arrived_ref,
     rows_ref,
     params_hbm,
@@ -643,6 +675,8 @@
     v_out,
     expo_ref,
     code_t_ref,
+    row_t_ref,
+    row_smem,
     cot_ref,
     grad_ref,
     spread_ref,
@@ -652,34 +686,38 @@
     v_ref,
     in_sems,
     out_sems,
+    row_sem,
     *tables,
 ):
     held = ((params_hbm, params_ref, params_out), (m_hbm, m_ref, m_out), (v_hbm, v_ref, v_out))
 
     def fetch(part):
-        span = pl.ds(part * SPAN, SPAN)
+        span = pl.ds(pl.multiple_of(part * SPAN, SPAN), SPAN)
         return [
             pltpu.make_async_copy(source.at[:, span], kept.at[:, span], in_sems.at[at, part])
             for at, (source, kept, unused) in enumerate(held)
         ]
 
     def give(part):
-        span = pl.ds(part * SPAN, SPAN)
+        span = pl.ds(pl.multiple_of(part * SPAN, SPAN), SPAN)
         return [
             pltpu.make_async_copy(kept.at[:, span], target.at[:, span], out_sems.at[at, part])
             for at, (unused, kept, target) in enumerate(held)
         ]
 
+    code_t_ref[...] = code_ref[...].T
+    row_t_ref[...] = code_t_ref[0:CAP, :] & (HALF - 1)
+    send_rows = pltpu.make_async_copy(row_t_ref, row_smem, row_sem)
+    send_rows.start()
     for part in range(PARTS):
         for copy in fetch(part):
             copy.start()
-    code_t_ref[...] = code_vec_ref[...].T
-    expo_ref[...] = jnp.broadcast_to(
-        jnp.sum(arrived_ref[:, 384:WIDE], axis=0, keepdims=True), (8, 128)
-    )
+    shares = jnp.sum(arrived_ref[:, 3, :], axis=0, keepdims=True) * (1.0 / DEVS)
+    for view in range(TILES):
+        first = USED - 384 + 3 * view
+        expo_ref[view : view + 1, :] = shares[:, first : first + 3]
     for part in range(WIDE // 128):
-        span = slice(part * 128, (part + 1) * 128)
-        cot_ref[span, :] = arrived_ref[:, span].T
+        cot_ref[part * 128 : (part + 1) * 128, :] = arrived_ref[:, part, :].T
     for table in tables:
         table[...] = jnp.zeros_like(table)
     grad_ref[PARAMS * CAP :, :] = jnp.zeros(((64 - PARAMS) * CAP, DEVS), F32)
@@ -696,38 +734,50 @@
         return carry
 
     lax.fori_loop(0, CAP // 8, chunk, 0)
-
-    def scatter(rank, carry):
-        half = (code_t_ref[pl.ds(rank, 1), :] >> 13) & 1
-        mine = jnp.concatenate(
-            [grad_ref[pl.ds(group * 8 * CAP + rank, 8, stride=CAP), :] for group in range(8)],
-            axis=0,
-        )
-        both = jnp.concatenate(
-            [jnp.where(half == 0, mine, 0.0), jnp.where(half == 1, mine, 0.0)], axis=0
-        )
-        spread_ref[...] = both.T
-        for src in range(DEVS):
-            row = code_ref[src, rank + 64]
-            table = tables[src % TABLES]
-            table[pl.ds(row, 1), :] = table[pl.ds(row, 1), :] + spread_ref[src : src + 1, :]
+    send_rows.wait()
+
+    def scatter(step, carry):
+        for odd in range(2):
+            rank = step * 2 + odd
+            half = (code_t_ref[pl.ds(rank, 1), :] >> 13) & 1
+            mine = jnp.concatenate(
+                [grad_ref[pl.ds(group * 8 * CAP + rank, 8, stride=CAP), :] for group in range(8)],
+                axis=0,
+            )
+            both = jnp.concatenate(
+                [jnp.where(half == 0, mine, 0.0), jnp.where(half == 1, mine, 0.0)], axis=0
+            )
+            spread_ref[odd] = both.T
+            for first in range(0, DEVS, 2 * TABLES):
+                rows = [row_smem[rank, first + at] for at in range(2 * TABLES)]
+                olds = [
+                    tables[at % TABLES][pl.ds(rows[at], 1), :] for at in range(2 * TABLES)
+                ]
+                news = [
+                    olds[at] + spread_ref[odd, first + at : first + at + 1, :]
+                    for at in range(TABLES)
+                ]
+                for at in range(TABLES, 2 * TABLES):
+                    old = jnp.where(rows[at] == rows[at - TABLES], news[at - TABLES], olds[at])
+                    news.append(old + spread_ref[odd, first + at : first + at + 1, :])
+                for at in range(2 * TABLES):
+                    tables[at % TABLES][pl.ds(rows[at], 1), :] = news[at]
         return carry
 
-    lax.fori_loop(0, CAP, scatter, 0)
-
-    for part in range(PARTS):
+    lax.fori_loop(0, CAP // 2, scatter, 0)
+
+    def finish(part, carry):
         for copy in fetch(part):
             copy.wait()
-
-        def step(at, carry):
+        for at in range(SPAN // 256):
             rows = pl.ds(pl.multiple_of(part * (SPAN // 2) + at * 128, 128), 128)
             total = tables[0][rows, :]
             for table in tables[1:]:
                 total = total + table[rows, :]
-            flip_ref[...] = total.T
+            flip_ref[at] = total.T
             for half in range(2):
                 span = pl.ds(pl.multiple_of(part * SPAN + at * 256 + half * 128, 128), 128)
-                gradient = flip_ref[half * 64 : half * 64 + PARAMS, :]
+                gradient = flip_ref[at, half * 64 : half * 64 + PARAMS, :]
                 new_m = beta_first * m_ref[:, span] + (1.0 - beta_first) * gradient
                 new_v = beta_second * v_ref[:, span] + (1.0 - beta_second) * gradient * gradient
                 m_ref[:, span] = new_m
@@ -735,11 +785,11 @@
                 params_ref[:, span] = params_ref[:, span] - learn_rate * (new_m / fix_first) / (
                     jnp.sqrt(new_v / fix_second) + adam_eps
                 )
-            return carry
-
-        lax.fori_loop(0, SPAN // 256, step, 0)
         for copy in give(part):
             copy.start()
+        return carry
+
+    lax.fori_loop(0, PARTS, finish, 0)
     for part in range(PARTS):
         for copy in give(part):
             copy.wait()
@@ -753,21 +803,24 @@
     return pl.pallas_call(
         update_kernel,
         name="update",
-        out_shape=(whole, whole, whole, jax.ShapeDtypeStruct((8, 128), F32)),
-        in_specs=[smem, smem, vmem, vmem, vmem, hbm, hbm, hbm],
+        out_shape=(whole, whole, whole, jax.ShapeDtypeStruct((4, 3), F32)),
+        in_specs=[smem, vmem, vmem, vmem, hbm, hbm, hbm],
         out_specs=(hbm, hbm, hbm, vmem),
         scratch_shapes=[
             pltpu.VMEM((DEVS, DEVS), jnp.int32),
+            pltpu.VMEM((CAP, DEVS), jnp.int32),
+            pltpu.SMEM((CAP, DEVS), jnp.int32),
             pltpu.VMEM((WIDE, DEVS), F32),
             pltpu.VMEM((64 * CAP, DEVS), F32),
-            pltpu.VMEM((DEVS, 128), F32),
-            pltpu.VMEM((128, 128), F32),
+            pltpu.VMEM((2, DEVS, 128), F32),
+            pltpu.VMEM((SPAN // 256, 128, 128), F32),
         ]
         + [pltpu.VMEM((PARAMS, GDEV), F32)] * 3
         + [pltpu.SemaphoreType.DMA((3, PARTS))] * 2
+        + [pltpu.SemaphoreType.DMA]
         + [pltpu.VMEM((HALF, 128), F32)] * TABLES,
         compiler_params=pltpu.CompilerParams(vmem_limit_bytes=48 << 20),
-    )(codes, cameras, codes, arrived, rows, params, adam_m, adam_v)
+    )(cameras, codes, arrived, rows, in_hbm(params), in_hbm(adam_m), in_hbm(adam_v))
 
 
 def exchange(value):
@@ -794,11 +847,9 @@
     arrived = exchange(reply)
     back = render_of(tile_view, tile_spot, exposure, d_image, entries, arrived)
     returned = exchange(back)
-    new_params, new_m, new_v, expo = update_of(
+    new_params, new_m, new_v, exposure_grad = update_of(
         codes, cameras, returned, rows, params, adam_m, adam_v
     )
-    first = USED - 384
-    exposure_grad = expo[0, first : first + 12].reshape(4, 3) / DEVS
     return (new_params, new_m, new_v, exposure_grad)
 
 

time: 130 us -> 107 us (0.82)
  local copies, waits for them, and re-layouts: 11.1 us -> 0.03 us
  Pallas kernels: 69.6 us -> 58.8 us
    pallas_call x1, Pallas kernels: 28.1 us -> 18.8 us  [update_of(): pl.pallas_call(update_kernel, name='update', out_shape=(whole, whole, who...]
    unnamed x27 -> x11, local copies, waits for them, and re-layouts: 9.18 us -> 0.03 us
    pallas_call x1, Pallas kernels: 5.36 us -> 2.96 us  [route(): pl.pallas_call(route_kernel, name='route', out_shape=(jax.ShapeDtypeStruc...]
    pallas_call x1, Pallas kernels: 5.33 us -> 7.21 us  [table_of(): pl.pallas_call(table_kernel, name='table', grid=(GDEV // COLS,), out_shap...]
  transfers between devices with their start and end apart: 2 -> 2, of which waited for: 2 -> 2; matrix products, arithmetic and copies ran while one was open for 0% -> 0% of each run, Pallas kernels for 4% -> 7%
where the time goes in v3:
time: 107 us
  Pallas kernels  58.8 us (55%)
  starting transfers between devices  19.2 us (18%)
  blocking collectives  15.3 us (14%)
  waiting for transfers between devices  13 us (12%)
    all_to_all x2, starting transfers between devices, exchange(): return lax.all_to_all(value, AXES, split_axis=0, concat_axis=0, tiled=True)  19.2 us
    pallas_call x1, Pallas kernels, update_of(): pl.pallas_call(update_kernel, name='update', out_shape=(whole, whole, who...  18.8 us
    pallas_call x1, Pallas kernels, render_of(): pl.pallas_call(render_kernel, name='render', out_shape=jax.ShapeDtypeStru...  17.8 us
    all_to_all x1, blocking collectives, exchange(): return lax.all_to_all(value, AXES, split_axis=0, concat_axis=0, tiled=True)  15.3 us
    all_to_all x2, waiting for transfers between devices, exchange(): return lax.all_to_all(value, AXES, split_axis=0, concat_axis=0, tiled=True)  13 us
    pallas_call x1, Pallas kernels, reply_of(): pl.pallas_call(reply_kernel, name='reply', out_shape=(jax.ShapeDtypeStruc...  12 us
    pallas_call x1, Pallas kernels, table_of(): pl.pallas_call(table_kernel, name='table', grid=(GDEV // COLS,), out_shap...  7.21 us
    pallas_call x1, Pallas kernels, route(): pl.pallas_call(route_kernel, name='route', out_shape=(jax.ShapeDtypeStruc...  2.96 us
  transfers between devices with their start and end apart: 2, of which 2 were waited for; matrix products, arithmetic and copies ran while one was open for 0% of the time, Pallas kernels for 7%

profile of v3, /device:TPU:1, one launch (start us, length us, event | category | flops | bytes accessed | tf_op | source)
XLA Modules:
  0.0 107.0 jit_solution(14058122168492661743)
XLA Ops:
  0.6 3.0 %route.1 = (s32[128,128]{1,0:T(8,128)}, s32[8,4096]{1,0:T(8,128)S(1)}) custom-call(s32[4]{0:T(128)} %view_ref.1, s32[4]{0:T(128)} %count_hbm.1, s32[4,1024]{1,0:T(4,128)} %owner_hbm.1, s32[4,1024]{1,0:T(4,128)} %local_hbm.1), custom_call_target="tpu_custom_call" | custom-call | tf_op jit(solution)/shard_map/route/pallas_call | solution.py:294
  3.6 11.5 %all-to-all-start = ((s32[128,1,128]{2,1,0:T(1,128)}), s32[128,1,128]{2,1,0:T(1,128)S(1)}, u32[]{:S(2)}, u32[]{:S(2)}) async-start(s32[128,1,128]{2,1,0:T(1,128)} %bitcast.1), calls=%async_computation | async-start | bytes 131072 | tf_op jit(solution)/shard_map/all_to_all | solution.py:827
  15.1 0.0 copy-start
  15.1 7.2 %table.1.table_hbm = f32[8192,128]{1,0:T(8,128)} custom-call(f32[59,16384]{1,0:T(8,128)} %params_hbm.1), custom_call_target="tpu_custom_call" | custom-call | flops 1048576 | bytes 9437184 | tf_op jit(solution)/shard_map/table/pallas_call | solution.py:330
  22.3 0.0 copy-start.4
  22.3 0.0 copy-start.1
  22.3 0.0 copy-start.2
  22.3 0.0 copy-start.3
  22.3 2.1 %all-to-all-done = s32[128,1,128]{2,1,0:T(1,128)S(1)} async-done(((s32[128,1,128]{2,1,0:T(1,128)}), s32[128,1,128]{2,1,0:T(1,128)S(1)}, u32[]{:S(2)}, u32[]{:S(2)}) %all-to-all-start) | async-done | bytes 65568 | tf_op jit(solution)/shard_map/all_to_all | solution.py:827
  24.4 0.0 copy-done
  24.4 12.0 %reply.1 = (f32[128,4,128]{2,1,0:T(4,128)}, f32[3072,128]{1,0:T(8,128)S(1)}) custom-call(f32[4,13]{1,0:T(4,128)S(1)} %copy-done, s32[128,128]{1,0:T(8,128)S(1)} %bitcast.4, f32[8192,128]{1,0:T(8,128)} %table.1.table_hbm), custom_call_target="tpu_custom_call" | custom-call | tf_op jit(solution)/shard_map/reply/pallas_call | solution.py:426
  36.5 7.7 %all-to-all-start.1 = ((f32[128,4,128]{2,1,0:T(4,128)}), f32[128,4,128]{2,1,0:T(4,128)S(1)}, u32[]{:S(2)}, u32[]{:S(2)}) async-start(f32[128,4,128]{2,1,0:T(4,128)} %get-tuple-element.10), calls=%async_computation.1 | async-start | bytes 524288 | tf_op jit(solution)/shard_map/all_to_all | solution.py:827
  44.2 0.0 copy-done.4
  44.2 10.9 %all-to-all-done.1.arrived_ref = f32[128,4,128]{2,1,0:T(4,128)S(1)} async-done(((f32[128,4,128]{2,1,0:T(4,128)}), f32[128,4,128]{2,1,0:T(4,128)S(1)}, u32[]{:S(2)}, u32[]{:S(2)}) %all-to-all-start.1) | async-done | bytes 262176 | tf_op jit(solution)/shard_map/all_to_all | solution.py:827
  55.1 0.0 copy-done.1
  55.1 0.0 copy-done.2
  55.1 0.0 copy-done.3
  55.1 17.8 %render.1 = f32[128,4,128]{2,1,0:T(4,128)S(1)} custom-call(s32[4]{0:T(128)S(1)} %copy-done.2, s32[4]{0:T(128)S(1)} %copy-done.3, f32[4,3]{1,0:T(4,128)S(1)} %copy-done.1, f32[4,3,256]{2,1,0:T(4,128)S(1)} %copy.17.d_image_ref, s32[8,4096]{1,0:T(8,128)S(1)} %get-tuple-element.9.entry_ref, f32[128,4,128]{2,1,0:T(4,128)S(1)} %all-to-all-done.1.arrived_ref), custom_call_target="tpu_custom_call" | custom-call | tf_op jit(solution)/shard_map/render/pallas_call | solution.py:640
  72.9 15.3 %all_to_all.21.arrived_ref = f32[128,4,128]{2,1,0:T(4,128)S(1)} all-to-all(f32[128,4,128]{2,1,0:T(4,128)S(1)} %render.1), channel_id=1, replica_groups=mesh['tiles'=16,'gauss'=8] {'tiles','gauss'}, dimensions={0} | all-to-all | bytes 524288 | tf_op jit(solution)/shard_map/all_to_all | solution.py:827
  88.2 18.8 %update.1 = (f32[59,16384]{1,0:T(8,128)}, f32[59,16384]{1,0:T(8,128)}, f32[59,16384]{1,0:T(8,128)}, f32[4,3]{1,0:T(4,128)}) custom-call(f32[4,13]{1,0:T(4,128)S(1)} %copy-done, s32[128,128]{1,0:T(8,128)S(1)} %bitcast.5, f32[128,4,128]{2,1,0:T(4,128)S(1)} %all_to_all.21.arrived_ref, f32[3072,128]{1,0:T(8,128)S(1)} %get-tuple-element.11.rows_ref, ...), custom_call_target="tpu_custom_call" | custom-call | tf_op jit(solution)/shard_map/update/pallas_call | solution.py:803
  (1 shorter events, 0.0 us)
Async XLA Ops:
  3.6 20.8 %all-to-all-start = ((s32[128,1,128]{2,1,0:T(1,128)}), s32[128,1,128]{2,1,0:T(1,128)S(1)}, u32[]{:S(2)}, u32[]{:S(2)}) async-start(s32[128,1,128]{2,1,0:T(1,128)} %bitcast.1), calls=%async_computation | async-start | bytes 131072 | tf_op jit(solution)/shard_map/all_to_all | solution.py:827
  15.1 9.3 %copy-start = (f32[4,13]{1,0:T(4,128)S(1)}, f32[4,13]{1,0:T(4,128)}, u32[]{:S(2)}) copy-start(f32[4,13]{1,0:T(4,128)} %camera_ref.3) | copy-start | bytes 628
  22.3 21.8 %copy-start.4 = (f32[4,3,256]{2,0,1:T(4,128)S(1)}, f32[4,3,256]{2,0,1:T(4,128)}, u32[]{:S(2)}) copy-start(f32[4,3,256]{2,0,1:T(4,128)} %param.21) | copy-start | bytes 36868
  22.3 32.7 %copy-start.1 = (f32[4,3]{1,0:T(4,128)S(1)}, f32[4,3]{1,0:T(4,128)}, u32[]{:S(2)}) copy-start(f32[4,3]{1,0:T(4,128)} %gain_ref.1) | copy-start | bytes 148
  22.3 32.7 %copy-start.2 = (s32[4]{0:T(128)S(1)}, s32[4]{0:T(128)}, u32[]{:S(2)}) copy-start(s32[4]{0:T(128)} %view_ref.1) | copy-start | bytes 52
  22.3 32.7 %copy-start.3 = (s32[4]{0:T(128)S(1)}, s32[4]{0:T(128)}, u32[]{:S(2)}) copy-start(s32[4]{0:T(128)} %spot_ref.1) | copy-start | bytes 52
  36.5 18.6 %all-to-all-start.1 = ((f32[128,4,128]{2,1,0:T(4,128)}), f32[128,4,128]{2,1,0:T(4,128)S(1)}, u32[]{:S(2)}, u32[]{:S(2)}) async-start(f32[128,4,128]{2,1,0:T(4,128)} %get-tuple-element.10), calls=%async_computation.1 | async-start | bytes 524288 | tf_op jit(solution)/shard_map/all_to_all | solution.py:827

commit v4 on v3

--- a/solution.py
+++ b/solution.py
@@ -312,29 +312,57 @@
     )(*[in_hbm(given) for given in (tile_view, block_counts, entry_owner, entry_local)])
 
 
-COLS = 2048
-
-
-def table_kernel(params_ref, table_ref, pad_ref):
-    @pl.when(pl.program_id(0) == 0)
-    def _():
-        pad_ref[...] = jnp.zeros_like(pad_ref)
-
-    for at in range(COLS // 256):
-        pad_ref[at, 0:PARAMS, :] = params_ref[:, at * 256 : at * 256 + 128]
-        pad_ref[at, 64 : 64 + PARAMS, :] = params_ref[:, at * 256 + 128 : at * 256 + 256]
-        table_ref[at * 128 : (at + 1) * 128, :] = pad_ref[at].T
+PIECES = 8
+PIECE = HALF // PIECES
+
+
+def table_kernel(params_hbm, table_hbm, params_ref, table_ref, in_sems, out_sems):
+    takes = []
+    gives = []
+    for piece in range(PIECES):
+        cols = pl.ds(piece * 2 * PIECE, 2 * PIECE)
+        takes.append(
+            pltpu.make_async_copy(params_hbm.at[:, cols], params_ref.at[:, cols], in_sems.at[piece])
+        )
+        rows = pl.ds(piece * PIECE, PIECE)
+        gives.append(
+            pltpu.make_async_copy(table_ref.at[rows], table_hbm.at[rows], out_sems.at[piece])
+        )
+    for copy in takes:
+        copy.start()
+    gap = jnp.zeros((64 - PARAMS, 128), F32)
+    for piece in range(PIECES):
+        takes[piece].wait()
+        for at in range(piece * (PIECE // 128), (piece + 1) * (PIECE // 128)):
+            both = jnp.concatenate(
+                [
+                    params_ref[:, at * 256 : at * 256 + 128],
+                    gap,
+                    params_ref[:, at * 256 + 128 : at * 256 + 256],
+                    gap,
+                ],
+                axis=0,
+            )
+            table_ref[at * 128 : (at + 1) * 128, :] = both.T
+        gives[piece].start()
+    for copy in gives:
+        copy.wait()
 
 
 def table_of(params):
+    hbm = pl.BlockSpec(memory_space=pltpu.HBM)
     return pl.pallas_call(
         table_kernel,
         name="table",
-        grid=(GDEV // COLS,),
         out_shape=pltpu.HBM((HALF, 128), F32),
-        in_specs=[pl.BlockSpec((PARAMS, COLS), lambda i: (0, i))],
-        out_specs=pl.BlockSpec((COLS // 2, 128), lambda i: (i, 0)),
-        scratch_shapes=[pltpu.VMEM((COLS // 256, 128, 128), F32)],
+        in_specs=[hbm],
+        out_specs=hbm,
+        scratch_shapes=[
+            pltpu.VMEM((PARAMS, GDEV), F32),
+            pltpu.VMEM((HALF, 128), F32),
+            pltpu.SemaphoreType.DMA((PIECES,)),
+            pltpu.SemaphoreType.DMA((PIECES,)),
+        ],
         compiler_params=pltpu.CompilerParams(vmem_limit_bytes=24 << 20),
         cost_estimate=pl.CostEstimate(flops=1 << 20, bytes_accessed=9 << 20, transcendentals=0),
     )(in_hbm(params))
@@ -353,9 +381,6 @@
         )
         for at in range(13)
     ]
-
-
-PIECES = 8
 
 
 def reply_kernel(
@@ -447,13 +472,18 @@
 
 
 def render_kernel(
+    view_hbm,
+    spot_hbm,
+    gain_hbm,
+    d_image_hbm,
+    entry_ref,
+    arrived_ref,
+    back_ref,
     view_ref,
     spot_ref,
     gain_ref,
     d_image_ref,
-    entry_ref,
-    arrived_ref,
-    back_ref,
+    sems,
     split_ref,
     tri_ref,
     low_ref,
@@ -464,6 +494,19 @@
     shade_ref,
     sum_ref,
 ):
+    copies = [
+        pltpu.make_async_copy(source, target, sems.at[at])
+        for at, (source, target) in enumerate(
+            (
+                (view_hbm, view_ref),
+                (spot_hbm, spot_ref),
+                (gain_hbm, gain_ref),
+                (d_image_hbm, d_image_ref),
+            )
+        )
+    ]
+    for copy in copies:
+        copy.start()
     for part in range(WIDE // 128):
         span = slice(part * 128, (part + 1) * 128)
         flipped = arrived_ref[:, part, :].T
@@ -524,7 +567,7 @@
         mid_x = ((spot - line * ACROSS) * TILE + TILE // 2).astype(F32)
         mid_y = (line * TILE + TILE // 2).astype(F32)
         gains = [gain_ref[view, ch] for ch in range(3)]
-        d_rows = [d_image_ref[tile, ch : ch + 1, :] for ch in range(3)]
+        d_rows = [d_image_ref[ch, pl.ds(tile, 1), :] for ch in range(3)]
         d1, d2, d3 = split_three(rows8(d_rows))
         pixel_rows = jnp.concatenate([d1, d2, d3, jnp.zeros((8, TPIX), F32)], axis=0).astype(BF16)
         pixel_rows = jnp.concatenate([pixel_rows, pixel_rows], axis=1)
@@ -625,6 +668,8 @@
             (lane_at == iota((8, 128), 0)) & (lane_at < 3), expo_cols, 0.0
         )
 
+    for copy in copies:
+        copy.wait()
     expo = lax.fori_loop(0, TILES, tile_step, jnp.zeros((8, 128), F32))
     for part in range(WIDE // 128):
         span = slice(part * 128, (part + 1) * 128)
@@ -635,15 +680,21 @@
 
 
 def render_of(tile_view, tile_spot, exposure, d_image, entries, arrived):
-    smem = pl.BlockSpec(memory_space=pltpu.SMEM)
+    hbm = pl.BlockSpec(memory_space=pltpu.HBM)
     vmem = pl.BlockSpec(memory_space=pltpu.VMEM)
+    given = (tile_view, tile_spot, exposure, jnp.transpose(d_image, (1, 0, 2)))
     return pl.pallas_call(
         render_kernel,
         name="render",
         out_shape=jax.ShapeDtypeStruct((DEVS, WIDE // 128, 128), F32),
-        in_specs=[smem, smem, smem, vmem, vmem, vmem],
+        in_specs=[hbm, hbm, hbm, hbm, vmem, vmem],
         out_specs=vmem,
         scratch_shapes=[
+            pltpu.SMEM((TILES,), jnp.int32),
+            pltpu.SMEM((TILES,), jnp.int32),
+            pltpu.SMEM((4, 3), F32),
+            pltpu.VMEM((3, TILES, TPIX), F32),
+            pltpu.SemaphoreType.DMA((4,)),
             pltpu.VMEM((WIDE, 3 * DEVS), BF16),
             pltpu.VMEM((2 * BLOCK, BLOCK), BF16),
             pltpu.VMEM((2 * BLOCK, BLOCK), BF16),
@@ -655,7 +706,7 @@
             pltpu.VMEM((WIDE, DEVS), F32),
         ],
         compiler_params=pltpu.CompilerParams(vmem_limit_bytes=32 << 20),
-    )(tile_view, tile_spot, exposure, d_image, entries, arrived)
+    )(*[in_hbm(value) for value in given], entries, arrived)
 
 
 PARTS = 8

time: 107 us -> 103 us (0.963)
  blocking collectives: 15.3 us -> 30.6 us
  starting transfers between devices: 19.2 us -> 11.5 us
  waiting for transfers between devices: 13 us -> 5.71 us
  Pallas kernels: 58.8 us -> 54.4 us
    all_to_all x1 -> x2, blocking collectives: 15.3 us -> 30.6 us  [exchange(): return lax.all_to_all(value, AXES, split_axis=0, concat_axis=0, tiled=True)]
    all_to_all x2 -> x1, starting transfers between devices: 19.2 us -> 11.5 us  [exchange(): return lax.all_to_all(value, AXES, split_axis=0, concat_axis=0, tiled=True)]
    all_to_all x2 -> x1, waiting for transfers between devices: 13 us -> 5.71 us  [exchange(): return lax.all_to_all(value, AXES, split_axis=0, concat_axis=0, tiled=True)]
    pallas_call x1, Pallas kernels: 7.21 us -> 3.6 us  [table_of(): pl.pallas_call(table_kernel, name='table', out_shape=pltpu.HBM((HALF, 128...]
  transfers between devices with their start and end apart: 2 -> 1, of which waited for: 2 -> 1; matrix products, arithmetic and copies ran while one was open for 0% -> 0% of each run, Pallas kernels for 7% -> 4%
where the time goes in v4:
time: 103 us
  Pallas kernels  54.4 us (53%)
  blocking collectives  30.6 us (30%)
  starting transfers between devices  11.5 us (11%)
  waiting for transfers between devices  5.71 us (6%)
    all_to_all x2, blocking collectives, exchange(): return lax.all_to_all(value, AXES, split_axis=0, concat_axis=0, tiled=True)  30.6 us
    pallas_call x1, Pallas kernels, update_of(): pl.pallas_call(update_kernel, name='update', out_shape=(whole, whole, who...  18.8 us
    pallas_call x1, Pallas kernels, render_of(): pl.pallas_call(render_kernel, name='render', out_shape=jax.ShapeDtypeStru...  17.8 us
    all_to_all x1, starting transfers between devices, exchange(): return lax.all_to_all(value, AXES, split_axis=0, concat_axis=0, tiled=True)  11.5 us
    pallas_call x1, Pallas kernels, reply_of(): pl.pallas_call(reply_kernel, name='reply', out_shape=(jax.ShapeDtypeStruc...  11.3 us
    all_to_all x1, waiting for transfers between devices, exchange(): return lax.all_to_all(value, AXES, split_axis=0, concat_axis=0, tiled=True)  5.71 us
    pallas_call x1, Pallas kernels, table_of(): pl.pallas_call(table_kernel, name='table', out_shape=pltpu.HBM((HALF, 128...  3.6 us
    pallas_call x1, Pallas kernels, route(): pl.pallas_call(route_kernel, name='route', out_shape=(jax.ShapeDtypeStruc...  2.96 us
  transfers between devices with their start and end apart: 1, of which 1 were waited for; matrix products, arithmetic and copies ran while one was open for 0% of the time, Pallas kernels for 4%

profile of v4, /device:TPU:1, one launch (start us, length us, event | category | flops | bytes accessed | tf_op | source)
XLA Modules:
  0.0 102.9 jit_solution(12456856025194317698)
XLA Ops:
  0.6 3.0 %route.1 = (s32[128,128]{1,0:T(8,128)}, s32[8,4096]{1,0:T(8,128)S(1)}) custom-call(s32[4]{0:T(128)} %view_hbm.3, s32[4]{0:T(128)} %count_hbm.1, s32[4,1024]{1,0:T(4,128)} %owner_hbm.1, s32[4,1024]{1,0:T(4,128)} %local_hbm.1), custom_call_target="tpu_custom_call" | custom-call | tf_op jit(solution)/shard_map/route/pallas_call | solution.py:294
  3.6 11.5 %all-to-all-start = ((s32[128,1,128]{2,1,0:T(1,128)}), s32[128,1,128]{2,1,0:T(1,128)S(1)}, u32[]{:S(2)}, u32[]{:S(2)}) async-start(s32[128,1,128]{2,1,0:T(1,128)} %bitcast.1), calls=%async_computation | async-start | bytes 131072 | tf_op jit(solution)/shard_map/all_to_all | solution.py:878
  15.1 0.0 copy-start
  15.1 3.6 %table.1.table_hbm = f32[8192,128]{1,0:T(8,128)} custom-call(f32[59,16384]{1,0:T(8,128)} %params_hbm.3), custom_call_target="tpu_custom_call" | custom-call | flops 1048576 | bytes 9437184 | tf_op jit(solution)/shard_map/table/pallas_call | solution.py:354
  18.7 5.7 %all-to-all-done = s32[128,1,128]{2,1,0:T(1,128)S(1)} async-done(((s32[128,1,128]{2,1,0:T(1,128)}), s32[128,1,128]{2,1,0:T(1,128)S(1)}, u32[]{:S(2)}, u32[]{:S(2)}) %all-to-all-start) | async-done | bytes 65568 | tf_op jit(solution)/shard_map/all_to_all | solution.py:878
  24.4 0.0 copy-done
  24.4 11.3 %reply.1 = (f32[128,4,128]{2,1,0:T(4,128)S(1)}, f32[3072,128]{1,0:T(8,128)S(1)}) custom-call(f32[4,13]{1,0:T(4,128)S(1)} %copy-done, s32[128,128]{1,0:T(8,128)S(1)} %bitcast.5, f32[8192,128]{1,0:T(8,128)} %table.1.table_hbm), custom_call_target="tpu_custom_call" | custom-call | tf_op jit(solution)/shard_map/reply/pallas_call | solution.py:451
  35.8 15.3 %all_to_all.21.arrived_ref = f32[128,4,128]{2,1,0:T(4,128)S(1)} all-to-all(f32[128,4,128]{2,1,0:T(4,128)S(1)} %get-tuple-element.10), channel_id=1, replica_groups=mesh['tiles'=16,'gauss'=8] {'tiles','gauss'}, dimensions={0} | all-to-all | bytes 524288 | tf_op jit(solution)/shard_map/all_to_all | solution.py:878
  51.1 17.8 %render.1 = f32[128,4,128]{2,1,0:T(4,128)S(1)} custom-call(s32[4]{0:T(128)} %view_hbm.3, s32[4]{0:T(128)} %spot_hbm.1, f32[4,3]{1,0:T(4,128)} %gain_hbm.1, f32[3,4,256]{2,1,0:T(4,128)} %bitcast.7, s32[8,4096]{1,0:T(8,128)S(1)} %get-tuple-element.9.entry_ref, f32[128,4,128]{2,1,0:T(4,128)S(1)} %all_to_all.21.arrived_ref), custom_call_target="tpu_custom_call" | custom-call | tf_op jit(solution)/shard_map/render/pallas_call | solution.py:686
  68.9 15.2 %all_to_all.22.arrived_ref = f32[128,4,128]{2,1,0:T(4,128)S(1)} all-to-all(f32[128,4,128]{2,1,0:T(4,128)S(1)} %render.1), channel_id=1, replica_groups=mesh['tiles'=16,'gauss'=8] {'tiles','gauss'}, dimensions={0} | all-to-all | bytes 524288 | tf_op jit(solution)/shard_map/all_to_all | solution.py:878
  84.1 18.8 %update.1 = (f32[59,16384]{1,0:T(8,128)}, f32[59,16384]{1,0:T(8,128)}, f32[59,16384]{1,0:T(8,128)}, f32[4,3]{1,0:T(4,128)}) custom-call(f32[4,13]{1,0:T(4,128)S(1)} %copy-done, s32[128,128]{1,0:T(8,128)S(1)} %bitcast.6, f32[128,4,128]{2,1,0:T(4,128)S(1)} %all_to_all.22.arrived_ref, f32[3072,128]{1,0:T(8,128)S(1)} %get-tuple-element.11.rows_ref, ...), custom_call_target="tpu_custom_call" | custom-call | tf_op jit(solution)/shard_map/update/pallas_call | solution.py:854
Async XLA Ops:
  3.6 20.8 %all-to-all-start = ((s32[128,1,128]{2,1,0:T(1,128)}), s32[128,1,128]{2,1,0:T(1,128)S(1)}, u32[]{:S(2)}, u32[]{:S(2)}) async-start(s32[128,1,128]{2,1,0:T(1,128)} %bitcast.1), calls=%async_computation | async-start | bytes 131072 | tf_op jit(solution)/shard_map/all_to_all | solution.py:878
  15.1 9.3 %copy-start = (f32[4,13]{1,0:T(4,128)S(1)}, f32[4,13]{1,0:T(4,128)}, u32[]{:S(2)}) copy-start(f32[4,13]{1,0:T(4,128)} %camera_ref.3) | copy-start | bytes 628

commit v5 on v4

--- a/solution.py
+++ b/solution.py
@@ -22,6 +22,8 @@
 HALF = GDEV // 2
 VALS = 9
 USED = CAP * VALS
+DEEP = CAP // 2
+ROWS = DEEP * VALS
 WIDE = 512
 TABLES = 4
 UNROLL = 16
@@ -493,6 +495,9 @@
     q_ref,
     shade_ref,
     sum_ref,
+    high_ref,
+    low_part_ref,
+    fold_ref,
 ):
     copies = [
         pltpu.make_async_copy(source, target, sems.at[at])
@@ -508,10 +513,14 @@
     for copy in copies:
         copy.start()
     for part in range(WIDE // 128):
-        span = slice(part * 128, (part + 1) * 128)
-        flipped = arrived_ref[:, part, :].T
-        for piece, value in enumerate(split_three(flipped)):
-            split_ref[span, piece * 128 : (piece + 1) * 128] = value.astype(BF16)
+        sum_ref[part * 128 : (part + 1) * 128, 0:128] = arrived_ref[:, part, :].T
+    for k in range(VALS):
+        for deep in range(2):
+            fold_ref[k * DEEP : (k + 1) * DEEP, deep * 128 : (deep + 1) * 128] = sum_ref[
+                k * CAP + deep * DEEP : k * CAP + (deep + 1) * DEEP, 0:128
+            ]
+    for piece, value in enumerate(split_three(fold_ref[...])):
+        split_ref[:, piece * 256 : (piece + 1) * 256] = value.astype(BF16)
     upper = upper_strict()
     lower = (iota((BLOCK, BLOCK), 0) > iota((BLOCK, BLOCK), 1)).astype(F32).astype(BF16)
     tri_ref[0:BLOCK, :] = upper
@@ -551,7 +560,7 @@
     ).astype(BF16)
     basis_ref[:, 0:TPIX] = basis
     basis_ref[:, TPIX : 2 * TPIX] = basis
-    sum_ref[...] = jnp.zeros_like(sum_ref)
+    fold_ref[...] = jnp.zeros_like(fold_ref)
 
     def rows8(rows):
         at_row = iota((8, rows[0].shape[1]), 0)
@@ -579,13 +588,12 @@
         slots = pl.ds(pl.multiple_of(tile * SLOTS, SLOTS), SLOTS)
         owner = entry_ref[0:1, slots]
         rank = entry_ref[1:2, slots]
-        one_hot = (iota((DEVS, SLOTS), 0) == owner).astype(F32).astype(BF16)
-        found = mxu(
-            split_ref[0:USED, :], jnp.concatenate([one_hot, one_hot, one_hot], axis=0)
-        )
-        here = iota((CAP, SLOTS), 0) == rank
+        deep = (rank >= DEEP).astype(jnp.int32)
+        one_hot = (iota((2 * DEVS, SLOTS), 0) == owner + DEVS * deep).astype(F32).astype(BF16)
+        found = mxu(split_ref[...], jnp.concatenate([one_hot, one_hot, one_hot], axis=0))
+        here = iota((DEEP, SLOTS), 0) == rank - DEEP * deep
         vals = [
-            jnp.sum(jnp.where(here, found[k * CAP : (k + 1) * CAP], 0.0), axis=0, keepdims=True)
+            jnp.sum(jnp.where(here, found[k * DEEP : (k + 1) * DEEP], 0.0), axis=0, keepdims=True)
             for k in range(VALS)
         ]
         shift_x = vals[0] - mid_x
@@ -614,32 +622,62 @@
         color_rows = jnp.concatenate(
             [c1, c2, c1, c2, c3, c1, jnp.zeros((80, SLOTS), F32)], axis=0
         ).astype(BF16)
+        spans = [slice(block * BLOCK, (block + 1) * BLOCK) for block in range(NBLK)]
+        for block, span in enumerate(spans):
+            alpha = jnp.exp(mxu(basis_t_ref[...], poly_rows[:, span]))
+            alpha_ref[block] = alpha
+            fade = alpha * (1.0 + alpha * (0.5 + alpha * (1.0 / 3.0)))
+            fade_hi, fade_lo = split_two(fade)
+            high_ref[block] = fade_hi
+            low_part_ref[block] = fade_lo
+        summed = mxu(
+            jnp.concatenate(
+                [
+                    high_ref[...].reshape(NBLK * TPIX, BLOCK),
+                    low_part_ref[...].reshape(NBLK * TPIX, BLOCK),
+                ],
+                axis=1,
+            ),
+            tri_ref[...],
+        )
         level = jnp.zeros((TPIX, 1), F32)
         seen_parts = []
-        for block in range(NBLK):
-            span = slice(block * BLOCK, (block + 1) * BLOCK)
-            alpha = jnp.exp(mxu(basis_t_ref[...], poly_rows[:, span]))
-            fade = alpha * (1.0 + alpha * (0.5 + alpha * (1.0 / 3.0)))
-            fade_hi, fade_lo = split_two(fade)
-            summed = mxu(jnp.concatenate([fade_hi, fade_lo], axis=1), tri_ref[...]) + level
-            weight = alpha * jnp.exp(-summed)
-            level = summed[:, BLOCK - 1 : BLOCK] + fade[:, BLOCK - 1 : BLOCK]
-            alpha_ref[block] = alpha
-            q_ref[block] = mxu(shade_ref[...], color_rows[:, span]) * weight
+        for block, span in enumerate(spans):
+            alpha = alpha_ref[block]
+            here_sum = summed[block * TPIX : (block + 1) * TPIX] + level
+            weight = alpha * jnp.exp(-here_sum)
+            edge = alpha[:, BLOCK - 1 : BLOCK]
+            level = here_sum[:, BLOCK - 1 : BLOCK] + edge * (
+                1.0 + edge * (0.5 + edge * (1.0 / 3.0))
+            )
+            q_val = mxu(shade_ref[...], color_rows[:, span]) * weight
+            q_ref[block] = q_val
+            q_hi, q_lo = split_two(q_val)
+            high_ref[block] = q_hi
+            low_part_ref[block] = q_lo
             weight_hi, weight_lo = split_two(weight)
             seen = mxu(pixel_rows, jnp.concatenate([weight_hi, weight_lo], axis=0))
             seen_parts.append(seen[0:8] + seen[8:16] + seen[16:24])
         seen = jnp.concatenate(seen_parts, axis=1)
         expo_cols = jnp.sum(color * seen, axis=1, keepdims=True)
+        later = mxu(
+            jnp.concatenate(
+                [
+                    high_ref[...].reshape(NBLK * TPIX, BLOCK),
+                    low_part_ref[...].reshape(NBLK * TPIX, BLOCK),
+                ],
+                axis=1,
+            ),
+            low_ref[...],
+        )
         tail = jnp.zeros((TPIX, 1), F32)
         grad_parts = [None] * NBLK
         for block in reversed(range(NBLK)):
             alpha = alpha_ref[block]
             q_val = q_ref[block]
-            q_hi, q_lo = split_two(q_val)
-            later = mxu(jnp.concatenate([q_hi, q_lo], axis=1), low_ref[...]) + tail
-            d_exp = q_val - later * (alpha * (1.0 + alpha * (1.0 + alpha)))
-            tail = later[:, 0:1] + q_val[:, 0:1]
+            here_sum = later[block * TPIX : (block + 1) * TPIX] + tail
+            d_exp = q_val - here_sum * (alpha * (1.0 + alpha * (1.0 + alpha)))
+            tail = here_sum[:, 0:1] + q_val[:, 0:1]
             d_hi, d_lo = split_two(d_exp)
             grad_parts[block] = mxu(basis_ref[...], jnp.concatenate([d_hi, d_lo], axis=0))[0:8]
         grad = jnp.concatenate(grad_parts, axis=1)
@@ -659,10 +697,10 @@
         low_rows = []
         for value in grads:
             high = value.astype(BF16).astype(F32)
-            high_rows.append(jnp.where(here, high, 0.0).astype(BF16))
-            low_rows.append(jnp.where(here, value - high, 0.0).astype(BF16))
-        both = mxu_bt(jnp.concatenate(high_rows + low_rows, axis=0), one_hot)
-        sum_ref[0:USED, :] += both[0:USED] + both[USED : 2 * USED]
+            high_rows.append(jnp.where(here, high, 0.0))
+            low_rows.append(jnp.where(here, value - high, 0.0))
+        both = mxu_bt(jnp.concatenate(high_rows + low_rows, axis=0).astype(BF16), one_hot)
+        fold_ref[...] += both[0:ROWS] + both[ROWS : 2 * ROWS]
         lane_at = iota((8, 128), 1) - (USED - 384) - 3 * view
         return expo + jnp.where(
             (lane_at == iota((8, 128), 0)) & (lane_at < 3), expo_cols, 0.0
@@ -671,6 +709,12 @@
     for copy in copies:
         copy.wait()
     expo = lax.fori_loop(0, TILES, tile_step, jnp.zeros((8, 128), F32))
+    sum_ref[USED:WIDE, :] = jnp.zeros((WIDE - USED, DEVS), F32)
+    for k in range(VALS):
+        for deep in range(2):
+            sum_ref[k * CAP + deep * DEEP : k * CAP + (deep + 1) * DEEP, :] = fold_ref[
+                k * DEEP : (k + 1) * DEEP, deep * 128 : (deep + 1) * 128
+            ]
     for part in range(WIDE // 128):
         span = slice(part * 128, (part + 1) * 128)
         back = sum_ref[span, :].T
@@ -695,7 +739,7 @@
             pltpu.SMEM((4, 3), F32),
             pltpu.VMEM((3, TILES, TPIX), F32),
             pltpu.SemaphoreType.DMA((4,)),
-            pltpu.VMEM((WIDE, 3 * DEVS), BF16),
+            pltpu.VMEM((ROWS, 6 * DEVS), BF16),
             pltpu.VMEM((2 * BLOCK, BLOCK), BF16),
             pltpu.VMEM((2 * BLOCK, BLOCK), BF16),
             pltpu.VMEM((TPIX, 128), BF16),
@@ -704,6 +748,9 @@
             pltpu.VMEM((NBLK, TPIX, BLOCK), F32),
             pltpu.VMEM((TPIX, 128), BF16),
             pltpu.VMEM((WIDE, DEVS), F32),
+            pltpu.VMEM((NBLK, TPIX, BLOCK), BF16),
+            pltpu.VMEM((NBLK, TPIX, BLOCK), BF16),
+            pltpu.VMEM((ROWS, 2 * DEVS), F32),
         ],
         compiler_params=pltpu.CompilerParams(vmem_limit_bytes=32 << 20),
     )(*[in_hbm(value) for value in given], entries, arrived)

time: 103 us -> 99.3 us (0.964)
  Pallas kernels: 54.4 us -> 50.5 us
    pallas_call x1, Pallas kernels: 17.8 us -> 13.8 us  [render_of(): pl.pallas_call(render_kernel, name='render', out_shape=jax.ShapeDtypeStru...]
where the time goes in v5:
time: 99.3 us; the launch traced here: 98.9 us
  Pallas kernels  50.5 us (51%)
  blocking collectives  30.6 us (31%)
  starting transfers between devices  11.5 us (12%)
  waiting for transfers between devices  5.71 us (6%)
    all_to_all x2, blocking collectives, exchange(): return lax.all_to_all(value, AXES, split_axis=0, concat_axis=0, tiled=True)  30.6 us
    pallas_call x1, Pallas kernels, update_of(): pl.pallas_call(update_kernel, name='update', out_shape=(whole, whole, who...  18.8 us
    pallas_call x1, Pallas kernels, render_of(): pl.pallas_call(render_kernel, name='render', out_shape=jax.ShapeDtypeStru...  13.8 us
    all_to_all x1, starting transfers between devices, exchange(): return lax.all_to_all(value, AXES, split_axis=0, concat_axis=0, tiled=True)  11.5 us
    pallas_call x1, Pallas kernels, reply_of(): pl.pallas_call(reply_kernel, name='reply', out_shape=(jax.ShapeDtypeStruc...  11.3 us
    all_to_all x1, waiting for transfers between devices, exchange(): return lax.all_to_all(value, AXES, split_axis=0, concat_axis=0, tiled=True)  5.71 us
    pallas_call x1, Pallas kernels, table_of(): pl.pallas_call(table_kernel, name='table', out_shape=pltpu.HBM((HALF, 128...  3.6 us
    pallas_call x1, Pallas kernels, route(): pl.pallas_call(route_kernel, name='route', out_shape=(jax.ShapeDtypeStruc...  2.96 us
  transfers between devices with their start and end apart: 1, of which 1 were waited for; matrix products, arithmetic and copies ran while one was open for 0% of the time, Pallas kernels for 4%

profile of v5, /device:TPU:1, one launch (start us, length us, event | category | flops | bytes accessed | tf_op | source)
XLA Modules:
  0.0 98.9 jit_solution(1872256686168374507)
XLA Ops:
  0.6 3.0 %route.1 = (s32[128,128]{1,0:T(8,128)}, s32[8,4096]{1,0:T(8,128)S(1)}) custom-call(s32[4]{0:T(128)} %view_hbm.3, s32[4]{0:T(128)} %count_hbm.1, s32[4,1024]{1,0:T(4,128)} %owner_hbm.1, s32[4,1024]{1,0:T(4,128)} %local_hbm.1), custom_call_target="tpu_custom_call" | custom-call | tf_op jit(solution)/shard_map/route/pallas_call | solution.py:296
  3.6 11.5 %all-to-all-start = ((s32[128,1,128]{2,1,0:T(1,128)}), s32[128,1,128]{2,1,0:T(1,128)S(1)}, u32[]{:S(2)}, u32[]{:S(2)}) async-start(s32[128,1,128]{2,1,0:T(1,128)} %bitcast.1), calls=%async_computation | async-start | bytes 131072 | tf_op jit(solution)/shard_map/all_to_all | solution.py:925
  15.1 0.0 copy-start
  15.1 3.6 %table.1.table_hbm = f32[8192,128]{1,0:T(8,128)} custom-call(f32[59,16384]{1,0:T(8,128)} %params_hbm.3), custom_call_target="tpu_custom_call" | custom-call | flops 1048576 | bytes 9437184 | tf_op jit(solution)/shard_map/table/pallas_call | solution.py:356
  18.7 5.7 %all-to-all-done = s32[128,1,128]{2,1,0:T(1,128)S(1)} async-done(((s32[128,1,128]{2,1,0:T(1,128)}), s32[128,1,128]{2,1,0:T(1,128)S(1)}, u32[]{:S(2)}, u32[]{:S(2)}) %all-to-all-start) | async-done | bytes 65568 | tf_op jit(solution)/shard_map/all_to_all | solution.py:925
  24.4 0.0 copy-done
  24.4 11.3 %reply.1 = (f32[128,4,128]{2,1,0:T(4,128)S(1)}, f32[3072,128]{1,0:T(8,128)S(1)}) custom-call(f32[4,13]{1,0:T(4,128)S(1)} %copy-done, s32[128,128]{1,0:T(8,128)S(1)} %bitcast.5, f32[8192,128]{1,0:T(8,128)} %table.1.table_hbm), custom_call_target="tpu_custom_call" | custom-call | tf_op jit(solution)/shard_map/reply/pallas_call | solution.py:453
  35.8 15.3 %all_to_all.21.arrived_ref = f32[128,4,128]{2,1,0:T(4,128)S(1)} all-to-all(f32[128,4,128]{2,1,0:T(4,128)S(1)} %get-tuple-element.10), channel_id=1, replica_groups=mesh['tiles'=16,'gauss'=8] {'tiles','gauss'}, dimensions={0} | all-to-all | bytes 524288 | tf_op jit(solution)/shard_map/all_to_all | solution.py:925
  51.1 13.8 %render.1 = f32[128,4,128]{2,1,0:T(4,128)S(1)} custom-call(s32[4]{0:T(128)} %view_hbm.3, s32[4]{0:T(128)} %spot_hbm.1, f32[4,3]{1,0:T(4,128)} %gain_hbm.1, f32[3,4,256]{2,1,0:T(4,128)} %bitcast.7, s32[8,4096]{1,0:T(8,128)S(1)} %get-tuple-element.9.entry_ref, f32[128,4,128]{2,1,0:T(4,128)S(1)} %all_to_all.21.arrived_ref), custom_call_target="tpu_custom_call" | custom-call | tf_op jit(solution)/shard_map/render/pallas_call | solution.py:730
  64.9 15.2 %all_to_all.22.arrived_ref = f32[128,4,128]{2,1,0:T(4,128)S(1)} all-to-all(f32[128,4,128]{2,1,0:T(4,128)S(1)} %render.1), channel_id=1, replica_groups=mesh['tiles'=16,'gauss'=8] {'tiles','gauss'}, dimensions={0} | all-to-all | bytes 524288 | tf_op jit(solution)/shard_map/all_to_all | solution.py:925
  80.1 18.8 %update.1 = (f32[59,16384]{1,0:T(8,128)}, f32[59,16384]{1,0:T(8,128)}, f32[59,16384]{1,0:T(8,128)}, f32[4,3]{1,0:T(4,128)}) custom-call(f32[4,13]{1,0:T(4,128)S(1)} %copy-done, s32[128,128]{1,0:T(8,128)S(1)} %bitcast.6, f32[128,4,128]{2,1,0:T(4,128)S(1)} %all_to_all.22.arrived_ref, f32[3072,128]{1,0:T(8,128)S(1)} %get-tuple-element.11.rows_ref, ...), custom_call_target="tpu_custom_call" | custom-call | tf_op jit(solution)/shard_map/update/pallas_call | solution.py:901
Async XLA Ops:
  3.6 20.8 %all-to-all-start = ((s32[128,1,128]{2,1,0:T(1,128)}), s32[128,1,128]{2,1,0:T(1,128)S(1)}, u32[]{:S(2)}, u32[]{:S(2)}) async-start(s32[128,1,128]{2,1,0:T(1,128)} %bitcast.1), calls=%async_computation | async-start | bytes 131072 | tf_op jit(solution)/shard_map/all_to_all | solution.py:925
  15.1 9.3 %copy-start = (f32[4,13]{1,0:T(4,128)S(1)}, f32[4,13]{1,0:T(4,128)}, u32[]{:S(2)}) copy-start(f32[4,13]{1,0:T(4,128)} %camera_ref.3) | copy-start | bytes 628

commit v6 on v5

--- a/solution.py
+++ b/solution.py
@@ -397,29 +397,22 @@
     table_ref,
     got_ref,
     proj_ref,
-    table_sems,
+    table_sem,
     row_sem,
 ):
-    copies = []
-    for piece in range(PIECES):
-        span = pl.ds(piece * (HALF // PIECES), HALF // PIECES)
-        copies.append(
-            pltpu.make_async_copy(table_hbm.at[span], table_ref.at[span], table_sems.at[piece])
-        )
-    for copy in copies:
-        copy.start()
+    take_table = pltpu.make_async_copy(table_hbm, table_ref, table_sem)
+    take_table.start()
     code_t_ref[...] = code_ref[...].T
     row_t_ref[...] = code_t_ref[0:CAP, :] & (HALF - 1)
     send_rows = pltpu.make_async_copy(row_t_ref, row_smem, row_sem)
     send_rows.start()
     proj_ref[USED:WIDE, :] = jnp.zeros((WIDE - USED, DEVS), F32)
     send_rows.wait()
-    for copy in copies:
-        copy.wait()
+    take_table.wait()
 
     def gather(step, carry):
-        for odd in range(2):
-            rank = step * 2 + odd
+        for odd in range(12):
+            rank = step * 12 + odd
             for src in range(DEVS):
                 got_ref[odd, src : src + 1, :] = table_ref[pl.ds(row_smem[rank, src], 1), :]
             both = got_ref[odd].T
@@ -431,7 +424,7 @@
                 ]
         return carry
 
-    lax.fori_loop(0, CAP // 2, gather, 0)
+    lax.fori_loop(0, CAP // 12, gather, 0)
 
     def chunk(at, carry):
         base = pl.multiple_of(at * 8, 8)
@@ -464,9 +457,9 @@
             pltpu.VMEM((CAP, DEVS), jnp.int32),
             pltpu.SMEM((CAP, DEVS), jnp.int32),
             pltpu.VMEM((HALF, 128), F32),
-            pltpu.VMEM((2, DEVS, 128), F32),
+            pltpu.VMEM((12, DEVS, 128), F32),
             pltpu.VMEM((WIDE, DEVS), F32),
-            pltpu.SemaphoreType.DMA((PIECES,)),
+            pltpu.SemaphoreType.DMA,
             pltpu.SemaphoreType.DMA,
         ],
         compiler_params=pltpu.CompilerParams(vmem_limit_bytes=48 << 20),
@@ -789,12 +782,10 @@
 ):
     held = ((params_hbm, params_ref, params_out), (m_hbm, m_ref, m_out), (v_hbm, v_ref, v_out))
 
-    def fetch(part):
-        span = pl.ds(pl.multiple_of(part * SPAN, SPAN), SPAN)
-        return [
-            pltpu.make_async_copy(source.at[:, span], kept.at[:, span], in_sems.at[at, part])
-            for at, (source, kept, unused) in enumerate(held)
-        ]
+    fetches = [
+        pltpu.make_async_copy(source, kept, in_sems.at[at])
+        for at, (source, kept, unused) in enumerate(held)
+    ]
 
     def give(part):
         span = pl.ds(pl.multiple_of(part * SPAN, SPAN), SPAN)
@@ -807,9 +798,8 @@
     row_t_ref[...] = code_t_ref[0:CAP, :] & (HALF - 1)
     send_rows = pltpu.make_async_copy(row_t_ref, row_smem, row_sem)
     send_rows.start()
-    for part in range(PARTS):
-        for copy in fetch(part):
-            copy.start()
+    for copy in fetches:
+        copy.start()
     shares = jnp.sum(arrived_ref[:, 3, :], axis=0, keepdims=True) * (1.0 / DEVS)
     for view in range(TILES):
         first = USED - 384 + 3 * view
@@ -835,8 +825,8 @@
     send_rows.wait()
 
     def scatter(step, carry):
-        for odd in range(2):
-            rank = step * 2 + odd
+        for odd in range(12):
+            rank = step * 12 + odd
             half = (code_t_ref[pl.ds(rank, 1), :] >> 13) & 1
             mine = jnp.concatenate(
                 [grad_ref[pl.ds(group * 8 * CAP + rank, 8, stride=CAP), :] for group in range(8)],
@@ -862,11 +852,12 @@
                     tables[at % TABLES][pl.ds(rows[at], 1), :] = news[at]
         return carry
 
-    lax.fori_loop(0, CAP // 2, scatter, 0)
+    lax.fori_loop(0, CAP // 12, scatter, 0)
+
+    for copy in fetches:
+        copy.wait()
 
     def finish(part, carry):
-        for copy in fetch(part):
-            copy.wait()
         for at in range(SPAN // 256):
             rows = pl.ds(pl.multiple_of(part * (SPAN // 2) + at * 128, 128), 128)
             total = tables[0][rows, :]
@@ -910,11 +901,11 @@
             pltpu.SMEM((CAP, DEVS), jnp.int32),
             pltpu.VMEM((WIDE, DEVS), F32),
             pltpu.VMEM((64 * CAP, DEVS), F32),
-            pltpu.VMEM((2, DEVS, 128), F32),
+            pltpu.VMEM((12, DEVS, 128), F32),
             pltpu.VMEM((SPAN // 256, 128, 128), F32),
         ]
         + [pltpu.VMEM((PARAMS, GDEV), F32)] * 3
-        + [pltpu.SemaphoreType.DMA((3, PARTS))] * 2
+        + [pltpu.SemaphoreType.DMA((3,)), pltpu.SemaphoreType.DMA((3, PARTS))]
         + [pltpu.SemaphoreType.DMA]
         + [pltpu.VMEM((HALF, 128), F32)] * TABLES,
         compiler_params=pltpu.CompilerParams(vmem_limit_bytes=48 << 20),

time: 99.3 us -> 96.7 us (0.974)
  Pallas kernels: 50.5 us -> 47.7 us
    pallas_call x1, Pallas kernels: 18.8 us -> 17.2 us  [update_of(): pl.pallas_call(update_kernel, name='update', out_shape=(whole, whole, who...]
    pallas_call x1, Pallas kernels: 11.3 us -> 10.1 us  [reply_of(): pl.pallas_call(reply_kernel, name='reply', out_shape=(jax.ShapeDtypeStruc...]
where the time goes in v6:
time: 96.7 us; the launch traced here: 96.3 us
  Pallas kernels  47.7 us (49%)
  blocking collectives  30.6 us (32%)
  starting transfers between devices  11.5 us (12%)
  waiting for transfers between devices  5.71 us (6%)
    all_to_all x2, blocking collectives, exchange(): return lax.all_to_all(value, AXES, split_axis=0, concat_axis=0, tiled=True)  30.6 us
    pallas_call x1, Pallas kernels, update_of(): pl.pallas_call(update_kernel, name='update', out_shape=(whole, whole, who...  17.2 us
    pallas_call x1, Pallas kernels, render_of(): pl.pallas_call(render_kernel, name='render', out_shape=jax.ShapeDtypeStru...  13.8 us
    all_to_all x1, starting transfers between devices, exchange(): return lax.all_to_all(value, AXES, split_axis=0, concat_axis=0, tiled=True)  11.5 us
    pallas_call x1, Pallas kernels, reply_of(): pl.pallas_call(reply_kernel, name='reply', out_shape=(jax.ShapeDtypeStruc...  10.1 us
    all_to_all x1, waiting for transfers between devices, exchange(): return lax.all_to_all(value, AXES, split_axis=0, concat_axis=0, tiled=True)  5.71 us
    pallas_call x1, Pallas kernels, table_of(): pl.pallas_call(table_kernel, name='table', out_shape=pltpu.HBM((HALF, 128...  3.6 us
    pallas_call x1, Pallas kernels, route(): pl.pallas_call(route_kernel, name='route', out_shape=(jax.ShapeDtypeStruc...  2.96 us
  transfers between devices with their start and end apart: 1, of which 1 were waited for; matrix products, arithmetic and copies ran while one was open for 0% of the time, Pallas kernels for 4%

profile of v6, /device:TPU:1, one launch (start us, length us, event | category | flops | bytes accessed | tf_op | source)
XLA Modules:
  0.0 96.3 jit_solution(16743069402408223566)
XLA Ops:
  0.6 3.0 %route.1 = (s32[128,128]{1,0:T(8,128)}, s32[8,4096]{1,0:T(8,128)S(1)}) custom-call(s32[4]{0:T(128)} %view_hbm.3, s32[4]{0:T(128)} %count_hbm.1, s32[4,1024]{1,0:T(4,128)} %owner_hbm.1, s32[4,1024]{1,0:T(4,128)} %local_hbm.1), custom_call_target="tpu_custom_call" | custom-call | tf_op jit(solution)/shard_map/route/pallas_call | solution.py:296
  3.6 11.5 %all-to-all-start = ((s32[128,1,128]{2,1,0:T(1,128)}), s32[128,1,128]{2,1,0:T(1,128)S(1)}, u32[]{:S(2)}, u32[]{:S(2)}) async-start(s32[128,1,128]{2,1,0:T(1,128)} %bitcast.1), calls=%async_computation | async-start | bytes 131072 | tf_op jit(solution)/shard_map/all_to_all | solution.py:916
  15.1 0.0 copy-start
  15.1 3.6 %table.1.table_hbm = f32[8192,128]{1,0:T(8,128)} custom-call(f32[59,16384]{1,0:T(8,128)} %params_hbm.3), custom_call_target="tpu_custom_call" | custom-call | flops 1048576 | bytes 9437184 | tf_op jit(solution)/shard_map/table/pallas_call | solution.py:356
  18.7 5.7 %all-to-all-done = s32[128,1,128]{2,1,0:T(1,128)S(1)} async-done(((s32[128,1,128]{2,1,0:T(1,128)}), s32[128,1,128]{2,1,0:T(1,128)S(1)}, u32[]{:S(2)}, u32[]{:S(2)}) %all-to-all-start) | async-done | bytes 65568 | tf_op jit(solution)/shard_map/all_to_all | solution.py:916
  24.4 0.0 copy-done
  24.4 10.1 %reply.1 = (f32[128,4,128]{2,1,0:T(4,128)S(1)}, f32[3072,128]{1,0:T(8,128)S(1)}) custom-call(f32[4,13]{1,0:T(4,128)S(1)} %copy-done, s32[128,128]{1,0:T(8,128)S(1)} %bitcast.5, f32[8192,128]{1,0:T(8,128)} %table.1.table_hbm), custom_call_target="tpu_custom_call" | custom-call | tf_op jit(solution)/shard_map/reply/pallas_call | solution.py:446
  34.6 15.3 %all_to_all.21.arrived_ref = f32[128,4,128]{2,1,0:T(4,128)S(1)} all-to-all(f32[128,4,128]{2,1,0:T(4,128)S(1)} %get-tuple-element.10), channel_id=1, replica_groups=mesh['tiles'=16,'gauss'=8] {'tiles','gauss'}, dimensions={0} | all-to-all | bytes 524288 | tf_op jit(solution)/shard_map/all_to_all | solution.py:916
  49.9 13.8 %render.1 = f32[128,4,128]{2,1,0:T(4,128)S(1)} custom-call(s32[4]{0:T(128)} %view_hbm.3, s32[4]{0:T(128)} %spot_hbm.1, f32[4,3]{1,0:T(4,128)} %gain_hbm.1, f32[3,4,256]{2,1,0:T(4,128)} %bitcast.7, s32[8,4096]{1,0:T(8,128)S(1)} %get-tuple-element.9.entry_ref, f32[128,4,128]{2,1,0:T(4,128)S(1)} %all_to_all.21.arrived_ref), custom_call_target="tpu_custom_call" | custom-call | tf_op jit(solution)/shard_map/render/pallas_call | solution.py:723
  63.7 15.2 %all_to_all.22.arrived_ref = f32[128,4,128]{2,1,0:T(4,128)S(1)} all-to-all(f32[128,4,128]{2,1,0:T(4,128)S(1)} %render.1), channel_id=1, replica_groups=mesh['tiles'=16,'gauss'=8] {'tiles','gauss'}, dimensions={0} | all-to-all | bytes 524288 | tf_op jit(solution)/shard_map/all_to_all | solution.py:916
  78.9 17.2 %update.1 = (f32[59,16384]{1,0:T(8,128)}, f32[59,16384]{1,0:T(8,128)}, f32[59,16384]{1,0:T(8,128)}, f32[4,3]{1,0:T(4,128)}) custom-call(f32[4,13]{1,0:T(4,128)S(1)} %copy-done, s32[128,128]{1,0:T(8,128)S(1)} %bitcast.6, f32[128,4,128]{2,1,0:T(4,128)S(1)} %all_to_all.22.arrived_ref, f32[3072,128]{1,0:T(8,128)S(1)} %get-tuple-element.11.rows_ref, ...), custom_call_target="tpu_custom_call" | custom-call | tf_op jit(solution)/shard_map/update/pallas_call | solution.py:892
Async XLA Ops:
  3.6 20.8 %all-to-all-start = ((s32[128,1,128]{2,1,0:T(1,128)}), s32[128,1,128]{2,1,0:T(1,128)S(1)}, u32[]{:S(2)}, u32[]{:S(2)}) async-start(s32[128,1,128]{2,1,0:T(1,128)} %bitcast.1), calls=%async_computation | async-start | bytes 131072 | tf_op jit(solution)/shard_map/all_to_all | solution.py:916
  15.1 9.3 %copy-start = (f32[4,13]{1,0:T(4,128)S(1)}, f32[4,13]{1,0:T(4,128)}, u32[]{:S(2)}) copy-start(f32[4,13]{1,0:T(4,128)} %camera_ref.3) | copy-start | bytes 628

commit v7 on v6

--- a/solution.py
+++ b/solution.py
@@ -411,8 +411,8 @@
     take_table.wait()
 
     def gather(step, carry):
-        for odd in range(12):
-            rank = step * 12 + odd
+        for odd in range(16):
+            rank = step * 16 + odd
             for src in range(DEVS):
                 got_ref[odd, src : src + 1, :] = table_ref[pl.ds(row_smem[rank, src], 1), :]
             both = got_ref[odd].T
@@ -424,7 +424,7 @@
                 ]
         return carry
 
-    lax.fori_loop(0, CAP // 12, gather, 0)
+    lax.fori_loop(0, CAP // 16, gather, 0)
 
     def chunk(at, carry):
         base = pl.multiple_of(at * 8, 8)
@@ -434,7 +434,7 @@
             proj_ref[pl.ds(k * CAP + base, 8), :] = value
         return carry
 
-    lax.fori_loop(0, CAP // 8, chunk, 0)
+    lax.fori_loop(0, CAP // 8, chunk, 0, unroll=2)
     for part in range(WIDE // 128):
         reply_ref[:, part, :] = proj_ref[part * 128 : (part + 1) * 128, :].T
 
@@ -457,7 +457,7 @@
             pltpu.VMEM((CAP, DEVS), jnp.int32),
             pltpu.SMEM((CAP, DEVS), jnp.int32),
             pltpu.VMEM((HALF, 128), F32),
-            pltpu.VMEM((12, DEVS, 128), F32),
+            pltpu.VMEM((16, DEVS, 128), F32),
             pltpu.VMEM((WIDE, DEVS), F32),
             pltpu.SemaphoreType.DMA,
             pltpu.SemaphoreType.DMA,
@@ -574,11 +574,11 @@
         pixel_rows = jnp.concatenate([d1, d2, d3, jnp.zeros((8, TPIX), F32)], axis=0).astype(BF16)
         pixel_rows = jnp.concatenate([pixel_rows, pixel_rows], axis=1)
         g1, g2, g3 = split_three(rows8([gains[ch] * d_rows[ch] for ch in range(3)]))
-        shade_ref[...] = (
+        shade_ref[tile % 2] = (
             jnp.concatenate([g1, g1, g2, g2, g1, g3, jnp.zeros((80, TPIX), F32)], axis=0)
             .T.astype(BF16)
         )
-        slots = pl.ds(pl.multiple_of(tile * SLOTS, SLOTS), SLOTS)
+        slots = slice(tile * SLOTS, (tile + 1) * SLOTS)
         owner = entry_ref[0:1, slots]
         rank = entry_ref[1:2, slots]
         deep = (rank >= DEEP).astype(jnp.int32)
@@ -617,17 +617,17 @@
         ).astype(BF16)
         spans = [slice(block * BLOCK, (block + 1) * BLOCK) for block in range(NBLK)]
         for block, span in enumerate(spans):
-            alpha = jnp.exp(mxu(basis_t_ref[...], poly_rows[:, span]))
-            alpha_ref[block] = alpha
+            alpha = jnp.exp(mxu(basis_t_ref[:, 0:32], poly_rows[0:32, span]))
+            alpha_ref[tile % 2, block] = alpha
             fade = alpha * (1.0 + alpha * (0.5 + alpha * (1.0 / 3.0)))
             fade_hi, fade_lo = split_two(fade)
-            high_ref[block] = fade_hi
-            low_part_ref[block] = fade_lo
+            high_ref[tile % 2, block] = fade_hi
+            low_part_ref[tile % 2, block] = fade_lo
         summed = mxu(
             jnp.concatenate(
                 [
-                    high_ref[...].reshape(NBLK * TPIX, BLOCK),
-                    low_part_ref[...].reshape(NBLK * TPIX, BLOCK),
+                    high_ref[tile % 2].reshape(NBLK * TPIX, BLOCK),
+                    low_part_ref[tile % 2].reshape(NBLK * TPIX, BLOCK),
                 ],
                 axis=1,
             ),
@@ -636,18 +636,18 @@
         level = jnp.zeros((TPIX, 1), F32)
         seen_parts = []
         for block, span in enumerate(spans):
-            alpha = alpha_ref[block]
+            alpha = alpha_ref[tile % 2, block]
             here_sum = summed[block * TPIX : (block + 1) * TPIX] + level
             weight = alpha * jnp.exp(-here_sum)
             edge = alpha[:, BLOCK - 1 : BLOCK]
             level = here_sum[:, BLOCK - 1 : BLOCK] + edge * (
                 1.0 + edge * (0.5 + edge * (1.0 / 3.0))
             )
-            q_val = mxu(shade_ref[...], color_rows[:, span]) * weight
-            q_ref[block] = q_val
+            q_val = mxu(shade_ref[tile % 2, :, 0:48], color_rows[0:48, span]) * weight
+            q_ref[tile % 2, block] = q_val
             q_hi, q_lo = split_two(q_val)
-            high_ref[block] = q_hi
-            low_part_ref[block] = q_lo
+            high_ref[tile % 2, block] = q_hi
+            low_part_ref[tile % 2, block] = q_lo
             weight_hi, weight_lo = split_two(weight)
             seen = mxu(pixel_rows, jnp.concatenate([weight_hi, weight_lo], axis=0))
             seen_parts.append(seen[0:8] + seen[8:16] + seen[16:24])
@@ -656,8 +656,8 @@
         later = mxu(
             jnp.concatenate(
                 [
-                    high_ref[...].reshape(NBLK * TPIX, BLOCK),
-                    low_part_ref[...].reshape(NBLK * TPIX, BLOCK),
+                    high_ref[tile % 2].reshape(NBLK * TPIX, BLOCK),
+                    low_part_ref[tile % 2].reshape(NBLK * TPIX, BLOCK),
                 ],
                 axis=1,
             ),
@@ -666,8 +666,8 @@
         tail = jnp.zeros((TPIX, 1), F32)
         grad_parts = [None] * NBLK
         for block in reversed(range(NBLK)):
-            alpha = alpha_ref[block]
-            q_val = q_ref[block]
+            alpha = alpha_ref[tile % 2, block]
+            q_val = q_ref[tile % 2, block]
             here_sum = later[block * TPIX : (block + 1) * TPIX] + tail
             d_exp = q_val - here_sum * (alpha * (1.0 + alpha * (1.0 + alpha)))
             tail = here_sum[:, 0:1] + q_val[:, 0:1]
@@ -701,7 +701,9 @@
 
     for copy in copies:
         copy.wait()
-    expo = lax.fori_loop(0, TILES, tile_step, jnp.zeros((8, 128), F32))
+    expo = jnp.zeros((8, 128), F32)
+    for tile in range(TILES):
+        expo = tile_step(tile, expo)
     sum_ref[USED:WIDE, :] = jnp.zeros((WIDE - USED, DEVS), F32)
     for k in range(VALS):
         for deep in range(2):
@@ -737,12 +739,12 @@
             pltpu.VMEM((2 * BLOCK, BLOCK), BF16),
             pltpu.VMEM((TPIX, 128), BF16),
             pltpu.VMEM((16, 2 * TPIX), BF16),
-            pltpu.VMEM((NBLK, TPIX, BLOCK), F32),
-            pltpu.VMEM((NBLK, TPIX, BLOCK), F32),
-            pltpu.VMEM((TPIX, 128), BF16),
+            pltpu.VMEM((2, NBLK, TPIX, BLOCK), F32),
+            pltpu.VMEM((2, NBLK, TPIX, BLOCK), F32),
+            pltpu.VMEM((2, TPIX, 128), BF16),
             pltpu.VMEM((WIDE, DEVS), F32),
-            pltpu.VMEM((NBLK, TPIX, BLOCK), BF16),
-            pltpu.VMEM((NBLK, TPIX, BLOCK), BF16),
+            pltpu.VMEM((2, NBLK, TPIX, BLOCK), BF16),
+            pltpu.VMEM((2, NBLK, TPIX, BLOCK), BF16),
             pltpu.VMEM((ROWS, 2 * DEVS), F32),
         ],
         compiler_params=pltpu.CompilerParams(vmem_limit_bytes=32 << 20),
@@ -821,12 +823,12 @@
             grad_ref[pl.ds(k * CAP + base, 8), :] = jnp.where(code >= 0, grads[k], 0.0)
         return carry
 
-    lax.fori_loop(0, CAP // 8, chunk, 0)
+    lax.fori_loop(0, CAP // 8, chunk, 0, unroll=2)
     send_rows.wait()
 
     def scatter(step, carry):
-        for odd in range(12):
-            rank = step * 12 + odd
+        for odd in range(16):
+            rank = step * 16 + odd
             half = (code_t_ref[pl.ds(rank, 1), :] >> 13) & 1
             mine = jnp.concatenate(
                 [grad_ref[pl.ds(group * 8 * CAP + rank, 8, stride=CAP), :] for group in range(8)],
@@ -852,7 +854,7 @@
                     tables[at % TABLES][pl.ds(rows[at], 1), :] = news[at]
         return carry
 
-    lax.fori_loop(0, CAP // 12, scatter, 0)
+    lax.fori_loop(0, CAP // 16, scatter, 0)
 
     for copy in fetches:
         copy.wait()
@@ -901,7 +903,7 @@
             pltpu.SMEM((CAP, DEVS), jnp.int32),
             pltpu.VMEM((WIDE, DEVS), F32),
             pltpu.VMEM((64 * CAP, DEVS), F32),
-            pltpu.VMEM((12, DEVS, 128), F32),
+            pltpu.VMEM((16, DEVS, 128), F32),
             pltpu.VMEM((SPAN // 256, 128, 128), F32),
         ]
         + [pltpu.VMEM((PARAMS, GDEV), F32)] * 3

time: 96.7 us -> 95.8 us (level)
  no operation moved by 1% of the time
where the time goes in v7:
time: 95.8 us; the launch traced here: 95.4 us
  Pallas kernels  46.8 us (49%)
  blocking collectives  30.6 us (32%)
  starting transfers between devices  11.5 us (12%)
  waiting for transfers between devices  5.71 us (6%)
    all_to_all x2, blocking collectives, exchange(): return lax.all_to_all(value, AXES, split_axis=0, concat_axis=0, tiled=True)  30.6 us
    pallas_call x1, Pallas kernels, update_of(): pl.pallas_call(update_kernel, name='update', out_shape=(whole, whole, who...  17.1 us
    pallas_call x1, Pallas kernels, render_of(): pl.pallas_call(render_kernel, name='render', out_shape=jax.ShapeDtypeStru...  13.2 us
    all_to_all x1, starting transfers between devices, exchange(): return lax.all_to_all(value, AXES, split_axis=0, concat_axis=0, tiled=True)  11.5 us
    pallas_call x1, Pallas kernels, reply_of(): pl.pallas_call(reply_kernel, name='reply', out_shape=(jax.ShapeDtypeStruc...  9.98 us
    all_to_all x1, waiting for transfers between devices, exchange(): return lax.all_to_all(value, AXES, split_axis=0, concat_axis=0, tiled=True)  5.71 us
    pallas_call x1, Pallas kernels, table_of(): pl.pallas_call(table_kernel, name='table', out_shape=pltpu.HBM((HALF, 128...  3.6 us
    pallas_call x1, Pallas kernels, route(): pl.pallas_call(route_kernel, name='route', out_shape=(jax.ShapeDtypeStruc...  2.96 us
  transfers between devices with their start and end apart: 1, of which 1 were waited for; matrix products, arithmetic and copies ran while one was open for 0% of the time, Pallas kernels for 4%

profile of v7, /device:TPU:1, one launch (start us, length us, event | category | flops | bytes accessed | tf_op | source)
XLA Modules:
  0.0 95.4 jit_solution(15640880002620472290)
XLA Ops:
  0.6 3.0 %route.1 = (s32[128,128]{1,0:T(8,128)}, s32[8,4096]{1,0:T(8,128)S(1)}) custom-call(s32[4]{0:T(128)} %view_hbm.3, s32[4]{0:T(128)} %count_hbm.1, s32[4,1024]{1,0:T(4,128)} %owner_hbm.1, s32[4,1024]{1,0:T(4,128)} %local_hbm.1), custom_call_target="tpu_custom_call" | custom-call | tf_op jit(solution)/shard_map/route/pallas_call | solution.py:296
  3.6 11.5 %all-to-all-start = ((s32[128,1,128]{2,1,0:T(1,128)}), s32[128,1,128]{2,1,0:T(1,128)S(1)}, u32[]{:S(2)}, u32[]{:S(2)}) async-start(s32[128,1,128]{2,1,0:T(1,128)} %bitcast.1), calls=%async_computation | async-start | bytes 131072 | tf_op jit(solution)/shard_map/all_to_all | solution.py:918
  15.1 0.0 copy-start
  15.1 3.6 %table.1.table_hbm = f32[8192,128]{1,0:T(8,128)} custom-call(f32[59,16384]{1,0:T(8,128)} %params_hbm.3), custom_call_target="tpu_custom_call" | custom-call | flops 1048576 | bytes 9437184 | tf_op jit(solution)/shard_map/table/pallas_call | solution.py:356
  18.7 5.7 %all-to-all-done = s32[128,1,128]{2,1,0:T(1,128)S(1)} async-done(((s32[128,1,128]{2,1,0:T(1,128)}), s32[128,1,128]{2,1,0:T(1,128)S(1)}, u32[]{:S(2)}, u32[]{:S(2)}) %all-to-all-start) | async-done | bytes 65568 | tf_op jit(solution)/shard_map/all_to_all | solution.py:918
  24.4 0.0 copy-done
  24.4 10.0 %reply.1 = (f32[128,4,128]{2,1,0:T(4,128)S(1)}, f32[3072,128]{1,0:T(8,128)S(1)}) custom-call(f32[4,13]{1,0:T(4,128)S(1)} %copy-done, s32[128,128]{1,0:T(8,128)S(1)} %bitcast.5, f32[8192,128]{1,0:T(8,128)} %table.1.table_hbm), custom_call_target="tpu_custom_call" | custom-call | tf_op jit(solution)/shard_map/reply/pallas_call | solution.py:446
  34.4 15.3 %all_to_all.21.arrived_ref = f32[128,4,128]{2,1,0:T(4,128)S(1)} all-to-all(f32[128,4,128]{2,1,0:T(4,128)S(1)} %get-tuple-element.10), channel_id=1, replica_groups=mesh['tiles'=16,'gauss'=8] {'tiles','gauss'}, dimensions={0} | all-to-all | bytes 524288 | tf_op jit(solution)/shard_map/all_to_all | solution.py:918
  49.8 13.2 %render.1 = f32[128,4,128]{2,1,0:T(4,128)S(1)} custom-call(s32[4]{0:T(128)} %view_hbm.3, s32[4]{0:T(128)} %spot_hbm.1, f32[4,3]{1,0:T(4,128)} %gain_hbm.1, f32[3,4,256]{2,1,0:T(4,128)} %bitcast.7, s32[8,4096]{1,0:T(8,128)S(1)} %get-tuple-element.9.entry_ref, f32[128,4,128]{2,1,0:T(4,128)S(1)} %all_to_all.21.arrived_ref), custom_call_target="tpu_custom_call" | custom-call | tf_op jit(solution)/shard_map/render/pallas_call | solution.py:725
  63.0 15.2 %all_to_all.22.arrived_ref = f32[128,4,128]{2,1,0:T(4,128)S(1)} all-to-all(f32[128,4,128]{2,1,0:T(4,128)S(1)} %render.1), channel_id=1, replica_groups=mesh['tiles'=16,'gauss'=8] {'tiles','gauss'}, dimensions={0} | all-to-all | bytes 524288 | tf_op jit(solution)/shard_map/all_to_all | solution.py:918
  78.2 17.1 %update.1 = (f32[59,16384]{1,0:T(8,128)}, f32[59,16384]{1,0:T(8,128)}, f32[59,16384]{1,0:T(8,128)}, f32[4,3]{1,0:T(4,128)}) custom-call(f32[4,13]{1,0:T(4,128)S(1)} %copy-done, s32[128,128]{1,0:T(8,128)S(1)} %bitcast.6, f32[128,4,128]{2,1,0:T(4,128)S(1)} %all_to_all.22.arrived_ref, f32[3072,128]{1,0:T(8,128)S(1)} %get-tuple-element.11.rows_ref, ...), custom_call_target="tpu_custom_call" | custom-call | tf_op jit(solution)/shard_map/update/pallas_call | solution.py:894
Async XLA Ops:
  3.6 20.8 %all-to-all-start = ((s32[128,1,128]{2,1,0:T(1,128)}), s32[128,1,128]{2,1,0:T(1,128)S(1)}, u32[]{:S(2)}, u32[]{:S(2)}) async-start(s32[128,1,128]{2,1,0:T(1,128)} %bitcast.1), calls=%async_computation | async-start | bytes 131072 | tf_op jit(solution)/shard_map/all_to_all | solution.py:918
  15.1 9.3 %copy-start = (f32[4,13]{1,0:T(4,128)S(1)}, f32[4,13]{1,0:T(4,128)}, u32[]{:S(2)}) copy-start(f32[4,13]{1,0:T(4,128)} %camera_ref.3) | copy-start | bytes 628
